TPU v7x, 256 devices: a whole 4x4x8 slice. The times are simulated.
256 devices in a mesh: stn: 8 (over x_hi, y), tm: 16 (over z, core), cores: 2 (over x_lo).
Axes of the slice: x: 4 (x_hi: 2, x_lo: 2; x = x_hi * 2 + x_lo), y: 4, z: 8, core: 2. Of those that a mesh axis runs over, the one named last changes fastest.
Arguments:
- samples: bfloat16 [64, 4194304], P('stn', ('tm', 'cores')), may hold values from -6 to 6
- delays: int32 [64], P('stn'), may hold values from 0 to 32768, as said below
- valid: int32 [64], P('stn'), may hold values 0 or 1
- tone_chan: int32 [64, 64], P('stn'), may hold values from 0 to 16383
Outputs:
- visibility: float32 [16384, 8192], P(('stn', 'tm', 'cores'))
- phase_cal: float32 [64, 128], P('stn')
Inputs may be any that keep to these rules, and one draw needn't show every extreme that they name: `delays`: each station's delay in samples; some station has a delay of exactly 32768.
All inputs are finite; a program needn't handle non-finite values. No bound on the sum of `valid` on one device may be relied on, other than what follows from the above.
Results may differ from a plain program's by a relative error of at most 0.007.
Values may be sent and summed in bfloat16 or wider, within the bound.
No kernel may reach another device: no remote copies, remote signals or barrier semaphores. Data moves between devices by JAX's collectives and lax.ppermute only.
A program may use at most 128 MiB of HBM per device.

v0:
```python
import math

import jax
import jax.numpy as jnp
from jax import lax
from jax.sharding import PartitionSpec as P

S = 64
NCH = 16384
FA = 256
FB = 128
NTONE = 64
MAXD = 32768


def passed_along(block, axis, distance):
    devices = range(lax.axis_size(axis))
    route = [(i - distance, i) for i in devices if i - distance in devices]
    return lax.ppermute(block, axis, route)


def make_tables():
    outer_idx = jnp.arange(FA, dtype=jnp.int32)
    phases = outer_idx[:, None] * outer_idx[None, :] % FA
    angles = 2.0 * math.pi / FA * phases.astype(jnp.float32)
    section_one = jnp.stack([jnp.cos(angles), -jnp.sin(angles)]).astype(jnp.bfloat16)
    inner_idx = jnp.arange(FB, dtype=jnp.int32)
    spectrum_len = FA * FB
    twist_idx = outer_idx[:, None] * inner_idx[None, :] % spectrum_len
    twists = 2.0 * math.pi / spectrum_len * twist_idx.astype(jnp.float32)
    norm_scale = 1.0 / math.sqrt(spectrum_len)
    twist_cos = jnp.cos(twists) * norm_scale
    twist_sin = jnp.sin(twists) * norm_scale
    half_idx = jnp.arange(FB // 2, dtype=jnp.int32)
    last_idx = inner_idx[:, None] * half_idx[None, :] % FB
    thetas = 2.0 * math.pi / FB * last_idx.astype(jnp.float32)
    cosine = jnp.cos(thetas)
    sine_val = jnp.sin(thetas)
    section_two = jnp.stack(
        [jnp.stack([cosine, -sine_val], axis=1), jnp.stack([sine_val, cosine], axis=1)]
    ).astype(jnp.bfloat16)
    return (section_one, twist_cos, twist_sin, section_two)


def channelize(window, usable, tables):
    section_one, twist_cos, twist_sin, section_two = tables
    spec_count = window.shape[0] // (FA * FB)
    blocks = window.reshape(spec_count, FA, FB)
    section_out = jnp.einsum(
        "xkn,bnm->bxkm", section_one, blocks, preferred_element_type=jnp.float32
    )
    real_part = section_out[:, 0] * twist_cos + section_out[:, 1] * twist_sin
    imag_part = section_out[:, 1] * twist_cos - section_out[:, 0] * twist_sin
    twisted = jnp.stack([real_part, imag_part], axis=1).astype(jnp.bfloat16)
    product = jnp.einsum(
        "xnrq,bxkn->brqk", section_two, twisted, preferred_element_type=jnp.float32
    )
    return (product.reshape(spec_count, 2, NCH) * usable).astype(jnp.bfloat16)


def cross_power(matrix):
    gram = jnp.einsum("cta,ctb->cab", matrix, matrix, preferred_element_type=jnp.float32)
    real_re = gram[:, :S, :S]
    imag_im = gram[:, S:, S:]
    imag_re = gram[:, S:, :S]
    real_im = gram[:, :S, S:]
    channels = gram.shape[0]
    first = (real_re + imag_im).reshape(channels, S * S)
    second = (imag_re - real_im).reshape(channels, S * S)
    return jnp.concatenate([first, second], axis=1)


def shards(samples, delays, valid, tone_chan):
    tables = make_tables()
    stretch = samples.shape[1]
    spectrum_len = FA * FB
    trailing = passed_along(samples[:, :MAXD], ("tm", "cores"), -1)
    extended = jnp.concatenate([samples, trailing], axis=1)
    chan_ids = jnp.arange(NCH, dtype=jnp.int32)

    def station(inputs):
        stream, shift_by, usable, tone_ids = inputs
        window = lax.dynamic_slice_in_dim(stream, shift_by, stretch)
        spectra = channelize(window, usable.astype(jnp.float32), tables)
        totals = jnp.sum(spectra, axis=0, dtype=jnp.float32)
        selector = (chan_ids[:, None] == tone_ids[None, :]).astype(jnp.float32)
        picked = jnp.dot(
            totals, selector, precision=lax.Precision.HIGHEST, preferred_element_type=jnp.float32
        )
        return (spectra, picked.reshape(2 * NTONE))

    spectra, tone_picks = lax.map(station, (extended, delays, valid, tone_chan))
    spectra_all = stretch // spectrum_len * lax.axis_size("tm") * lax.axis_size("cores")
    norm_scale = 1.0 / math.sqrt(spectra_all)
    phase_cal = lax.psum(tone_picks, ("tm", "cores")) * norm_scale
    local_stn = spectra.shape[0]
    spec_here = spectra.shape[1]
    n_stn = lax.axis_size("stn")
    n_tm = lax.axis_size("tm")
    received = lax.all_to_all(spectra[None], ("stn", "tm"), split_axis=4, concat_axis=0, tiled=True)
    block_in = received.shape[4]
    arranged = received.reshape(n_stn, n_tm, local_stn, spec_here, 2, block_in)
    turned = jnp.transpose(arranged, (0, 2, 1, 3, 4, 5)).reshape(
        n_stn * local_stn, n_tm * spec_here, 2, block_in
    )
    block = turned.shape[3]
    halves = turned.reshape(turned.shape[0], turned.shape[1], 2, 2, block // 2)
    halves = lax.all_to_all(halves, "cores", split_axis=3, concat_axis=1, tiled=True)
    turned = halves.reshape(halves.shape[0], halves.shape[1], 2, block // 2)
    rows = turned.shape[1]
    matrix = jnp.transpose(turned, (3, 1, 2, 0)).reshape(turned.shape[3], rows, 2 * S)
    partial_value = cross_power(matrix)
    return (partial_value * norm_scale, phase_cal)


def solution(mesh):
    return jax.shard_map(
        shards,
        mesh=mesh,
        in_specs=(P("stn", ("tm", "cores")), P("stn"), P("stn"), P("stn", None)),
        out_specs=(P(("stn", "tm", "cores"), None), P("stn", None)),
        check_vma=False,
    )
```

profile of v0, /device:TPU:1, one launch (start us, length us, event | category | flops | bytes accessed | tf_op | source)
XLA Modules:
  0.0 494.0 jit_solution(5231773992774877988)
XLA Ops:
  1.7 4.5 collective-permute-start
  8.4 9.6 %collective-permute-done = bf16[8,32768]{1,0:T(8,128)(2,1)} collective-permute-done((bf16[8,32768]{1,0:T(8,128)(2,1)S(1)}, bf16[8,32768]{1,0:T(8,128)(2,1)}, u32[]{:S(2)}, u32[]{:S(2)}) %collective-permute-start) | collective-permute-done | bytes 524320 | tf_op jit(solution)/shard_map/ppermute | solution.py:19
  18.0 2.7 pad_maximum_fusion
  20.6 93.6 %while.17 = (s32[]{:T(128)}, bf16[8,4,2,16384]{3,2,1,0:T(2,128)(2,1)}, f32[8,128]{1,0:T(8,128)S(1)}, s32[8]{0:T(128)S(1)}, bf16[8,163840]{1,0:T(8,128)(2,1)S(1)}...) while((s32[]{:T(128)}, ...), condition=%wide.region_2.3_spmd.clone.clone, body=%wide.region_0.2_spmd.clone.clone.sunk | while | flops 230653952 | bytes 6622727 | solution.py:92
  29.3 2.1 fusion.47
  64.3 2.1 fusion.47
  114.2 43.7 %copy.54 = bf16[8,4,2,16384]{0,1,2,3:T(4,128)(2,1)} copy(bf16[8,4,2,16384]{3,2,1,0:T(2,128)(2,1)} %get-tuple-element.188) | data formatting | bytes 4194304 | tf_op jit(solution)/shard_map/while | solution.py:92
  157.9 23.3 %bitcast_bitcast_fusion = bf16[16384,1,2,4,8]{4,3,2,1,0:T(4,128)(2,1)} fusion(bf16[8,4,2,16384]{0,1,2,3:T(4,128)(2,1)} %copy.54), kind=kLoop, calls=%fused_computation.66 | loop fusion | bytes 4194304
  181.3 38.6 %reshape.221 = bf16[128,2,4096]{2,1,0:T(2,128)(2,1)S(1)} reshape(bf16[16384,1,2,4,8]{4,3,2,1,0:T(4,128)(2,1)} %bitcast_bitcast_fusion) | data formatting | bytes 4194304
  219.8 68.0 %all_to_all.30 = bf16[128,2,4096]{2,1,0:T(2,128)(2,1)} all-to-all(bf16[128,2,4096]{2,1,0:T(2,128)(2,1)S(1)} %reshape.221), channel_id=1, replica_groups=mesh['stn'=8,'tm'=16,'cores'=2] {'stn','tm'}, dimensions={0} | all-to-all | bytes 4194304 | tf_op jit(solution)/shard_map/all_to_all | solution.py:100
  287.9 41.0 %reshape.222 = bf16[16384,1,2,4,8]{4,3,2,1,0:T(4,128)(2,1)} reshape(bf16[128,2,4096]{2,1,0:T(2,128)(2,1)} %all_to_all.30) | data formatting | bytes 4194304
  328.9 36.1 %copy.67 = bf16[1,8,4,2,128,128]{5,1,3,2,4,0:T(8,128)(2,1)S(1)} copy(bf16[1,8,4,2,128,128]{1,2,3,5,4,0:T(4,128)(2,1)} %bitcast.106) | data formatting | bytes 4194304 | tf_op jit(solution)/shard_map/all_to_all | solution.py:100
  366.9 8.2 %reshape_reshape.3 = bf16[64,64,2,2,64]{4,3,0,2,1:T(2,128)(2,1)} reshape(bf16[8,8,16,4,2,128]{5,1,0,4,3,2:T(8,128)(2,1)} %copy.57) | data formatting | bytes 4194304 | tf_op jit(solution)/shard_map/reshape;reshape | solution.py:107
  375.1 5.3 %copy.78 = bf16[64,64,2,2,64]{4,0,2,1,3:T(8,128)(2,1)} copy(bf16[64,64,2,2,64]{4,3,0,2,1:T(2,128)(2,1)} %reshape_reshape.3) | data formatting | bytes 4194304 | tf_op jit(solution)/shard_map/reshape;reshape | solution.py:107
  380.4 5.8 %reshape.223 = bf16[2,2,262144]{2,1,0:T(2,128)(2,1)} reshape(bf16[2,64,2,64,64]{4,3,2,1,0:T(8,128)(2,1)} %bitcast.110) | data formatting | bytes 4194304
  386.2 3.8 all-to-all-start.1
  390.0 71.2 %psum.7 = f32[8,128]{1,0:T(8,128)S(1)} all-reduce(f32[8,128]{1,0:T(8,128)S(1)} %get-tuple-element.189), channel_id=1, replica_groups=mesh['stn'=8,'tm'=16,'cores'=2] {'tm','cores'}, use_global_device_ids=true, to_apply=%region_3.4 | all-reduce | flops 1024 | bytes 8192 | tf_op jit(solution)/shard_map/psum | solution.py:95
  461.8 3.9 reshape.224
  465.6 7.8 %copy.60 = bf16[64,128,2,64]{1,3,2,0:T(8,128)(2,1)S(1)} copy(bf16[64,128,2,64]{0,3,2,1:T(8,128)(2,1)} %bitcast.107) | data formatting | bytes 4194304 | tf_op jit(solution)/shard_map/transpose | solution.py:111
  473.4 8.4 %copy.65 = bf16[64,128,128]{1,2,0:T(8,128)(2,1)} copy(bf16[64,128,128]{0,2,1:T(8,128)(2,1)} %bitcast.108) | data formatting | bytes 4194304 | tf_op jit(solution)/shard_map/reshape | solution.py:111
  481.9 3.2 fusion.35
  485.0 2.5 slice_add_fusion
  487.5 2.1 reshape.211
  491.2 2.7 maximum_multiply_fusion
  (127 shorter events, 76.4 us)
Async XLA Ops:
  1.7 16.2 %collective-permute-start = (bf16[8,32768]{1,0:T(8,128)(2,1)S(1)}, bf16[8,32768]{1,0:T(8,128)(2,1)}, u32[]{:S(2)}, u32[]{:S(2)}) collective-permute-start(bf16[8,32768]{1,0:T(8,128)(2,1)S(1)} %slice.31), channel_id=1, source_target_pairs={{1,0},{2,1},{3,2},{4,3},{5,4},{6,5},{7,6},{8,7},{9,8},{10,9},{11,1... | collective-permute-start | bytes 1572872 | tf_op jit(solution)/shard_map/ppermute | solution.py:19
  8.3 12.3 %copy-start = (s32[8]{0:T(128)S(1)}, s32[8]{0:T(128)}, u32[]{:S(2)}) copy-start(s32[8]{0:T(128)} %param.7) | copy-start | bytes 100
  8.4 12.3 %copy-start.1 = (s32[8]{0:T(128)S(1)}, s32[8]{0:T(128)}, u32[]{:S(2)}) copy-start(s32[8]{0:T(128)} %param.8) | copy-start | bytes 100
  386.2 75.5 %all-to-all-start.1 = ((bf16[2,2,262144]{2,1,0:T(2,128)(2,1)}), bf16[2,2,262144]{2,1,0:T(2,128)(2,1)S(1)}, u32[]{:S(2)}, u32[]{:S(2)}) async-start(bf16[2,2,262144]{2,1,0:T(2,128)(2,1)} %reshape.223), calls=%async_computation.1 | async-start | bytes 4194304 | tf_op jit(solution)/shard_map/all_to_all | solution.py:108
where the time goes:
time: 503 us; the launch traced here: 494 us
  local copies, waits for them, and re-layouts  269 us (53%)
  blocking collectives  139 us (28%)
  matrix products  31.4 us (6%)
  loops' own time  20.3 us (4%)
  other arithmetic  15.9 us (3%)
  waiting for transfers between devices  9.58 us (2%)
  starting transfers between devices  8.27 us (2%)
    unnamed x9, local copies, waits for them, and re-layouts  113 us
    psum x1, blocking collectives, shards(): phase_cal = lax.psum(tone_picks, ('tm', 'cores')) * norm_scale  71.2 us
    all_to_all x1, blocking collectives, shards(): lax.all_to_all(spectra[None], ('stn', 'tm'), split_axis=4, concat_axis=0,...  68 us
    while x1, local copies, waits for them, and re-layouts, shards(): spectra, tone_picks = lax.map(station, (extended, delays, valid, tone_chan))  43.7 us
    all_to_all x1, local copies, waits for them, and re-layouts, shards(): lax.all_to_all(spectra[None], ('stn', 'tm'), split_axis=4, concat_axis=0,...  36.1 us
    another operation x1, loops' own time, shards(): spectra, tone_picks = lax.map(station, (extended, delays, valid, tone_chan))  20.3 us
    dot_general x8, matrix products, station(): jnp.dot(totals, selector, precision=lax.Precision.HIGHEST, preferred_elem...  16.6 us
    dynamic_slice x8, local copies, waits for them, and re-layouts, station(): window = lax.dynamic_slice_in_dim(stream, shift_by, stretch)  15.2 us
  transfers between devices with their start and end apart: 2, of which 1 were waited for; matrix products, arithmetic and copies ran while one was open for 1% of the time, Pallas kernels for 0%

commit v1 on v0

v1 whole, which is shorter than its diff:
```python
import math

import jax
import jax.numpy as jnp
import ml_dtypes
import numpy as np
from jax import lax
from jax.experimental import pallas as pl
from jax.experimental.pallas import tpu as pltpu
from jax.sharding import PartitionSpec as P

S = 64
NCH = 16384
FA = 256
FB = 128
NTONE = 64
MAXD = 32768
NQ = FB // 2
NHI = 4
LO = FA // NHI
LANES = 128

f32 = jnp.float32
bf16 = jnp.bfloat16


def make_tables():
    k1 = np.arange(FA)
    angles = 2.0 * np.pi / FA * (k1[:, None] * k1[None, :] % FA)
    section_one = np.concatenate([np.cos(angles), -np.sin(angles)]).astype(ml_dtypes.bfloat16)
    n2 = np.arange(FB)
    length = FA * FB
    twists = 2.0 * np.pi / length * (k1[:, None] * n2[None, :] % length)
    scale = 1.0 / math.sqrt(length)
    twist_cos = (np.cos(twists) * scale).astype(np.float32)
    twist_sin = (np.sin(twists) * scale).astype(np.float32)
    q = np.arange(NQ)
    thetas = 2.0 * np.pi / FB * (q[:, None] * n2[None, :] % FB)
    section_two = np.concatenate([np.cos(thetas), np.sin(thetas)], axis=1).astype(
        ml_dtypes.bfloat16
    )
    return (section_one, twist_cos, twist_sin, section_two)


def f_kernel(
    delays, valid, x, halo, tones, one, tcos, tsin, two, msgs, picks, xs, obuf
):
    stations = x.shape[0]
    rows = x.shape[1] // LANES
    halo_rows = halo.shape[1] // LANES
    nt = rows // FA

    def spread(j, _):
        at = pl.multiple_of(j * LANES, LANES)
        xs[pl.ds(pl.multiple_of(j * stations, stations), stations), :] = x[
            :, pl.ds(at, LANES)
        ].astype(f32)
        return 0

    lax.fori_loop(0, rows, spread, 0, unroll=16)

    def spread_halo(j, _):
        at = pl.multiple_of(j * LANES, LANES)
        row = pl.multiple_of((rows + j) * stations, stations)
        xs[pl.ds(row, stations), :] = halo[:, pl.ds(at, LANES)].astype(f32)
        return 0

    lax.fori_loop(0, halo_rows, spread_halo, 0, unroll=16)
    xs[pl.ds((rows + halo_rows) * stations, stations), :] = jnp.zeros((stations, LANES), f32)

    def station(s, _):
        shift = delays[s]
        lead = shift // LANES
        within = shift - lead * LANES
        usable = valid[s].astype(f32)
        first = xs[pl.ds(lead * stations + s, rows, stride=stations), :]
        second = xs[pl.ds((lead + 1) * stations + s, rows, stride=stations), :]
        pair = jnp.concatenate([first.astype(bf16), second.astype(bf16)], axis=1)
        src = lax.broadcasted_iota(jnp.int32, (2 * LANES, LANES), 0)
        dst = lax.broadcasted_iota(jnp.int32, (2 * LANES, LANES), 1)
        move = (src == dst + within).astype(f32).astype(bf16)
        moved = jnp.dot(pair, move, preferred_element_type=f32).astype(bf16)
        tone = tones[pl.ds(s, 1), :]
        tone_q = tone // FA
        tone_k = tone - tone_q * FA
        col = lax.broadcasted_iota(jnp.int32, (2 * FA, 2 * NTONE), 0)
        lane = lax.broadcasted_iota(jnp.int32, (2 * FA, 2 * NTONE), 1)
        hi = col // (2 * LO)
        part = (col // LO) % 2
        chan = hi * LO + col % LO
        pick = ((chan == tone_k) & (part == lane // NTONE)).astype(f32).astype(bf16)
        total = jnp.zeros((NQ, 2 * NTONE), f32)
        for t in range(nt):
            block = moved[t * FA : (t + 1) * FA]
            section = jnp.dot(one[...], block, preferred_element_type=f32)
            re, im = section[:FA], section[FA:]
            cosine, sine = tcos[...], tsin[...]
            tr = re * cosine + im * sine
            ti = im * cosine - re * sine
            tr, ti, mr = tr.astype(bf16), ti.astype(bf16), (-tr).astype(bf16)
            real = jnp.concatenate([tr, ti], axis=1)
            imag = jnp.concatenate([ti, mr], axis=1)
            weights = jnp.concatenate(
                [p[h * LO : (h + 1) * LO] for h in range(NHI) for p in (real, imag)], axis=0
            )
            spec = lax.dot_general(
                two[...], weights, (((1,), (1,)), ((), ())), preferred_element_type=f32
            )
            spec = (spec * usable).astype(bf16)
            total = total + jnp.dot(spec, pick, preferred_element_type=f32)
            wide = spec.astype(f32)
            for h in range(NHI):
                at = pl.multiple_of(((h * nt + t) * stations + s) * NQ, NQ)
                obuf[pl.ds(at, NQ), :] = wide[:, h * LANES : (h + 1) * LANES]
        at_q = lax.broadcasted_iota(jnp.int32, (NQ, 2 * NTONE), 0)
        total = jnp.where(at_q == tone_q, total, 0.0)
        picks[pl.ds(s, 1), :] = jnp.sum(total, axis=0, keepdims=True)
        return 0

    lax.fori_loop(0, stations, station, 0)

    def gather(q, _):
        for h in range(NHI):
            got = obuf[pl.ds(h * nt * stations * NQ + q, nt * stations, stride=NQ), :]
            msgs[q * NHI + h] = got.astype(bf16)
        return 0

    lax.fori_loop(0, NQ, gather, 0, unroll=4)


def channelized(samples, trailing, delays, valid, tones, tables):
    stations, stretch = samples.shape
    rows = stretch // LANES
    nt = rows // FA
    smem = pl.BlockSpec(memory_space=pltpu.SMEM)
    vmem = pl.BlockSpec(memory_space=pltpu.VMEM)
    return pl.pallas_call(
        f_kernel,
        out_shape=(
            jax.ShapeDtypeStruct((NQ * NHI, nt * stations, LANES), bf16),
            jax.ShapeDtypeStruct((stations, 2 * NTONE), f32),
        ),
        in_specs=[smem, smem] + [vmem] * 7,
        out_specs=(vmem, vmem),
        scratch_shapes=[
            pltpu.VMEM(((rows + trailing.shape[1] // LANES + 1) * stations, LANES), f32),
            pltpu.VMEM((NHI * nt * stations * NQ, LANES), f32),
        ],
        compiler_params=pltpu.CompilerParams(vmem_limit_bytes=56 << 20),
        name="channelize",
    )(delays, valid, samples, trailing, tones, *tables)


PITCH = 136


def x_kernel(norm_scale, per_source, recv, vis, rs, ts, gs):
    sources, rows, _ = recv.shape
    local = per_source
    groups = S // local
    times = sources // groups * rows // local

    def widen(i, _):
        at = pl.multiple_of(i * rows, rows)
        rs[pl.ds(at, rows), :] = recv[i].astype(f32)
        return 0

    lax.fori_loop(0, sources, widen, 0, unroll=8)

    def turn(i, _):
        g = i // local
        s = i - g * local
        got = rs[pl.ds(g * times * local + s, times, stride=local), :]
        ts[pl.ds(pl.multiple_of(i * PITCH, 8), LANES), :] = got.T
        return 0

    lax.fori_loop(0, S, turn, 0, unroll=4)

    lane = lax.broadcasted_iota(jnp.int32, (8, LANES), 1)

    def eight(o, _):
        base = o * 8
        for c in range(8):
            re = ts[pl.ds(base + c, S, stride=PITCH), :]
            im = ts[pl.ds(base + c + LO, S, stride=PITCH), :]
            plus, quad, minus = re.astype(bf16), im.astype(bf16), (-re).astype(bf16)
            straight = jnp.concatenate([plus, quad], axis=1)
            turned = jnp.concatenate([quad, minus], axis=1)
            left = jnp.concatenate([straight, turned], axis=0)
            right = jnp.concatenate([straight, straight], axis=0)
            gram = lax.dot_general(
                left, right, (((1,), (1,)), ((), ())), preferred_element_type=f32
            )
            gs[pl.ds(c * PITCH, 2 * S), :] = gram * norm_scale
        top = pl.multiple_of(base, 8)
        for j in range(S):
            even = gs[pl.ds(2 * j, 8, stride=PITCH), :]
            odd = gs[pl.ds(2 * j + 1, 8, stride=PITCH), :]
            vis[pl.ds(top, 8), pl.ds(j * LANES, LANES)] = jnp.where(lane < S, even, odd)
        return 0

    lax.fori_loop(0, LO // 8, eight, 0)


def correlated(recv, per_source, norm_scale):
    vmem = pl.BlockSpec(memory_space=pltpu.VMEM)
    sources, rows, _ = recv.shape
    return pl.pallas_call(
        lambda *refs: x_kernel(norm_scale, per_source, *refs),
        out_shape=jax.ShapeDtypeStruct((LO, 2 * S * S), f32),
        in_specs=[vmem],
        out_specs=vmem,
        scratch_shapes=[
            pltpu.VMEM((sources * rows, LANES), f32),
            pltpu.VMEM((S * PITCH, LANES), f32),
            pltpu.VMEM((8 * PITCH, LANES), f32),
        ],
        compiler_params=pltpu.CompilerParams(vmem_limit_bytes=56 << 20),
        name="correlate",
    )(recv)


def passed_along(block, axis, distance):
    devices = range(lax.axis_size(axis))
    route = [(i - distance, i) for i in devices if i - distance in devices]
    return lax.ppermute(block, axis, route)


def summed(value):
    for axis in ("cores", "tm"):
        size = lax.axis_size(axis)
        step = 1
        while step < size:
            value = value + lax.ppermute(value, axis, [(i, i ^ step) for i in range(size)])
            step *= 2
    return value


def shards(samples, delays, valid, tone_chan):
    tables = make_tables()
    stations, stretch = samples.shape
    trailing = passed_along(samples[:, :MAXD], ("tm", "cores"), -1)
    tones = jnp.concatenate([tone_chan, tone_chan], axis=1)
    msgs, picks = channelized(samples, trailing, delays, valid, tones, tables)
    spectra_all = stretch // (FA * FB) * lax.axis_size("tm") * lax.axis_size("cores")
    norm_scale = 1.0 / math.sqrt(spectra_all)
    phase_cal = summed(picks) * norm_scale
    recv = lax.all_to_all(msgs, ("stn", "tm", "cores"), split_axis=0, concat_axis=0, tiled=True)
    return (correlated(recv, stations, norm_scale), phase_cal)


def solution(mesh):
    return jax.shard_map(
        shards,
        mesh=mesh,
        in_specs=(P("stn", ("tm", "cores")), P("stn"), P("stn"), P("stn", None)),
        out_specs=(P(("stn", "tm", "cores"), None), P("stn", None)),
        check_vma=False,
    )
```

time: 503 us -> 125 us (0.25); the launches traced: 494 us -> 123 us
  local copies, waits for them, and re-layouts: 269 us -> 3.2 us
  blocking collectives: 139 us -> 0 us
  waiting for transfers between devices: 9.58 us -> 54.3 us
  Pallas kernels: 0 us -> 32.2 us
  matrix products: 31.4 us -> 0 us
  starting transfers between devices: 8.27 us -> 31 us
  loops' own time: 20.3 us -> 0 us
  other arithmetic: 15.9 us -> 2.04 us
    unnamed x9 -> x6, local copies, waits for them, and re-layouts: 113 us -> 2.12 us
    psum x1 -> x0, blocking collectives: 71.2 us -> none  [shards(): phase_cal = lax.psum(tone_picks, ('tm', 'cores')) * norm_scale]
    all_to_all x1 -> x0, blocking collectives: 68 us -> none  [shards(): lax.all_to_all(spectra[None], ('stn', 'tm'), split_axis=4, concat_axis=0,...]
    while x9 -> x0, local copies, waits for them, and re-layouts: 44.5 us -> none  [the longest x1 43.7 us: shards(): spectra, tone_picks = lax.map(station, (extended, delays, valid, tone_chan))]
    ppermute x0 -> x5, waiting for transfers between devices: none -> 44 us  [summed(): lax.ppermute(value, axis, [(i, i ^ step) for i in range(size)])]
    all_to_all x1 -> x0, local copies, waits for them, and re-layouts: 36.1 us -> none  [shards(): lax.all_to_all(spectra[None], ('stn', 'tm'), split_axis=4, concat_axis=0,...]
    pallas_call x0 -> x2, Pallas kernels: none -> 32.2 us  [the longest x1 23.5 us: channelized(): pl.pallas_call(f_kernel, out_shape=(jax.ShapeDtypeStruct((NQ * NHI, nt *...]
    dot_general x25 -> x0, matrix products: 31.4 us -> none  [the longest x8 16.6 us: station(): jnp.dot(totals, selector, precision=lax.Precision.HIGHEST, preferred_elem...]
  transfers between devices with their start and end apart: 2 -> 7, of which waited for: 1 -> 6; matrix products, arithmetic and copies ran while one was open for 1% -> 2% of each run, Pallas kernels for 0% -> 0%
where the time goes in v1:
time: 125 us; the launch traced here: 123 us
  waiting for transfers between devices  54.3 us (43%)
  Pallas kernels  32.2 us (26%)
  starting transfers between devices  31 us (25%)
  local copies, waits for them, and re-layouts  3.2 us (3%)
  other arithmetic  2.04 us (2%)
    ppermute x5, waiting for transfers between devices, summed(): lax.ppermute(value, axis, [(i, i ^ step) for i in range(size)])  44 us
    pallas_call x1, Pallas kernels, channelized(): pl.pallas_call(f_kernel, out_shape=(jax.ShapeDtypeStruct((NQ * NHI, nt *...  23.5 us
    all_to_all x1, starting transfers between devices, shards(): lax.all_to_all(msgs, ('stn', 'tm', 'cores'), split_axis=0, concat_axis=0,...  15.3 us
    ppermute x5, starting transfers between devices, summed(): lax.ppermute(value, axis, [(i, i ^ step) for i in range(size)])  11.2 us
    ppermute x1, waiting for transfers between devices, passed_along(): return lax.ppermute(block, axis, route)  10.3 us
    pallas_call x1, Pallas kernels, correlated(): pl.pallas_call(lambda *refs: x_kernel(norm_scale, per_source, *refs), out...  8.66 us
    ppermute x1, starting transfers between devices, passed_along(): return lax.ppermute(block, axis, route)  4.51 us
  transfers between devices with their start and end apart: 7, of which 6 were waited for; matrix products, arithmetic and copies ran while one was open for 2% of the time, Pallas kernels for 0%

profile of v1, /device:TPU:1, one launch (start us, length us, event | category | flops | bytes accessed | tf_op | source)
XLA Modules:
  0.0 123.4 jit_solution(7603914799951672297)
XLA Ops:
  0.6 1.1 slice.3
  1.7 4.5 %collective-permute-start = (bf16[8,32768]{1,0:T(8,128)(2,1)S(1)}, bf16[8,32768]{1,0:T(8,128)(2,1)S(1)}, u32[]{:S(2)}, u32[]{:S(2)}) collective-permute-start(bf16[8,32768]{1,0:T(8,128)(2,1)S(1)} %slice.3), channel_id=1, source_target_pairs={{1,0},{2,1},{3,2},{4,3},{5,4},{6,5},{7,6},{8,7},{9,8},{10,9},{11,1... | collective-permute-start | bytes 1572872 | tf_op jit(solution)/shard_map/ppermute | solution.py:226
  6.2 1.4 %pad_add_fusion.tones = s32[8,128]{1,0:T(8,128)} fusion(s32[8,64]{1,0:T(8,128)} %param.11), kind=kLoop, calls=%fused_computation | loop fusion | flops 1024 | bytes 6144 | tf_op jit(solution)/shard_map/concatenate | solution.py:243
  7.7 10.3 %collective-permute-done.halo = bf16[8,32768]{1,0:T(8,128)(2,1)S(1)} collective-permute-done((bf16[8,32768]{1,0:T(8,128)(2,1)S(1)}, bf16[8,32768]{1,0:T(8,128)(2,1)S(1)}, u32[]{:S(2)}, u32[]{:S(2)}) %collective-permute-start) | collective-permute-done | bytes 524320 | tf_op jit(solution)/shard_map/ppermute | solution.py:226
  17.9 0.0 copy-start.1
  18.0 0.8 copy-done.1
  18.7 23.5 %channelize.1 = (bf16[256,32,128]{2,1,0:T(8,128)(2,1)}, f32[8,128]{1,0:T(8,128)}) custom-call(s32[8]{0:T(128)} %delays.1, s32[8]{0:T(128)} %valid.1, bf16[8,131072]{1,0:T(8,128)(2,1)} %x.1, bf16[8,32768]{1,0:T(8,128)(2,1)} %copy-done.1, s32[8,128]{1,0:T(8,128)} %pad_add_fusion.tones, bf16[512,256]{1,0:T(8,128)(2,1)} %constant.10.clone.one, ...), custom_call_target="tpu_custom_call" | custom-call | tf_op jit(solution)/shard_map/channelize/pallas_call | solution.py:137
  42.2 0.0 copy-start.2
  42.2 15.3 %all-to-all-start = ((bf16[256,32,128]{2,1,0:T(8,128)(2,1)}), bf16[256,32,128]{2,1,0:T(8,128)(2,1)S(1)}, u32[]{:S(2)}, u32[]{:S(2)}) async-start(bf16[256,32,128]{2,1,0:T(8,128)(2,1)} %get-tuple-element.4), calls=%async_computation | async-start | bytes 4194304 | tf_op jit(solution)/shard_map/all_to_all | solution.py:248
  57.5 0.0 copy-done.2
  57.5 1.5 %collective-permute-start.1 = (f32[8,128]{1,0:T(8,128)S(1)}, f32[8,128]{1,0:T(8,128)S(1)}, u32[]{:S(2)}, u32[]{:S(2)}) collective-permute-start(f32[8,128]{1,0:T(8,128)S(1)} %copy-done.2), channel_id=1, source_target_pairs={{0,1},{1,0},{2,3},{3,2},{4,5},{5,4},{6,7},{7,6},{8,9},{9,8},{10,11... | collective-permute-start | bytes 12296 | tf_op jit(solution)/shard_map/ppermute | solution.py:234
  59.0 2.2 %collective-permute-done.1 = f32[8,128]{1,0:T(8,128)S(1)} collective-permute-done((f32[8,128]{1,0:T(8,128)S(1)}, f32[8,128]{1,0:T(8,128)S(1)}, u32[]{:S(2)}, u32[]{:S(2)}) %collective-permute-start.1) | collective-permute-done | bytes 4128 | tf_op jit(solution)/shard_map/ppermute | solution.py:234
  61.2 2.2 %collective-permute-start.2 = (f32[8,128]{1,0:T(8,128)S(1)}, f32[8,128]{1,0:T(8,128)S(1)}, u32[]{:S(2)}, u32[]{:S(2)}) collective-permute-start(f32[8,128]{1,0:T(8,128)S(1)} %add.15), channel_id=1, source_target_pairs={{0,2},{2,0},{4,6},{6,4},{8,10},{10,8},{12,14},{14,12},{16,18},{18,... | collective-permute-start | bytes 12296 | tf_op jit(solution)/shard_map/ppermute | solution.py:234
  63.4 0.8 collective-permute-done.2
  64.2 1.0 collective-permute-start.3
  65.2 37.3 %collective-permute-done.3 = f32[8,128]{1,0:T(8,128)S(1)} collective-permute-done((f32[8,128]{1,0:T(8,128)S(1)}, f32[8,128]{1,0:T(8,128)S(1)}, u32[]{:S(2)}, u32[]{:S(2)}) %collective-permute-start.3) | collective-permute-done | bytes 4128 | tf_op jit(solution)/shard_map/ppermute | solution.py:234
  102.5 0.9 collective-permute-start.4
  103.4 2.7 %collective-permute-done.4 = f32[8,128]{1,0:T(8,128)S(1)} collective-permute-done((f32[8,128]{1,0:T(8,128)S(1)}, f32[8,128]{1,0:T(8,128)S(1)}, u32[]{:S(2)}, u32[]{:S(2)}) %collective-permute-start.4) | collective-permute-done | bytes 4128 | tf_op jit(solution)/shard_map/ppermute | solution.py:234
  106.1 5.7 %collective-permute-start.5 = (f32[8,128]{1,0:T(8,128)S(1)}, f32[8,128]{1,0:T(8,128)S(1)}, u32[]{:S(2)}, u32[]{:S(2)}) collective-permute-start(f32[8,128]{1,0:T(8,128)S(1)} %add.18), channel_id=1, source_target_pairs={{0,16},{2,18},{4,20},{6,22},{8,24},{10,26},{12,28},{14,30},{16,0},... | collective-permute-start | bytes 12296 | tf_op jit(solution)/shard_map/ppermute | solution.py:234
  111.8 1.0 collective-permute-done.5
  112.8 0.6 add_multiply_fusion
  113.4 0.0 all-to-all-done.refs_0_
  113.4 1.3 %copy-done = bf16[256,32,128]{2,1,0:T(8,128)(2,1)} copy-done((bf16[256,32,128]{2,1,0:T(8,128)(2,1)}, bf16[256,32,128]{2,1,0:T(8,128)(2,1)S(1)}, u32[]{:S(2)}) %copy-start) | copy-done | bytes 2097176
  114.7 8.7 %correlate.1 = f32[64,8192]{1,0:T(8,128)} custom-call(bf16[256,32,128]{2,1,0:T(8,128)(2,1)} %copy-done), custom_call_target="tpu_custom_call" | custom-call | tf_op jit(solution)/shard_map/correlate/pallas_call | solution.py:208
  (5 shorter events, 0.0 us)
Async XLA Ops:
  1.7 16.2 %collective-permute-start = (bf16[8,32768]{1,0:T(8,128)(2,1)S(1)}, bf16[8,32768]{1,0:T(8,128)(2,1)S(1)}, u32[]{:S(2)}, u32[]{:S(2)}) collective-permute-start(bf16[8,32768]{1,0:T(8,128)(2,1)S(1)} %slice.3), channel_id=1, source_target_pairs={{1,0},{2,1},{3,2},{4,3},{5,4},{6,5},{7,6},{8,7},{9,8},{10,9},{11,1... | collective-permute-start | bytes 1572872 | tf_op jit(solution)/shard_map/ppermute | solution.py:226
  17.9 0.8 copy-start.1
  42.2 15.3 %copy-start.2 = (f32[8,128]{1,0:T(8,128)S(1)}, f32[8,128]{1,0:T(8,128)}, u32[]{:S(2)}) copy-start(f32[8,128]{1,0:T(8,128)} %get-tuple-element.5) | copy-start | bytes 12292
  42.2 71.1 %all-to-all-start = ((bf16[256,32,128]{2,1,0:T(8,128)(2,1)}), bf16[256,32,128]{2,1,0:T(8,128)(2,1)S(1)}, u32[]{:S(2)}, u32[]{:S(2)}) async-start(bf16[256,32,128]{2,1,0:T(8,128)(2,1)} %get-tuple-element.4), calls=%async_computation | async-start | bytes 4194304 | tf_op jit(solution)/shard_map/all_to_all | solution.py:248
  57.5 3.6 %collective-permute-start.1 = (f32[8,128]{1,0:T(8,128)S(1)}, f32[8,128]{1,0:T(8,128)S(1)}, u32[]{:S(2)}, u32[]{:S(2)}) collective-permute-start(f32[8,128]{1,0:T(8,128)S(1)} %copy-done.2), channel_id=1, source_target_pairs={{0,1},{1,0},{2,3},{3,2},{4,5},{5,4},{6,7},{7,6},{8,9},{9,8},{10,11... | collective-permute-start | bytes 12296 | tf_op jit(solution)/shard_map/ppermute | solution.py:234
  61.2 3.0 %collective-permute-start.2 = (f32[8,128]{1,0:T(8,128)S(1)}, f32[8,128]{1,0:T(8,128)S(1)}, u32[]{:S(2)}, u32[]{:S(2)}) collective-permute-start(f32[8,128]{1,0:T(8,128)S(1)} %add.15), channel_id=1, source_target_pairs={{0,2},{2,0},{4,6},{6,4},{8,10},{10,8},{12,14},{14,12},{16,18},{18,... | collective-permute-start | bytes 12296 | tf_op jit(solution)/shard_map/ppermute | solution.py:234
  64.2 38.3 %collective-permute-start.3 = (f32[8,128]{1,0:T(8,128)S(1)}, f32[8,128]{1,0:T(8,128)S(1)}, u32[]{:S(2)}, u32[]{:S(2)}) collective-permute-start(f32[8,128]{1,0:T(8,128)S(1)} %add.16), channel_id=1, source_target_pairs={{0,4},{2,6},{4,0},{6,2},{8,12},{10,14},{12,8},{14,10},{16,20},{18,... | collective-permute-start | bytes 12296 | tf_op jit(solution)/shard_map/ppermute | solution.py:234
  102.5 3.7 %collective-permute-start.4 = (f32[8,128]{1,0:T(8,128)S(1)}, f32[8,128]{1,0:T(8,128)S(1)}, u32[]{:S(2)}, u32[]{:S(2)}) collective-permute-start(f32[8,128]{1,0:T(8,128)S(1)} %add.17), channel_id=1, source_target_pairs={{0,8},{2,10},{4,12},{6,14},{8,0},{10,2},{12,4},{14,6},{16,24},{18,... | collective-permute-start | bytes 12296 | tf_op jit(solution)/shard_map/ppermute | solution.py:234
  106.1 6.6 %collective-permute-start.5 = (f32[8,128]{1,0:T(8,128)S(1)}, f32[8,128]{1,0:T(8,128)S(1)}, u32[]{:S(2)}, u32[]{:S(2)}) collective-permute-start(f32[8,128]{1,0:T(8,128)S(1)} %add.18), channel_id=1, source_target_pairs={{0,16},{2,18},{4,20},{6,22},{8,24},{10,26},{12,28},{14,30},{16,0},... | collective-permute-start | bytes 12296 | tf_op jit(solution)/shard_map/ppermute | solution.py:234
  113.4 1.3 %copy-start = (bf16[256,32,128]{2,1,0:T(8,128)(2,1)}, bf16[256,32,128]{2,1,0:T(8,128)(2,1)S(1)}, u32[]{:S(2)}) copy-start(bf16[256,32,128]{2,1,0:T(8,128)(2,1)S(1)} %all-to-all-done.refs_0_) | copy-start | bytes 6291460

commit v2 on v1

v2 whole, which is shorter than its diff:
```python
import math

import jax
import jax.numpy as jnp
import ml_dtypes
import numpy as np
from jax import lax
from jax.experimental import pallas as pl
from jax.experimental.pallas import tpu as pltpu
from jax.sharding import PartitionSpec as P

S = 64
NCH = 16384
FA = 256
FB = 128
NTONE = 64
MAXD = 32768
NQ = FB // 2
NHI = 4
LO = FA // NHI
LANES = 128

f32 = jnp.float32
bf16 = jnp.bfloat16


def make_tables():
    k1 = np.arange(FA)
    angles = 2.0 * np.pi / FA * (k1[:, None] * k1[None, :] % FA)
    section_one = np.concatenate([np.cos(angles), -np.sin(angles)], axis=1).astype(
        ml_dtypes.bfloat16
    )
    n2 = np.arange(FB)
    length = FA * FB
    twists = 2.0 * np.pi / length * (n2[:, None] * k1[None, :] % length)
    scale = 1.0 / math.sqrt(length)
    twist_cos = (np.cos(twists) * scale).astype(np.float32)
    twist_sin = (np.sin(twists) * scale).astype(np.float32)
    q = np.arange(NQ)
    thetas = 2.0 * np.pi / FB * (q[:, None] * n2[None, :] % FB)
    cosine, sine = np.cos(thetas), np.sin(thetas)
    section_two = np.block([[cosine, sine], [-sine, cosine]]).astype(ml_dtypes.bfloat16)
    return (section_one, twist_cos, twist_sin, section_two)


OPITCH = NQ + 8
PIECES = 4


def f_kernel(nt, n_in, at_row, delays, valid, *refs):
    streams = refs[:n_in]
    before, tones, one, tcos, tsin, two = refs[n_in : n_in + 6]
    msgs, picks, xin, xs, obuf, mbuf, in_sem, out_sem = refs[-8:]
    stations = tones.shape[0]
    rows = nt * FA
    chunk = FA * LANES
    chunks = xin.shape[1] // chunk
    pitch = xs.shape[0] // stations
    copies = []
    for stream in streams:
        for k in range(stream.shape[1] // chunk):
            i = len(copies)
            copies.append(
                pltpu.make_async_copy(
                    stream.at[:, pl.ds(k * chunk, chunk)],
                    xin.at[:, pl.ds(i * chunk, chunk)],
                    in_sem.at[i],
                )
            )
            copies[-1].start()
    for i in range(chunks):
        copies[i].wait()

        def spread(j, _):
            at = pl.multiple_of(j * LANES, LANES)
            xs[pl.ds(j, stations, stride=pitch), :] = xin[:, pl.ds(at, LANES)].astype(f32)
            return 0

        lax.fori_loop(i * FA, (i + 1) * FA, spread, 0, unroll=16)
    xs[pl.ds(chunks * FA, stations, stride=pitch), :] = jnp.zeros((stations, LANES), f32)
    src = lax.broadcasted_iota(jnp.int32, (2 * LANES, LANES), 0)
    dst = lax.broadcasted_iota(jnp.int32, (2 * LANES, LANES), 1)
    low = lax.broadcasted_iota(jnp.int32, (NQ, LANES), 1) < LO
    at_q = lax.broadcasted_iota(jnp.int32, (NQ, 2 * NTONE), 0)
    in_re = lax.broadcasted_iota(jnp.int32, (NQ, 2 * NTONE), 1) < NTONE
    col = lax.broadcasted_iota(jnp.int32, (FA, 2 * NTONE), 0)

    def station(s, _):
        shift = delays[s]
        lead = shift // LANES
        within = shift - lead * LANES
        usable = valid[s].astype(f32)
        first = xs[pl.ds(s * pitch + lead, rows), :]
        second = xs[pl.ds(s * pitch + lead + 1, rows), :]
        pair = jnp.concatenate([first.astype(bf16), second.astype(bf16)], axis=1)
        move = (src == dst + within).astype(f32).astype(bf16)
        moved = jnp.dot(pair, move, preferred_element_type=f32).astype(bf16)
        last = (two[...].astype(f32) * usable).astype(bf16)
        kept = []
        for t in range(nt):
            block = moved[t * FA : (t + 1) * FA]
            section = lax.dot_general(
                block, one[...], (((0,), (0,)), ((), ())), preferred_element_type=f32
            )
            re, im = section[:, :FA], section[:, FA:]
            cosine, sine = tcos[...], tsin[...]
            tr = (re * cosine + im * sine).astype(bf16)
            ti = (im * cosine - re * sine).astype(bf16)
            spec = jnp.dot(
                last, jnp.concatenate([tr, ti], axis=0), preferred_element_type=f32
            )
            kept.append(spec.astype(bf16))
            for j in range(FA // LANES):
                a = spec[:NQ, j * LANES : (j + 1) * LANES]
                b = spec[NQ:, j * LANES : (j + 1) * LANES]
                even = jnp.where(low, a, pltpu.roll(b, LO, 1))
                odd = jnp.where(low, pltpu.roll(a, LO, 1), b)
                for h, piece in ((2 * j, even), (2 * j + 1, odd)):
                    at = pl.multiple_of(((h * nt + t) * stations + s) * OPITCH, 8)
                    obuf[pl.ds(at, NQ), :] = piece
        tone = tones[pl.ds(s, 1), :]
        tone_q = tone // FA
        tone_k = tone - tone_q * FA
        pick = (col == tone_k).astype(f32).astype(bf16)
        found = jnp.dot(jnp.concatenate(kept, axis=0), pick, preferred_element_type=f32)
        total = jnp.zeros((NQ, 2 * NTONE), f32)
        for t in range(nt):
            own = found[2 * t * NQ : 2 * (t + 1) * NQ]
            total = total + jnp.where(in_re, own[:NQ], own[NQ:])
        total = jnp.where(at_q == tone_q, total, 0.0)
        picks[pl.ds(s, 1), :] = before[pl.ds(s, 1), :] + jnp.sum(total, axis=0, keepdims=True)
        return 0

    lax.fori_loop(0, stations, station, 0)

    per = NQ // PIECES
    sent = []
    for i in range(PIECES):

        def gather(q, _):
            for h in range(NHI):
                got = obuf[
                    pl.ds(h * nt * stations * OPITCH + q, nt * stations, stride=OPITCH), :
                ]
                mbuf[q * NHI + h] = got.astype(bf16)
            return 0

        lax.fori_loop(i * per, (i + 1) * per, gather, 0, unroll=4)
        span = pl.ds(i * per * NHI, per * NHI)
        sent.append(
            pltpu.make_async_copy(
                mbuf.at[span], msgs.at[span, pl.ds(at_row, nt * stations), :], out_sem.at[i]
            )
        )
        sent[-1].start()
    for copy in sent:
        copy.wait()


def channelized(streams, nt, at_row, total_rows, delays, valid, before, tones, tables, msgs=None):
    stations = tones.shape[0]
    smem = pl.BlockSpec(memory_space=pltpu.SMEM)
    vmem = pl.BlockSpec(memory_space=pltpu.VMEM)
    hbm = pl.BlockSpec(memory_space=pl.ANY)
    length = sum(stream.shape[1] for stream in streams)
    pitch = (length // LANES // 16 + 1) * 16 + 8
    args = (delays, valid, *streams, before, tones, *tables)
    specs = [smem, smem] + [hbm] * len(streams) + [vmem] * 6
    aliases = {}
    if msgs is not None:
        aliases = {len(args): 0}
        args += (msgs,)
        specs += [hbm]
    return pl.pallas_call(
        lambda *refs: f_kernel(nt, len(streams), at_row, *refs),
        out_shape=(
            jax.ShapeDtypeStruct((NQ * NHI, total_rows, LANES), bf16),
            jax.ShapeDtypeStruct((stations, 2 * NTONE), f32),
        ),
        in_specs=specs,
        out_specs=(hbm, vmem),
        scratch_shapes=[
            pltpu.VMEM((stations, length), bf16),
            pltpu.VMEM((stations * pitch, LANES), f32),
            pltpu.VMEM((NHI * nt * stations * OPITCH, LANES), f32),
            pltpu.VMEM((NQ * NHI, nt * stations, LANES), bf16),
            pltpu.SemaphoreType.DMA((length // (FA * LANES),)),
            pltpu.SemaphoreType.DMA((PIECES,)),
        ],
        input_output_aliases=aliases,
        compiler_params=pltpu.CompilerParams(vmem_limit_bytes=56 << 20),
        name="channelize",
    )(*args)


PITCH = 136


def x_kernel(norm_scale, per_source, recv, vis, rs, ts, gs):
    sources, rows, _ = recv.shape
    local = per_source
    groups = S // local
    times = sources // groups * rows // local

    def widen(i, _):
        at = pl.multiple_of(i * rows, rows)
        rs[pl.ds(at, rows), :] = recv[i].astype(f32)
        return 0

    lax.fori_loop(0, sources, widen, 0, unroll=8)

    def turn(i, _):
        g = i // local
        s = i - g * local
        got = rs[pl.ds(g * times * local + s, times, stride=local), :]
        ts[pl.ds(pl.multiple_of(i * PITCH, 8), LANES), :] = got.T
        return 0

    lax.fori_loop(0, S, turn, 0, unroll=4)

    lane = lax.broadcasted_iota(jnp.int32, (8, LANES), 1)

    def eight(o, _):
        base = o * 8
        for c in range(8):
            re = ts[pl.ds(base + c, S, stride=PITCH), :]
            im = ts[pl.ds(base + c + LO, S, stride=PITCH), :]
            plus, quad, minus = re.astype(bf16), im.astype(bf16), (-re).astype(bf16)
            straight = jnp.concatenate([plus, quad], axis=1)
            turned = jnp.concatenate([quad, minus], axis=1)
            left = jnp.concatenate([straight, turned], axis=0)
            right = jnp.concatenate([straight, straight], axis=0)
            gram = lax.dot_general(
                left, right, (((1,), (1,)), ((), ())), preferred_element_type=f32
            )
            gs[pl.ds(c * PITCH, 2 * S), :] = gram * norm_scale
        top = pl.multiple_of(base, 8)
        for j in range(S):
            even = gs[pl.ds(2 * j, 8, stride=PITCH), :]
            odd = gs[pl.ds(2 * j + 1, 8, stride=PITCH), :]
            vis[pl.ds(top, 8), pl.ds(j * LANES, LANES)] = jnp.where(lane < S, even, odd)
        return 0

    lax.fori_loop(0, LO // 8, eight, 0)


def correlated(recv, per_source, norm_scale):
    vmem = pl.BlockSpec(memory_space=pltpu.VMEM)
    sources, rows, _ = recv.shape
    return pl.pallas_call(
        lambda *refs: x_kernel(norm_scale, per_source, *refs),
        out_shape=jax.ShapeDtypeStruct((LO, 2 * S * S), f32),
        in_specs=[vmem],
        out_specs=vmem,
        scratch_shapes=[
            pltpu.VMEM((sources * rows, LANES), f32),
            pltpu.VMEM((S * PITCH, LANES), f32),
            pltpu.VMEM((8 * PITCH, LANES), f32),
        ],
        compiler_params=pltpu.CompilerParams(vmem_limit_bytes=56 << 20),
        name="correlate",
    )(recv)


def passed_along(block, axis, distance):
    devices = range(lax.axis_size(axis))
    route = [(i - distance, i) for i in devices if i - distance in devices]
    return lax.ppermute(block, axis, route)


def summed(value, axis):
    size = lax.axis_size(axis)
    parts = [value]
    for step in range(1, size):
        parts.append(lax.ppermute(value, axis, [(i, (i + step) % size) for i in range(size)]))
    return sum(parts)


def shards(samples, delays, valid, tone_chan):
    tables = make_tables()
    stations, stretch = samples.shape
    whole = ("stn", "tm", "cores")
    here = stretch // (FA * FB)
    trailing = passed_along(samples[:, :MAXD], ("tm", "cores"), -1)
    tones = jnp.concatenate([tone_chan, tone_chan], axis=1)
    nothing = jnp.zeros((stations, 2 * NTONE), f32)
    most = here - 1
    rows = here * stations
    msgs, picks = channelized(
        [samples], most, 0, rows, delays, valid, nothing, tones, tables
    )
    msgs, picks = channelized(
        [samples[:, most * FA * FB :], trailing],
        1,
        most * stations,
        rows,
        delays,
        valid,
        picks,
        tones,
        tables,
        msgs,
    )
    spectra_all = here * lax.axis_size("tm") * lax.axis_size("cores")
    norm_scale = 1.0 / math.sqrt(spectra_all)
    recv = lax.all_to_all(msgs, whole, split_axis=0, concat_axis=0, tiled=True)
    phase_cal = summed(picks, ("tm", "cores")) * norm_scale
    return (correlated(recv, stations, norm_scale), phase_cal)


def solution(mesh):
    return jax.shard_map(
        shards,
        mesh=mesh,
        in_specs=(P("stn", ("tm", "cores")), P("stn"), P("stn"), P("stn", None)),
        out_specs=(P(("stn", "tm", "cores"), None), P("stn", None)),
        check_vma=False,
    )
```

time: 125 us -> 164 us (1.31); the launches traced: 123 us -> 164 us
  starting transfers between devices: 31 us -> 120 us
  waiting for transfers between devices: 54.3 us -> 3.27 us
  Pallas kernels: 32.2 us -> 34.2 us
    ppermute x5 -> x31, starting transfers between devices: 11.2 us -> 101 us  [summed(): lax.ppermute(value, axis, [(i, (i + step) % size) for i in range(size)])]
    ppermute x5 -> x31, waiting for transfers between devices: 44 us -> 3.26 us  [summed(): lax.ppermute(value, axis, [(i, (i + step) % size) for i in range(size)])]
    ppermute x1, waiting for transfers between devices: 10.3 us -> 0.01 us  [passed_along(): return lax.ppermute(block, axis, route)]
    pallas_call x1 -> x2, Pallas kernels: 23.5 us -> 25.6 us  [channelized(): pl.pallas_call(lambda *refs: f_kernel(nt, len(streams), at_row, *refs), o...]
  transfers between devices with their start and end apart: 7 -> 33, of which waited for: 6 -> 3; matrix products, arithmetic and copies ran while one was open for 2% -> 1% of each run, Pallas kernels for 0% -> 9%
where the time goes in v2:
time: 164 us
  starting transfers between devices  120 us (73%)
  Pallas kernels  34.2 us (21%)
  local copies, waits for them, and re-layouts  4.83 us (3%)
  waiting for transfers between devices  3.27 us (2%)
    ppermute x31, starting transfers between devices, summed(): lax.ppermute(value, axis, [(i, (i + step) % size) for i in range(size)])  101 us
    pallas_call x2, Pallas kernels, channelized(): pl.pallas_call(lambda *refs: f_kernel(nt, len(streams), at_row, *refs), o...  25.6 us
    all_to_all x1, starting transfers between devices, shards(): recv = lax.all_to_all(msgs, whole, split_axis=0, concat_axis=0, tiled=True)  14 us
    pallas_call x1, Pallas kernels, correlated(): pl.pallas_call(lambda *refs: x_kernel(norm_scale, per_source, *refs), out...  8.65 us
    ppermute x1, starting transfers between devices, passed_along(): return lax.ppermute(block, axis, route)  4.5 us
  transfers between devices with their start and end apart: 33, of which 3 were waited for; matrix products, arithmetic and copies ran while one was open for 1% of the time, Pallas kernels for 9%

profile of v2, /device:TPU:1, one launch (start us, length us, event | category | flops | bytes accessed | tf_op | source)
XLA Modules:
  0.0 164.0 jit_solution(12822044146745005160)
XLA Ops:
  0.6 2.1 %fusion = (bf16[8,32768]{1,0:T(8,128)(2,1)S(1)}, bf16[8,32768]{1,0:T(8,128)(2,1)}) fusion(bf16[8,131072]{1,0:T(8,128)(2,1)} %refs_2_.1), kind=kLoop, calls=%fused_computation.2 | loop fusion | bytes 2097152 | tf_op jit(solution)/shard_map/slice | solution.py:284
  2.7 4.5 %collective-permute-start = (bf16[8,32768]{1,0:T(8,128)(2,1)S(1)}, bf16[8,32768]{1,0:T(8,128)(2,1)S(1)}, u32[]{:S(2)}, u32[]{:S(2)}) collective-permute-start(bf16[8,32768]{1,0:T(8,128)(2,1)S(1)} %get-tuple-element.10), channel_id=1, source_target_pairs={{1,0},{2,1},{3,2},{4,3},{5,4},{6,5},{7,6},{8,7},{9,8},{10,9},{11,1... | collective-permute-start | bytes 1572872 | tf_op jit(solution)/shard_map/ppermute | solution.py:268
  8.5 15.2 %channelize.2 = (bf16[256,32,128]{2,1,0:T(8,128)(2,1)}, f32[8,128]{1,0:T(8,128)}) custom-call(s32[8]{0:T(128)} %refs_0_.3, s32[8]{0:T(128)} %refs_1_.3, bf16[8,131072]{1,0:T(8,128)(2,1)} %refs_2_.1, f32[8,128]{1,0:T(8,128)} %broadcast_in_dim.3.refs_3_, s32[8,128]{1,0:T(8,128)} %pad_add_fusion.refs_4_.refs_5_, ...), custom_call_target="tpu_custom_call" | custom-call | tf_op jit(solution)/shard_map/channelize/pallas_call | solution.py:174
  24.5 10.4 %channelize.3 = (bf16[256,32,128]{2,1,0:T(8,128)(2,1)}, f32[8,128]{1,0:T(8,128)}) custom-call(s32[8]{0:T(128)} %refs_0_.3, s32[8]{0:T(128)} %refs_1_.3, bf16[8,32768]{1,0:T(8,128)(2,1)} %get-tuple-element.11.refs_2_, bf16[8,32768]{1,0:T(8,128)(2,1)} %copy-done.1, f32[8,128]{1,0:T(8,128)} %get-tuple-element.6.refs_4_, ...), custom_call_target="tpu_custom_call", output_to_operand_aliasing={{0}: (10, {})} | custom-call | tf_op jit(solution)/shard_map/channelize/pallas_call | solution.py:174
  34.9 14.0 %all-to-all-start = ((bf16[256,32,128]{2,1,0:T(8,128)(2,1)}), bf16[256,32,128]{2,1,0:T(8,128)(2,1)S(1)}, u32[]{:S(2)}, u32[]{:S(2)}) async-start(bf16[256,32,128]{2,1,0:T(8,128)(2,1)} %get-tuple-element.8), calls=%async_computation | async-start | bytes 4194304 | tf_op jit(solution)/shard_map/all_to_all | solution.py:306
  48.9 1.7 %collective-permute-start.31 = (f32[8,128]{1,0:T(8,128)S(1)}, f32[8,128]{1,0:T(8,128)S(1)}, u32[]{:S(2)}, u32[]{:S(2)}) collective-permute-start(f32[8,128]{1,0:T(8,128)S(1)} %copy-done.2), channel_id=1, source_target_pairs={{0,31},{1,0},{2,1},{3,2},{4,3},{5,4},{6,5},{7,6},{8,7},{9,8},{10,9... | collective-permute-start | bytes 12296 | tf_op jit(solution)/shard_map/ppermute | solution.py:275
  50.6 4.0 %collective-permute-start.30 = (f32[8,128]{1,0:T(8,128)S(1)}, f32[8,128]{1,0:T(8,128)S(1)}, u32[]{:S(2)}, u32[]{:S(2)}) collective-permute-start(f32[8,128]{1,0:T(8,128)S(1)} %copy-done.2), channel_id=1, source_target_pairs={{0,30},{1,31},{2,0},{3,1},{4,2},{5,3},{6,4},{7,5},{8,6},{9,7},{10,... | collective-permute-start | bytes 12296 | tf_op jit(solution)/shard_map/ppermute | solution.py:275
  56.0 2.8 %collective-permute-start.27 = (f32[8,128]{1,0:T(8,128)S(1)}, f32[8,128]{1,0:T(8,128)S(1)}, u32[]{:S(2)}, u32[]{:S(2)}) collective-permute-start(f32[8,128]{1,0:T(8,128)S(1)} %copy-done.2), channel_id=1, source_target_pairs={{0,27},{1,28},{2,29},{3,30},{4,31},{5,0},{6,1},{7,2},{8,3},{9,4},{... | collective-permute-start | bytes 12296 | tf_op jit(solution)/shard_map/ppermute | solution.py:275
  58.8 37.3 %collective-permute-start.26 = (f32[8,128]{1,0:T(8,128)S(1)}, f32[8,128]{1,0:T(8,128)S(1)}, u32[]{:S(2)}, u32[]{:S(2)}) collective-permute-start(f32[8,128]{1,0:T(8,128)S(1)} %copy-done.2), channel_id=1, source_target_pairs={{0,26},{1,27},{2,28},{3,29},{4,30},{5,31},{6,0},{7,1},{8,2},{9,3},... | collective-permute-start | bytes 12296 | tf_op jit(solution)/shard_map/ppermute | solution.py:275
  96.1 2.7 %collective-permute-start.25 = (f32[8,128]{1,0:T(8,128)S(1)}, f32[8,128]{1,0:T(8,128)S(1)}, u32[]{:S(2)}, u32[]{:S(2)}) collective-permute-start(f32[8,128]{1,0:T(8,128)S(1)} %copy-done.2), channel_id=1, source_target_pairs={{0,25},{1,26},{2,27},{3,28},{4,29},{5,30},{6,31},{7,0},{8,1},{9,2}... | collective-permute-start | bytes 12296 | tf_op jit(solution)/shard_map/ppermute | solution.py:275
  98.8 2.8 %collective-permute-start.24 = (f32[8,128]{1,0:T(8,128)S(1)}, f32[8,128]{1,0:T(8,128)S(1)}, u32[]{:S(2)}, u32[]{:S(2)}) collective-permute-start(f32[8,128]{1,0:T(8,128)S(1)} %copy-done.2), channel_id=1, source_target_pairs={{0,24},{1,25},{2,26},{3,27},{4,28},{5,29},{6,30},{7,31},{8,0},{9,1... | collective-permute-start | bytes 12296 | tf_op jit(solution)/shard_map/ppermute | solution.py:275
  102.2 1.5 collective-permute-start.22
  103.7 7.5 %collective-permute-start.21 = (f32[8,128]{1,0:T(8,128)S(1)}, f32[8,128]{1,0:T(8,128)S(1)}, u32[]{:S(2)}, u32[]{:S(2)}) collective-permute-start(f32[8,128]{1,0:T(8,128)S(1)} %copy-done.2), channel_id=1, source_target_pairs={{0,21},{1,22},{2,23},{3,24},{4,25},{5,26},{6,27},{7,28},{8,29},{9,... | collective-permute-start | bytes 12296 | tf_op jit(solution)/shard_map/ppermute | solution.py:275
  111.3 5.3 %collective-permute-start.18 = (f32[8,128]{1,0:T(8,128)S(1)}, f32[8,128]{1,0:T(8,128)S(1)}, u32[]{:S(2)}, u32[]{:S(2)}) collective-permute-start(f32[8,128]{1,0:T(8,128)S(1)} %copy-done.2), channel_id=1, source_target_pairs={{0,18},{1,19},{2,20},{3,21},{4,22},{5,23},{6,24},{7,25},{8,26},{9,... | collective-permute-start | bytes 12296 | tf_op jit(solution)/shard_map/ppermute | solution.py:275
  116.7 1.6 collective-permute-start.17
  118.2 4.6 %collective-permute-start.16 = (f32[8,128]{1,0:T(8,128)S(1)}, f32[8,128]{1,0:T(8,128)S(1)}, u32[]{:S(2)}, u32[]{:S(2)}) collective-permute-start(f32[8,128]{1,0:T(8,128)S(1)} %copy-done.2), channel_id=1, source_target_pairs={{0,16},{1,17},{2,18},{3,19},{4,20},{5,21},{6,22},{7,23},{8,24},{9,... | collective-permute-start | bytes 12296 | tf_op jit(solution)/shard_map/ppermute | solution.py:275
  124.2 2.9 %collective-permute-start.14 = (f32[8,128]{1,0:T(8,128)S(1)}, f32[8,128]{1,0:T(8,128)S(1)}, u32[]{:S(2)}, u32[]{:S(2)}) collective-permute-start(f32[8,128]{1,0:T(8,128)S(1)} %copy-done.2), channel_id=1, source_target_pairs={{0,14},{1,15},{2,16},{3,17},{4,18},{5,19},{6,20},{7,21},{8,22},{9,... | collective-permute-start | bytes 12296 | tf_op jit(solution)/shard_map/ppermute | solution.py:275
  127.1 4.8 %collective-permute-start.13 = (f32[8,128]{1,0:T(8,128)S(1)}, f32[8,128]{1,0:T(8,128)S(1)}, u32[]{:S(2)}, u32[]{:S(2)}) collective-permute-start(f32[8,128]{1,0:T(8,128)S(1)} %copy-done.2), channel_id=1, source_target_pairs={{0,13},{1,14},{2,15},{3,16},{4,17},{5,18},{6,19},{7,20},{8,21},{9,... | collective-permute-start | bytes 12296 | tf_op jit(solution)/shard_map/ppermute | solution.py:275
  132.5 2.2 %collective-permute-start.11 = (f32[8,128]{1,0:T(8,128)S(1)}, f32[8,128]{1,0:T(8,128)S(1)}, u32[]{:S(2)}, u32[]{:S(2)}) collective-permute-start(f32[8,128]{1,0:T(8,128)S(1)} %copy-done.2), channel_id=1, source_target_pairs={{0,11},{1,12},{2,13},{3,14},{4,15},{5,16},{6,17},{7,18},{8,19},{9,... | collective-permute-start | bytes 12296 | tf_op jit(solution)/shard_map/ppermute | solution.py:275
  134.6 1.5 collective-permute-start.10
  136.1 4.0 %collective-permute-start.9 = (f32[8,128]{1,0:T(8,128)S(1)}, f32[8,128]{1,0:T(8,128)S(1)}, u32[]{:S(2)}, u32[]{:S(2)}) collective-permute-start(f32[8,128]{1,0:T(8,128)S(1)} %copy-done.2), channel_id=1, source_target_pairs={{0,9},{1,10},{2,11},{3,12},{4,13},{5,14},{6,15},{7,16},{8,17},{9,1... | collective-permute-start | bytes 12296 | tf_op jit(solution)/shard_map/ppermute | solution.py:275
  143.3 4.2 %collective-permute-start.5 = (f32[8,128]{1,0:T(8,128)S(1)}, f32[8,128]{1,0:T(8,128)S(1)}, u32[]{:S(2)}, u32[]{:S(2)}) collective-permute-start(f32[8,128]{1,0:T(8,128)S(1)} %copy-done.2), channel_id=1, source_target_pairs={{0,5},{1,6},{2,7},{3,8},{4,9},{5,10},{6,11},{7,12},{8,13},{9,14},{... | collective-permute-start | bytes 12296 | tf_op jit(solution)/shard_map/ppermute | solution.py:275
  148.2 1.9 %collective-permute-start.2 = (f32[8,128]{1,0:T(8,128)S(1)}, f32[8,128]{1,0:T(8,128)S(1)}, u32[]{:S(2)}, u32[]{:S(2)}) collective-permute-start(f32[8,128]{1,0:T(8,128)S(1)} %copy-done.2), channel_id=1, source_target_pairs={{0,2},{1,3},{2,4},{3,5},{4,6},{5,7},{6,8},{7,9},{8,10},{9,11},{10,... | collective-permute-start | bytes 12296 | tf_op jit(solution)/shard_map/ppermute | solution.py:275
  155.4 8.6 %correlate.1 = f32[64,8192]{1,0:T(8,128)} custom-call(bf16[256,32,128]{2,1,0:T(8,128)(2,1)} %copy-done), custom_call_target="tpu_custom_call" | custom-call | tf_op jit(solution)/shard_map/correlate/pallas_call | solution.py:250
  (57 shorter events, 15.3 us)
Async XLA Ops:
  2.7 21.0 %collective-permute-start = (bf16[8,32768]{1,0:T(8,128)(2,1)S(1)}, bf16[8,32768]{1,0:T(8,128)(2,1)S(1)}, u32[]{:S(2)}, u32[]{:S(2)}) collective-permute-start(bf16[8,32768]{1,0:T(8,128)(2,1)S(1)} %get-tuple-element.10), channel_id=1, source_target_pairs={{1,0},{2,1},{3,2},{4,3},{5,4},{6,5},{7,6},{8,7},{9,8},{10,9},{11,1... | collective-permute-start | bytes 1572872 | tf_op jit(solution)/shard_map/ppermute | solution.py:268
  34.9 119.1 %all-to-all-start = ((bf16[256,32,128]{2,1,0:T(8,128)(2,1)}), bf16[256,32,128]{2,1,0:T(8,128)(2,1)S(1)}, u32[]{:S(2)}, u32[]{:S(2)}) async-start(bf16[256,32,128]{2,1,0:T(8,128)(2,1)} %get-tuple-element.8), calls=%async_computation | async-start | bytes 4194304 | tf_op jit(solution)/shard_map/all_to_all | solution.py:306
  48.9 9.9 %collective-permute-start.31 = (f32[8,128]{1,0:T(8,128)S(1)}, f32[8,128]{1,0:T(8,128)S(1)}, u32[]{:S(2)}, u32[]{:S(2)}) collective-permute-start(f32[8,128]{1,0:T(8,128)S(1)} %copy-done.2), channel_id=1, source_target_pairs={{0,31},{1,0},{2,1},{3,2},{4,3},{5,4},{6,5},{7,6},{8,7},{9,8},{10,9... | collective-permute-start | bytes 12296 | tf_op jit(solution)/shard_map/ppermute | solution.py:275
  50.6 45.5 %collective-permute-start.30 = (f32[8,128]{1,0:T(8,128)S(1)}, f32[8,128]{1,0:T(8,128)S(1)}, u32[]{:S(2)}, u32[]{:S(2)}) collective-permute-start(f32[8,128]{1,0:T(8,128)S(1)} %copy-done.2), channel_id=1, source_target_pairs={{0,30},{1,31},{2,0},{3,1},{4,2},{5,3},{6,4},{7,5},{8,6},{9,7},{10,... | collective-permute-start | bytes 12296 | tf_op jit(solution)/shard_map/ppermute | solution.py:275
  54.6 44.2 %collective-permute-start.29 = (f32[8,128]{1,0:T(8,128)S(1)}, f32[8,128]{1,0:T(8,128)S(1)}, u32[]{:S(2)}, u32[]{:S(2)}) collective-permute-start(f32[8,128]{1,0:T(8,128)S(1)} %copy-done.2), channel_id=1, source_target_pairs={{0,29},{1,30},{2,31},{3,0},{4,1},{5,2},{6,3},{7,4},{8,5},{9,6},{10... | collective-permute-start | bytes 12296 | tf_op jit(solution)/shard_map/ppermute | solution.py:275
  55.1 46.5 %collective-permute-start.28 = (f32[8,128]{1,0:T(8,128)S(1)}, f32[8,128]{1,0:T(8,128)S(1)}, u32[]{:S(2)}, u32[]{:S(2)}) collective-permute-start(f32[8,128]{1,0:T(8,128)S(1)} %copy-done.2), channel_id=1, source_target_pairs={{0,28},{1,29},{2,30},{3,31},{4,0},{5,1},{6,2},{7,3},{8,4},{9,5},{1... | collective-permute-start | bytes 12296 | tf_op jit(solution)/shard_map/ppermute | solution.py:275
  56.0 46.2 %collective-permute-start.27 = (f32[8,128]{1,0:T(8,128)S(1)}, f32[8,128]{1,0:T(8,128)S(1)}, u32[]{:S(2)}, u32[]{:S(2)}) collective-permute-start(f32[8,128]{1,0:T(8,128)S(1)} %copy-done.2), channel_id=1, source_target_pairs={{0,27},{1,28},{2,29},{3,30},{4,31},{5,0},{6,1},{7,2},{8,3},{9,4},{... | collective-permute-start | bytes 12296 | tf_op jit(solution)/shard_map/ppermute | solution.py:275
  58.8 44.9 %collective-permute-start.26 = (f32[8,128]{1,0:T(8,128)S(1)}, f32[8,128]{1,0:T(8,128)S(1)}, u32[]{:S(2)}, u32[]{:S(2)}) collective-permute-start(f32[8,128]{1,0:T(8,128)S(1)} %copy-done.2), channel_id=1, source_target_pairs={{0,26},{1,27},{2,28},{3,29},{4,30},{5,31},{6,0},{7,1},{8,2},{9,3},... | collective-permute-start | bytes 12296 | tf_op jit(solution)/shard_map/ppermute | solution.py:275
  96.1 15.1 %collective-permute-start.25 = (f32[8,128]{1,0:T(8,128)S(1)}, f32[8,128]{1,0:T(8,128)S(1)}, u32[]{:S(2)}, u32[]{:S(2)}) collective-permute-start(f32[8,128]{1,0:T(8,128)S(1)} %copy-done.2), channel_id=1, source_target_pairs={{0,25},{1,26},{2,27},{3,28},{4,29},{5,30},{6,31},{7,0},{8,1},{9,2}... | collective-permute-start | bytes 12296 | tf_op jit(solution)/shard_map/ppermute | solution.py:275
  98.8 12.4 %collective-permute-start.24 = (f32[8,128]{1,0:T(8,128)S(1)}, f32[8,128]{1,0:T(8,128)S(1)}, u32[]{:S(2)}, u32[]{:S(2)}) collective-permute-start(f32[8,128]{1,0:T(8,128)S(1)} %copy-done.2), channel_id=1, source_target_pairs={{0,24},{1,25},{2,26},{3,27},{4,28},{5,29},{6,30},{7,31},{8,0},{9,1... | collective-permute-start | bytes 12296 | tf_op jit(solution)/shard_map/ppermute | solution.py:275
  101.6 9.7 %collective-permute-start.23 = (f32[8,128]{1,0:T(8,128)S(1)}, f32[8,128]{1,0:T(8,128)S(1)}, u32[]{:S(2)}, u32[]{:S(2)}) collective-permute-start(f32[8,128]{1,0:T(8,128)S(1)} %copy-done.2), channel_id=1, source_target_pairs={{0,23},{1,24},{2,25},{3,26},{4,27},{5,28},{6,29},{7,30},{8,31},{9,... | collective-permute-start | bytes 12296 | tf_op jit(solution)/shard_map/ppermute | solution.py:275
  102.2 14.5 %collective-permute-start.22 = (f32[8,128]{1,0:T(8,128)S(1)}, f32[8,128]{1,0:T(8,128)S(1)}, u32[]{:S(2)}, u32[]{:S(2)}) collective-permute-start(f32[8,128]{1,0:T(8,128)S(1)} %copy-done.2), channel_id=1, source_target_pairs={{0,22},{1,23},{2,24},{3,25},{4,26},{5,27},{6,28},{7,29},{8,30},{9,... | collective-permute-start | bytes 12296 | tf_op jit(solution)/shard_map/ppermute | solution.py:275
  103.7 14.5 %collective-permute-start.21 = (f32[8,128]{1,0:T(8,128)S(1)}, f32[8,128]{1,0:T(8,128)S(1)}, u32[]{:S(2)}, u32[]{:S(2)}) collective-permute-start(f32[8,128]{1,0:T(8,128)S(1)} %copy-done.2), channel_id=1, source_target_pairs={{0,21},{1,22},{2,23},{3,24},{4,25},{5,26},{6,27},{7,28},{8,29},{9,... | collective-permute-start | bytes 12296 | tf_op jit(solution)/shard_map/ppermute | solution.py:275
  111.2 11.7 %collective-permute-start.20 = (f32[8,128]{1,0:T(8,128)S(1)}, f32[8,128]{1,0:T(8,128)S(1)}, u32[]{:S(2)}, u32[]{:S(2)}) collective-permute-start(f32[8,128]{1,0:T(8,128)S(1)} %copy-done.2), channel_id=1, source_target_pairs={{0,20},{1,21},{2,22},{3,23},{4,24},{5,25},{6,26},{7,27},{8,28},{9,... | collective-permute-start | bytes 12296 | tf_op jit(solution)/shard_map/ppermute | solution.py:275
  111.2 13.0 %collective-permute-start.19 = (f32[8,128]{1,0:T(8,128)S(1)}, f32[8,128]{1,0:T(8,128)S(1)}, u32[]{:S(2)}, u32[]{:S(2)}) collective-permute-start(f32[8,128]{1,0:T(8,128)S(1)} %copy-done.2), channel_id=1, source_target_pairs={{0,19},{1,20},{2,21},{3,22},{4,23},{5,24},{6,25},{7,26},{8,27},{9,... | collective-permute-start | bytes 12296 | tf_op jit(solution)/shard_map/ppermute | solution.py:275
  111.3 15.7 %collective-permute-start.18 = (f32[8,128]{1,0:T(8,128)S(1)}, f32[8,128]{1,0:T(8,128)S(1)}, u32[]{:S(2)}, u32[]{:S(2)}) collective-permute-start(f32[8,128]{1,0:T(8,128)S(1)} %copy-done.2), channel_id=1, source_target_pairs={{0,18},{1,19},{2,20},{3,21},{4,22},{5,23},{6,24},{7,25},{8,26},{9,... | collective-permute-start | bytes 12296 | tf_op jit(solution)/shard_map/ppermute | solution.py:275
  116.7 15.2 %collective-permute-start.17 = (f32[8,128]{1,0:T(8,128)S(1)}, f32[8,128]{1,0:T(8,128)S(1)}, u32[]{:S(2)}, u32[]{:S(2)}) collective-permute-start(f32[8,128]{1,0:T(8,128)S(1)} %copy-done.2), channel_id=1, source_target_pairs={{0,17},{1,18},{2,19},{3,20},{4,21},{5,22},{6,23},{7,24},{8,25},{9,... | collective-permute-start | bytes 12296 | tf_op jit(solution)/shard_map/ppermute | solution.py:275
  118.2 14.2 %collective-permute-start.16 = (f32[8,128]{1,0:T(8,128)S(1)}, f32[8,128]{1,0:T(8,128)S(1)}, u32[]{:S(2)}, u32[]{:S(2)}) collective-permute-start(f32[8,128]{1,0:T(8,128)S(1)} %copy-done.2), channel_id=1, source_target_pairs={{0,16},{1,17},{2,18},{3,19},{4,20},{5,21},{6,22},{7,23},{8,24},{9,... | collective-permute-start | bytes 12296 | tf_op jit(solution)/shard_map/ppermute | solution.py:275
  122.9 11.8 %collective-permute-start.15 = (f32[8,128]{1,0:T(8,128)S(1)}, f32[8,128]{1,0:T(8,128)S(1)}, u32[]{:S(2)}, u32[]{:S(2)}) collective-permute-start(f32[8,128]{1,0:T(8,128)S(1)} %copy-done.2), channel_id=1, source_target_pairs={{0,15},{1,16},{2,17},{3,18},{4,19},{5,20},{6,21},{7,22},{8,23},{9,... | collective-permute-start | bytes 12296 | tf_op jit(solution)/shard_map/ppermute | solution.py:275
  124.2 12.0 %collective-permute-start.14 = (f32[8,128]{1,0:T(8,128)S(1)}, f32[8,128]{1,0:T(8,128)S(1)}, u32[]{:S(2)}, u32[]{:S(2)}) collective-permute-start(f32[8,128]{1,0:T(8,128)S(1)} %copy-done.2), channel_id=1, source_target_pairs={{0,14},{1,15},{2,16},{3,17},{4,18},{5,19},{6,20},{7,21},{8,22},{9,... | collective-permute-start | bytes 12296 | tf_op jit(solution)/shard_map/ppermute | solution.py:275
  127.1 13.1 %collective-permute-start.13 = (f32[8,128]{1,0:T(8,128)S(1)}, f32[8,128]{1,0:T(8,128)S(1)}, u32[]{:S(2)}, u32[]{:S(2)}) collective-permute-start(f32[8,128]{1,0:T(8,128)S(1)} %copy-done.2), channel_id=1, source_target_pairs={{0,13},{1,14},{2,15},{3,16},{4,17},{5,18},{6,19},{7,20},{8,21},{9,... | collective-permute-start | bytes 12296 | tf_op jit(solution)/shard_map/ppermute | solution.py:275
  131.9 9.4 %collective-permute-start.12 = (f32[8,128]{1,0:T(8,128)S(1)}, f32[8,128]{1,0:T(8,128)S(1)}, u32[]{:S(2)}, u32[]{:S(2)}) collective-permute-start(f32[8,128]{1,0:T(8,128)S(1)} %copy-done.2), channel_id=1, source_target_pairs={{0,12},{1,13},{2,14},{3,15},{4,16},{5,17},{6,18},{7,19},{8,20},{9,... | collective-permute-start | bytes 12296 | tf_op jit(solution)/shard_map/ppermute | solution.py:275
  132.5 10.2 %collective-permute-start.11 = (f32[8,128]{1,0:T(8,128)S(1)}, f32[8,128]{1,0:T(8,128)S(1)}, u32[]{:S(2)}, u32[]{:S(2)}) collective-permute-start(f32[8,128]{1,0:T(8,128)S(1)} %copy-done.2), channel_id=1, source_target_pairs={{0,11},{1,12},{2,13},{3,14},{4,15},{5,16},{6,17},{7,18},{8,19},{9,... | collective-permute-start | bytes 12296 | tf_op jit(solution)/shard_map/ppermute | solution.py:275
  136.1 11.4 %collective-permute-start.9 = (f32[8,128]{1,0:T(8,128)S(1)}, f32[8,128]{1,0:T(8,128)S(1)}, u32[]{:S(2)}, u32[]{:S(2)}) collective-permute-start(f32[8,128]{1,0:T(8,128)S(1)} %copy-done.2), channel_id=1, source_target_pairs={{0,9},{1,10},{2,11},{3,12},{4,13},{5,14},{6,15},{7,16},{8,17},{9,1... | collective-permute-start | bytes 12296 | tf_op jit(solution)/shard_map/ppermute | solution.py:275
  (13 other events, 75.5 us)

commit v3 on v2

--- a/solution.py
+++ b/solution.py
@@ -47,37 +47,44 @@
 PIECES = 4
 
 
-def f_kernel(nt, n_in, at_row, delays, valid, *refs):
-    streams = refs[:n_in]
-    before, tones, one, tcos, tsin, two = refs[n_in : n_in + 6]
+def f_kernel(nt, span, at_row, more, delays, valid, *refs):
+    stream, tones, one, tcos, tsin, two = refs[:6]
+    trail, before = refs[6:8] if more else (None, None)
     msgs, picks, xin, xs, obuf, mbuf, in_sem, out_sem = refs[-8:]
     stations = tones.shape[0]
     rows = nt * FA
     chunk = FA * LANES
-    chunks = xin.shape[1] // chunk
     pitch = xs.shape[0] // stations
     copies = []
-    for stream in streams:
-        for k in range(stream.shape[1] // chunk):
-            i = len(copies)
-            copies.append(
-                pltpu.make_async_copy(
-                    stream.at[:, pl.ds(k * chunk, chunk)],
-                    xin.at[:, pl.ds(i * chunk, chunk)],
-                    in_sem.at[i],
-                )
-            )
-            copies[-1].start()
-    for i in range(chunks):
-        copies[i].wait()
-
+    start, length = span
+    for i in range(length // chunk):
+        piece = pl.ds(i * chunk, chunk)
+        copies.append(
+            pltpu.make_async_copy(
+                stream.at[:, pl.ds(start + i * chunk, chunk)], xin.at[:, piece], in_sem.at[i]
+            )
+        )
+        copies[i].start()
+
+    def spread_from(source, base):
         def spread(j, _):
             at = pl.multiple_of(j * LANES, LANES)
-            xs[pl.ds(j, stations, stride=pitch), :] = xin[:, pl.ds(at, LANES)].astype(f32)
+            xs[pl.ds(base + j, stations, stride=pitch), :] = source[:, pl.ds(at, LANES)].astype(
+                f32
+            )
             return 0
 
-        lax.fori_loop(i * FA, (i + 1) * FA, spread, 0, unroll=16)
-    xs[pl.ds(chunks * FA, stations, stride=pitch), :] = jnp.zeros((stations, LANES), f32)
+        return spread
+
+    filled = length // LANES
+    if more:
+        lax.fori_loop(0, trail.shape[1] // LANES, spread_from(trail, filled), 0, unroll=16)
+    for i in range(length // chunk):
+        copies[i].wait()
+        lax.fori_loop(i * FA, (i + 1) * FA, spread_from(xin, 0), 0, unroll=16)
+    if more:
+        filled += trail.shape[1] // LANES
+    xs[pl.ds(filled, stations, stride=pitch), :] = jnp.zeros((stations, LANES), f32)
     src = lax.broadcasted_iota(jnp.int32, (2 * LANES, LANES), 0)
     dst = lax.broadcasted_iota(jnp.int32, (2 * LANES, LANES), 1)
     low = lax.broadcasted_iota(jnp.int32, (NQ, LANES), 1) < LO
@@ -119,6 +126,7 @@
                     at = pl.multiple_of(((h * nt + t) * stations + s) * OPITCH, 8)
                     obuf[pl.ds(at, NQ), :] = piece
         tone = tones[pl.ds(s, 1), :]
+        tone = jnp.concatenate([tone, tone], axis=1)
         tone_q = tone // FA
         tone_k = tone - tone_q * FA
         pick = (col == tone_k).astype(f32).astype(bf16)
@@ -128,10 +136,13 @@
             own = found[2 * t * NQ : 2 * (t + 1) * NQ]
             total = total + jnp.where(in_re, own[:NQ], own[NQ:])
         total = jnp.where(at_q == tone_q, total, 0.0)
-        picks[pl.ds(s, 1), :] = before[pl.ds(s, 1), :] + jnp.sum(total, axis=0, keepdims=True)
+        total = jnp.sum(total, axis=0, keepdims=True)
+        if more:
+            total = total + before[pl.ds(s, 1), :]
+        picks[pl.ds(s, 1), :] = total
         return 0
 
-    lax.fori_loop(0, stations, station, 0)
+    lax.fori_loop(0, stations, station, 0, unroll=2 if nt > 1 else stations)
 
     per = NQ // PIECES
     sent = []
@@ -157,22 +168,24 @@
         copy.wait()
 
 
-def channelized(streams, nt, at_row, total_rows, delays, valid, before, tones, tables, msgs=None):
+def channelized(stream, span, nt, at_row, total_rows, delays, valid, tones, tables, trail=()):
     stations = tones.shape[0]
     smem = pl.BlockSpec(memory_space=pltpu.SMEM)
     vmem = pl.BlockSpec(memory_space=pltpu.VMEM)
     hbm = pl.BlockSpec(memory_space=pl.ANY)
-    length = sum(stream.shape[1] for stream in streams)
-    pitch = (length // LANES // 16 + 1) * 16 + 8
-    args = (delays, valid, *streams, before, tones, *tables)
-    specs = [smem, smem] + [hbm] * len(streams) + [vmem] * 6
+    args = (delays, valid, stream, tones, *tables)
+    specs = [smem, smem, hbm] + [vmem] * 5
+    rows = span[1] // LANES
     aliases = {}
-    if msgs is not None:
-        aliases = {len(args): 0}
-        args += (msgs,)
-        specs += [hbm]
+    if trail:
+        after, msgs, picks = trail
+        rows += after.shape[1] // LANES
+        aliases = {len(args) + 2: 0}
+        args += (pltpu.with_memory_space_constraint(after, pltpu.VMEM), picks, msgs)
+        specs += [vmem, vmem, hbm]
+    pitch = (rows // 16 + 1) * 16 + 8
     return pl.pallas_call(
-        lambda *refs: f_kernel(nt, len(streams), at_row, *refs),
+        lambda *refs: f_kernel(nt, span, at_row, bool(trail), *refs),
         out_shape=(
             jax.ShapeDtypeStruct((NQ * NHI, total_rows, LANES), bf16),
             jax.ShapeDtypeStruct((stations, 2 * NTONE), f32),
@@ -180,11 +193,11 @@
         in_specs=specs,
         out_specs=(hbm, vmem),
         scratch_shapes=[
-            pltpu.VMEM((stations, length), bf16),
+            pltpu.VMEM((stations, span[1]), bf16),
             pltpu.VMEM((stations * pitch, LANES), f32),
             pltpu.VMEM((NHI * nt * stations * OPITCH, LANES), f32),
             pltpu.VMEM((NQ * NHI, nt * stations, LANES), bf16),
-            pltpu.SemaphoreType.DMA((length // (FA * LANES),)),
+            pltpu.SemaphoreType.DMA((span[1] // (FA * LANES),)),
             pltpu.SemaphoreType.DMA((PIECES,)),
         ],
         input_output_aliases=aliases,
@@ -259,7 +272,7 @@
         ],
         compiler_params=pltpu.CompilerParams(vmem_limit_bytes=56 << 20),
         name="correlate",
-    )(recv)
+    )(pltpu.with_memory_space_constraint(recv, pltpu.VMEM))
 
 
 def passed_along(block, axis, distance):
@@ -268,11 +281,11 @@
     return lax.ppermute(block, axis, route)
 
 
-def summed(value, axis):
+def joined(value, axis, steps):
     size = lax.axis_size(axis)
     parts = [value]
-    for step in range(1, size):
-        parts.append(lax.ppermute(value, axis, [(i, (i + step) % size) for i in range(size)]))
+    for step in steps:
+        parts.append(lax.ppermute(value, axis, [(i, i ^ step) for i in range(size)]))
     return sum(parts)
 
 
@@ -280,31 +293,30 @@
     tables = make_tables()
     stations, stretch = samples.shape
     whole = ("stn", "tm", "cores")
-    here = stretch // (FA * FB)
-    trailing = passed_along(samples[:, :MAXD], ("tm", "cores"), -1)
-    tones = jnp.concatenate([tone_chan, tone_chan], axis=1)
-    nothing = jnp.zeros((stations, 2 * NTONE), f32)
+    section = FA * FB
+    here = stretch // section
     most = here - 1
     rows = here * stations
+    trailing = passed_along(samples[:, :MAXD], ("tm", "cores"), -1)
+    own = (delays, valid, tone_chan, tables)
+    early = channelized(samples, (0, stretch), most, 0, rows, *own)
     msgs, picks = channelized(
-        [samples], most, 0, rows, delays, valid, nothing, tones, tables
-    )
-    msgs, picks = channelized(
-        [samples[:, most * FA * FB :], trailing],
+        samples,
+        (most * section, section),
         1,
         most * stations,
         rows,
-        delays,
-        valid,
-        picks,
-        tones,
-        tables,
-        msgs,
+        *own,
+        (trailing, *early),
     )
     spectra_all = here * lax.axis_size("tm") * lax.axis_size("cores")
     norm_scale = 1.0 / math.sqrt(spectra_all)
     recv = lax.all_to_all(msgs, whole, split_axis=0, concat_axis=0, tiled=True)
-    phase_cal = summed(picks, ("tm", "cores")) * norm_scale
+    picks = joined(picks, "cores", [1])
+    picks = joined(picks, "tm", [1])
+    picks = joined(picks, "tm", [2, 4, 6])
+    recv, picks = lax.optimization_barrier((recv, picks))
+    phase_cal = joined(picks, "tm", [8]) * norm_scale
     return (correlated(recv, stations, norm_scale), phase_cal)
 
 

time: 164 us -> 106 us (0.65)
  starting transfers between devices: 120 us -> 30.1 us
  waiting for transfers between devices: 3.27 us -> 44.3 us
  Pallas kernels: 34.2 us -> 29.1 us
  local copies, waits for them, and re-layouts: 4.83 us -> 1.08 us
    ppermute x31 -> x6, starting transfers between devices: 101 us -> 11.6 us  [joined(): lax.ppermute(value, axis, [(i, i ^ step) for i in range(size)])]
    ppermute x31 -> x6, waiting for transfers between devices: 3.26 us -> 37.9 us  [joined(): lax.ppermute(value, axis, [(i, i ^ step) for i in range(size)])]
    all_to_all x1, waiting for transfers between devices: 0.01 us -> 6.42 us  [shards(): recv = lax.all_to_all(msgs, whole, split_axis=0, concat_axis=0, tiled=True)]
    pallas_call x2, Pallas kernels: 25.6 us -> 22.1 us  [channelized(): pl.pallas_call(lambda *refs: f_kernel(nt, span, at_row, bool(trail), *ref...]
    unnamed x8 -> x2, local copies, waits for them, and re-layouts: 2.17 us -> 0.01 us
  transfers between devices with their start and end apart: 33 -> 8, of which waited for: 3 -> 5; matrix products, arithmetic and copies ran while one was open for 1% -> 0% of each run, Pallas kernels for 9% -> 20%
where the time goes in v3:
time: 106 us
  waiting for transfers between devices  44.3 us (42%)
  starting transfers between devices  30.1 us (28%)
  Pallas kernels  29.1 us (27%)
  local copies, waits for them, and re-layouts  1.08 us (1%)
    ppermute x6, waiting for transfers between devices, joined(): lax.ppermute(value, axis, [(i, i ^ step) for i in range(size)])  37.9 us
    pallas_call x2, Pallas kernels, channelized(): pl.pallas_call(lambda *refs: f_kernel(nt, span, at_row, bool(trail), *ref...  22.1 us
    all_to_all x1, starting transfers between devices, shards(): recv = lax.all_to_all(msgs, whole, split_axis=0, concat_axis=0, tiled=True)  14 us
    ppermute x6, starting transfers between devices, joined(): lax.ppermute(value, axis, [(i, i ^ step) for i in range(size)])  11.6 us
    pallas_call x1, Pallas kernels, correlated(): pl.pallas_call(lambda *refs: x_kernel(norm_scale, per_source, *refs), out...  7.05 us
    all_to_all x1, waiting for transfers between devices, shards(): recv = lax.all_to_all(msgs, whole, split_axis=0, concat_axis=0, tiled=True)  6.42 us
    ppermute x1, starting transfers between devices, passed_along(): return lax.ppermute(block, axis, route)  4.51 us
  transfers between devices with their start and end apart: 8, of which 5 were waited for; matrix products, arithmetic and copies ran while one was open for 0% of the time, Pallas kernels for 20%

profile of v3, /device:TPU:1, one launch (start us, length us, event | category | flops | bytes accessed | tf_op | source)
XLA Modules:
  0.0 105.9 jit_solution(12145911566851668387)
XLA Ops:
  0.6 1.1 %slice.3 = bf16[8,32768]{1,0:T(8,128)(2,1)S(1)} slice(bf16[8,131072]{1,0:T(8,128)(2,1)} %refs_2_.3), slice={[0:8], [0:32768]} | slice | bytes 1048576 | tf_op jit(solution)/shard_map/slice | solution.py:300
  1.7 4.5 %collective-permute-start = (bf16[8,32768]{1,0:T(8,128)(2,1)S(1)}, bf16[8,32768]{1,0:T(8,128)(2,1)S(1)}, u32[]{:S(2)}, u32[]{:S(2)}) collective-permute-start(bf16[8,32768]{1,0:T(8,128)(2,1)S(1)} %slice.3), channel_id=1, source_target_pairs={{1,0},{2,1},{3,2},{4,3},{5,4},{6,5},{7,6},{8,7},{9,8},{10,9},{11,1... | collective-permute-start | bytes 1572872 | tf_op jit(solution)/shard_map/ppermute | solution.py:281
  6.2 14.0 %channelize.2 = (bf16[256,32,128]{2,1,0:T(8,128)(2,1)}, f32[8,128]{1,0:T(8,128)}) custom-call(s32[8]{0:T(128)} %refs_0_.3, s32[8]{0:T(128)} %refs_1_.3, bf16[8,131072]{1,0:T(8,128)(2,1)} %refs_2_.3, s32[8,64]{1,0:T(8,128)} %refs_3_.3, bf16[256,512]{1,0:T(8,128)(2,1)} %constant.10.clone.refs_4_, f32[128,256]{1,0:T(8,128)} %constant.11.clone.refs_5_, ...), custom_call_target="tpu_custom_call" | custom-call | tf_op jit(solution)/shard_map/channelize/pallas_call | solution.py:187
  20.3 0.0 collective-permute-done.refs_8_
  20.3 8.1 %channelize.3 = (bf16[256,32,128]{2,1,0:T(8,128)(2,1)}, f32[8,128]{1,0:T(8,128)}) custom-call(s32[8]{0:T(128)} %refs_0_.3, s32[8]{0:T(128)} %refs_1_.3, bf16[8,131072]{1,0:T(8,128)(2,1)} %refs_2_.3, s32[8,64]{1,0:T(8,128)} %refs_3_.3, bf16[256,512]{1,0:T(8,128)(2,1)} %constant.10.clone.refs_4_, ...), custom_call_target="tpu_custom_call", output_to_operand_aliasing={{0}: (10, {})} | custom-call | tf_op jit(solution)/shard_map/channelize/pallas_call | solution.py:187
  28.3 0.0 copy-start
  28.4 14.0 %all-to-all-start = ((bf16[256,32,128]{2,1,0:T(8,128)(2,1)}), bf16[256,32,128]{2,1,0:T(8,128)(2,1)S(1)}, u32[]{:S(2)}, u32[]{:S(2)}) async-start(bf16[256,32,128]{2,1,0:T(8,128)(2,1)} %get-tuple-element.10), calls=%async_computation | async-start | bytes 4194304 | tf_op jit(solution)/shard_map/all_to_all | solution.py:314
  42.3 0.0 copy-done
  42.4 1.5 %collective-permute-start.1 = (f32[8,128]{1,0:T(8,128)S(1)}, f32[8,128]{1,0:T(8,128)S(1)}, u32[]{:S(2)}, u32[]{:S(2)}) collective-permute-start(f32[8,128]{1,0:T(8,128)S(1)} %copy-done), channel_id=1, source_target_pairs={{0,1},{1,0},{2,3},{3,2},{4,5},{5,4},{6,7},{7,6},{8,9},{9,8},{10,11... | collective-permute-start | bytes 12296 | tf_op jit(solution)/shard_map/ppermute | solution.py:288
  43.8 2.2 %collective-permute-done.1 = f32[8,128]{1,0:T(8,128)S(1)} collective-permute-done((f32[8,128]{1,0:T(8,128)S(1)}, f32[8,128]{1,0:T(8,128)S(1)}, u32[]{:S(2)}, u32[]{:S(2)}) %collective-permute-start.1) | collective-permute-done | bytes 4128 | tf_op jit(solution)/shard_map/ppermute | solution.py:288
  46.0 2.2 %collective-permute-start.2 = (f32[8,128]{1,0:T(8,128)S(1)}, f32[8,128]{1,0:T(8,128)S(1)}, u32[]{:S(2)}, u32[]{:S(2)}) collective-permute-start(f32[8,128]{1,0:T(8,128)S(1)} %add.18), channel_id=1, source_target_pairs={{0,2},{2,0},{4,6},{6,4},{8,10},{10,8},{12,14},{14,12},{16,18},{18,... | collective-permute-start | bytes 12296 | tf_op jit(solution)/shard_map/ppermute | solution.py:288
  48.2 0.8 collective-permute-done.2
  49.0 3.7 %collective-permute-start.5 = (f32[8,128]{1,0:T(8,128)S(1)}, f32[8,128]{1,0:T(8,128)S(1)}, u32[]{:S(2)}, u32[]{:S(2)}) collective-permute-start(f32[8,128]{1,0:T(8,128)S(1)} %add.19), channel_id=1, source_target_pairs={{0,12},{2,14},{4,8},{6,10},{8,4},{10,6},{12,0},{14,2},{16,28},{18,... | collective-permute-start | bytes 12296 | tf_op jit(solution)/shard_map/ppermute | solution.py:288
  52.7 0.0 collective-permute-start.4
  52.7 0.3 collective-permute-start.3
  53.0 34.6 %collective-permute-done.5 = f32[8,128]{1,0:T(8,128)S(1)} collective-permute-done((f32[8,128]{1,0:T(8,128)S(1)}, f32[8,128]{1,0:T(8,128)S(1)}, u32[]{:S(2)}, u32[]{:S(2)}) %collective-permute-start.5) | collective-permute-done | bytes 4128 | tf_op jit(solution)/shard_map/ppermute | solution.py:288
  87.6 0.3 collective-permute-done.4
  87.8 0.0 collective-permute-done.3
  87.8 6.4 %all-to-all-done.refs_0_ = bf16[256,32,128]{2,1,0:T(8,128)(2,1)S(1)} async-done(((bf16[256,32,128]{2,1,0:T(8,128)(2,1)}), bf16[256,32,128]{2,1,0:T(8,128)(2,1)S(1)}, u32[]{:S(2)}, u32[]{:S(2)}) %all-to-all-start) | async-done | bytes 2097184 | tf_op jit(solution)/shard_map/all_to_all | solution.py:314
  94.3 4.0 %collective-permute-start.6 = (f32[8,128]{1,0:T(8,128)S(1)}, f32[8,128]{1,0:T(8,128)S(1)}, u32[]{:S(2)}, u32[]{:S(2)}) collective-permute-start(f32[8,128]{1,0:T(8,128)S(1)} %add_add_fusion), channel_id=1, source_target_pairs={{0,16},{2,18},{4,20},{6,22},{8,24},{10,26},{12,28},{14,30},{16,0},... | collective-permute-start | bytes 12296 | tf_op jit(solution)/shard_map/ppermute | solution.py:288
  98.2 7.1 %correlate.1 = f32[64,8192]{1,0:T(8,128)} custom-call(bf16[256,32,128]{2,1,0:T(8,128)(2,1)S(1)} %all-to-all-done.refs_0_), custom_call_target="tpu_custom_call" | custom-call | tf_op jit(solution)/shard_map/correlate/pallas_call | solution.py:263
  105.3 0.0 collective-permute-done.6
  105.3 0.6 add_multiply_fusion
  (3 shorter events, 0.0 us)
Async XLA Ops:
  1.7 18.5 %collective-permute-start = (bf16[8,32768]{1,0:T(8,128)(2,1)S(1)}, bf16[8,32768]{1,0:T(8,128)(2,1)S(1)}, u32[]{:S(2)}, u32[]{:S(2)}) collective-permute-start(bf16[8,32768]{1,0:T(8,128)(2,1)S(1)} %slice.3), channel_id=1, source_target_pairs={{1,0},{2,1},{3,2},{4,3},{5,4},{6,5},{7,6},{8,7},{9,8},{10,9},{11,1... | collective-permute-start | bytes 1572872 | tf_op jit(solution)/shard_map/ppermute | solution.py:281
  28.3 14.0 %copy-start = (f32[8,128]{1,0:T(8,128)S(1)}, f32[8,128]{1,0:T(8,128)}, u32[]{:S(2)}) copy-start(f32[8,128]{1,0:T(8,128)} %get-tuple-element.11) | copy-start | bytes 12292
  28.4 65.9 %all-to-all-start = ((bf16[256,32,128]{2,1,0:T(8,128)(2,1)}), bf16[256,32,128]{2,1,0:T(8,128)(2,1)S(1)}, u32[]{:S(2)}, u32[]{:S(2)}) async-start(bf16[256,32,128]{2,1,0:T(8,128)(2,1)} %get-tuple-element.10), calls=%async_computation | async-start | bytes 4194304 | tf_op jit(solution)/shard_map/all_to_all | solution.py:314
  42.4 3.6 %collective-permute-start.1 = (f32[8,128]{1,0:T(8,128)S(1)}, f32[8,128]{1,0:T(8,128)S(1)}, u32[]{:S(2)}, u32[]{:S(2)}) collective-permute-start(f32[8,128]{1,0:T(8,128)S(1)} %copy-done), channel_id=1, source_target_pairs={{0,1},{1,0},{2,3},{3,2},{4,5},{5,4},{6,7},{7,6},{8,9},{9,8},{10,11... | collective-permute-start | bytes 12296 | tf_op jit(solution)/shard_map/ppermute | solution.py:288
  46.0 3.0 %collective-permute-start.2 = (f32[8,128]{1,0:T(8,128)S(1)}, f32[8,128]{1,0:T(8,128)S(1)}, u32[]{:S(2)}, u32[]{:S(2)}) collective-permute-start(f32[8,128]{1,0:T(8,128)S(1)} %add.18), channel_id=1, source_target_pairs={{0,2},{2,0},{4,6},{6,4},{8,10},{10,8},{12,14},{14,12},{16,18},{18,... | collective-permute-start | bytes 12296 | tf_op jit(solution)/shard_map/ppermute | solution.py:288
  49.0 38.5 %collective-permute-start.5 = (f32[8,128]{1,0:T(8,128)S(1)}, f32[8,128]{1,0:T(8,128)S(1)}, u32[]{:S(2)}, u32[]{:S(2)}) collective-permute-start(f32[8,128]{1,0:T(8,128)S(1)} %add.19), channel_id=1, source_target_pairs={{0,12},{2,14},{4,8},{6,10},{8,4},{10,6},{12,0},{14,2},{16,28},{18,... | collective-permute-start | bytes 12296 | tf_op jit(solution)/shard_map/ppermute | solution.py:288
  52.7 35.1 %collective-permute-start.4 = (f32[8,128]{1,0:T(8,128)S(1)}, f32[8,128]{1,0:T(8,128)S(1)}, u32[]{:S(2)}, u32[]{:S(2)}) collective-permute-start(f32[8,128]{1,0:T(8,128)S(1)} %add.19), channel_id=1, source_target_pairs={{0,8},{2,10},{4,12},{6,14},{8,0},{10,2},{12,4},{14,6},{16,24},{18,... | collective-permute-start | bytes 12296 | tf_op jit(solution)/shard_map/ppermute | solution.py:288
  52.7 35.1 %collective-permute-start.3 = (f32[8,128]{1,0:T(8,128)S(1)}, f32[8,128]{1,0:T(8,128)S(1)}, u32[]{:S(2)}, u32[]{:S(2)}) collective-permute-start(f32[8,128]{1,0:T(8,128)S(1)} %add.19), channel_id=1, source_target_pairs={{0,4},{2,6},{4,0},{6,2},{8,12},{10,14},{12,8},{14,10},{16,20},{18,... | collective-permute-start | bytes 12296 | tf_op jit(solution)/shard_map/ppermute | solution.py:288
  94.3 11.0 %collective-permute-start.6 = (f32[8,128]{1,0:T(8,128)S(1)}, f32[8,128]{1,0:T(8,128)S(1)}, u32[]{:S(2)}, u32[]{:S(2)}) collective-permute-start(f32[8,128]{1,0:T(8,128)S(1)} %add_add_fusion), channel_id=1, source_target_pairs={{0,16},{2,18},{4,20},{6,22},{8,24},{10,26},{12,28},{14,30},{16,0},... | collective-permute-start | bytes 12296 | tf_op jit(solution)/shard_map/ppermute | solution.py:288

commit v4 on v2

v4 whole, which is shorter than its diff:
```python
import math

import jax
import jax.numpy as jnp
import ml_dtypes
import numpy as np
from jax import lax
from jax.experimental import pallas as pl
from jax.experimental.pallas import tpu as pltpu
from jax.sharding import PartitionSpec as P

S = 64
NCH = 16384
FA = 256
FB = 128
NTONE = 64
MAXD = 32768
NQ = FB // 2
NHI = 4
LO = FA // NHI
LANES = 128

f32 = jnp.float32
bf16 = jnp.bfloat16


def make_tables():
    k1 = np.arange(FA)
    angles = 2.0 * np.pi / FA * (k1[:, None] * k1[None, :] % FA)
    section_one = np.concatenate([np.cos(angles), -np.sin(angles)], axis=1).astype(
        ml_dtypes.bfloat16
    )
    n2 = np.arange(FB)
    length = FA * FB
    twists = 2.0 * np.pi / length * (n2[:, None] * k1[None, :] % length)
    scale = 1.0 / math.sqrt(length)
    twist_cos = (np.cos(twists) * scale).astype(np.float32)
    twist_sin = (np.sin(twists) * scale).astype(np.float32)
    q = np.arange(NQ)
    thetas = 2.0 * np.pi / FB * (q[:, None] * n2[None, :] % FB)
    cosine, sine = np.cos(thetas), np.sin(thetas)
    section_two = np.block([[cosine, sine], [-sine, cosine]]).astype(ml_dtypes.bfloat16)
    return (section_one, twist_cos, twist_sin, section_two)


OPITCH = NQ + 8
PIECES = 4
GROUP = (8, 2)
UNROLL = (1, 2)


def f_kernel(nt, at_row, more, delays, valid, *refs):
    stream, one, tcos, tsin, two = refs[:5]
    xs, obuf, mbuf, out_sem = refs[-4:]
    stations = stream.shape[0]
    rows = nt * FA
    chunk = FA * LANES
    pitch = xs.shape[0] // stations

    def spread(source, to):
        def one_row(j, _):
            at = pl.multiple_of(j * LANES, LANES)
            xs[pl.ds(to + j, stations, stride=pitch), :] = source[:, pl.ds(at, LANES)].astype(
                f32
            )
            return 0

        count = source.shape[1] // LANES
        lax.fori_loop(0, count, one_row, 0, unroll=16)
        return to + count

    filled = 0
    if more:
        trail, msgs = refs[5], refs[7]
        for source in (stream, trail):
            filled = spread(source, filled)
    else:
        msgs, tail, xin, in_sem = refs[5:9]
        targets = [xin.at[:, pl.ds(i * chunk, chunk)] for i in range(nt)] + [tail]
        copies = [
            pltpu.make_async_copy(stream.at[:, pl.ds(i * chunk, chunk)], target, in_sem.at[i])
            for i, target in enumerate(targets)
        ]
        for copy in copies:
            copy.start()
        for copy, target in zip(copies, targets):
            copy.wait()
            filled = spread(target, filled)
    xs[pl.ds(filled, stations, stride=pitch), :] = jnp.zeros((stations, LANES), f32)
    src = lax.broadcasted_iota(jnp.int32, (2 * LANES, LANES), 0)
    dst = lax.broadcasted_iota(jnp.int32, (2 * LANES, LANES), 1)
    low = lax.broadcasted_iota(jnp.int32, (NQ, LANES), 1) < LO

    def group(g, _):
        blocks = []
        for k in range(GROUP[nt > 1]):
            s = g * GROUP[nt > 1] + k
            shift = delays[s]
            lead = shift // LANES
            within = shift - lead * LANES
            first = xs[pl.ds(s * pitch + lead, rows), :]
            second = xs[pl.ds(s * pitch + lead + 1, rows), :]
            pair = jnp.concatenate([first.astype(bf16), second.astype(bf16)], axis=1)
            move = (src == dst + within).astype(f32).astype(bf16)
            moved = jnp.dot(pair, move, preferred_element_type=f32).astype(bf16)
            blocks += [moved[t * FA : (t + 1) * FA] for t in range(nt)]
        sections = lax.dot_general(
            jnp.concatenate(blocks, axis=1),
            one[...],
            (((0,), (0,)), ((), ())),
            preferred_element_type=f32,
        )
        for k in range(GROUP[nt > 1]):
            s = g * GROUP[nt > 1] + k
            last = (two[...].astype(f32) * valid[s].astype(f32)).astype(bf16)
            for t in range(nt):
                at = (k * nt + t) * FB
                re, im = sections[at : at + FB, :FA], sections[at : at + FB, FA:]
                cosine, sine = tcos[...], tsin[...]
                tr = (re * cosine + im * sine).astype(bf16)
                ti = (im * cosine - re * sine).astype(bf16)
                spec = jnp.dot(
                    last, jnp.concatenate([tr, ti], axis=0), preferred_element_type=f32
                )
                for j in range(FA // LANES):
                    a = spec[:NQ, j * LANES : (j + 1) * LANES]
                    b = spec[NQ:, j * LANES : (j + 1) * LANES]
                    even = jnp.where(low, a, pltpu.roll(b, LO, 1))
                    odd = jnp.where(low, pltpu.roll(a, LO, 1), b)
                    for h, piece in ((2 * j, even), (2 * j + 1, odd)):
                        to = pl.multiple_of(((h * nt + t) * stations + s) * OPITCH, 8)
                        obuf[pl.ds(to, NQ), :] = piece
        return 0

    lax.fori_loop(0, stations // GROUP[nt > 1], group, 0, unroll=UNROLL[nt > 1])

    per = NQ // PIECES
    sent = []
    for i in range(PIECES):

        def gather(q, _):
            for h in range(NHI):
                got = obuf[
                    pl.ds(h * nt * stations * OPITCH + q, nt * stations, stride=OPITCH), :
                ]
                mbuf[q * NHI + h] = got.astype(bf16)
            return 0

        lax.fori_loop(i * per, (i + 1) * per, gather, 0, unroll=4)
        span = pl.ds(i * per * NHI, per * NHI)
        sent.append(
            pltpu.make_async_copy(
                mbuf.at[span], msgs.at[span, pl.ds(at_row, nt * stations), :], out_sem.at[i]
            )
        )
        sent[i].start()
    for copy in sent:
        copy.wait()


def on_chip(value):
    return pltpu.with_memory_space_constraint(value, pltpu.VMEM)


def off_chip(value):
    return pltpu.with_memory_space_constraint(value, pltpu.HBM)


def channelized(stream, delays, valid, tables, so_far=()):
    stations = stream.shape[0]
    smem = pl.BlockSpec(memory_space=pltpu.SMEM)
    vmem = pl.BlockSpec(memory_space=pltpu.VMEM)
    hbm = pl.BlockSpec(memory_space=pltpu.HBM)
    chunk = FA * LANES
    here = stream.shape[1] // chunk
    if so_far:
        msgs, trailing = so_far
        nt, at_row = 1, msgs.shape[1] - stations
        rows = (stream.shape[1] + trailing.shape[1]) // LANES
        stream = on_chip(stream)
        tables = [on_chip(jnp.asarray(table)) for table in tables]
        extra = (on_chip(trailing), off_chip(msgs))
        specs = [smem, smem] + [vmem] * 6 + [hbm]
        outs, out_specs = pltpu.HBM(msgs.shape, bf16), hbm
        aliases = {8: 0}
        buffers = []
    else:
        nt, at_row, extra = here - 1, 0, ()
        stream = off_chip(stream)
        rows = here * FA
        specs = [smem, smem, hbm] + [vmem] * 4
        outs = (
            pltpu.HBM((NQ * NHI, here * stations, LANES), bf16),
            pltpu.VMEM((stations, chunk), bf16),
        )
        out_specs = (hbm, vmem)
        aliases = {}
        buffers = [
            pltpu.VMEM((stations, nt * chunk), bf16),
            pltpu.SemaphoreType.DMA((here,)),
        ]
    pitch = (rows // 16 + 1) * 16 + 8
    return pl.pallas_call(
        lambda *refs: f_kernel(nt, at_row, bool(so_far), *refs),
        out_shape=outs,
        in_specs=specs,
        out_specs=out_specs,
        scratch_shapes=buffers
        + [
            pltpu.VMEM((stations * pitch, LANES), f32),
            pltpu.VMEM((NHI * nt * stations * OPITCH, LANES), f32),
            pltpu.VMEM((NQ * NHI, nt * stations, LANES), bf16),
            pltpu.SemaphoreType.DMA((PIECES,)),
        ],
        input_output_aliases=aliases,
        compiler_params=pltpu.CompilerParams(vmem_limit_bytes=28 << 20),
        name="channelize",
    )(delays, valid, stream, *tables, *extra)


def tone_kernel(tones, msgs, picks):
    stations, count = tones.shape
    sub = lax.broadcasted_iota(jnp.int32, (stations, LANES), 0)
    slot = lax.broadcasted_iota(jnp.int32, (stations, LANES), 1) % NTONE

    def one_tone(k, acc):
        for s in range(stations):
            chan = tones[s, k]
            place = chan // LO
            within = chan - place * LO
            tile = msgs[place].astype(f32)
            total = tile[:stations]
            for t in range(1, tile.shape[0] // stations):
                total = total + tile[t * stations : (t + 1) * stations]
            turned = pltpu.roll(total, (k - within + LANES) % LANES, 1)
            acc = jnp.where((sub == s) & (slot == k), turned, acc)
        return acc

    picks[...] = lax.fori_loop(0, count, one_tone, jnp.zeros((stations, LANES), f32), unroll=2)


def tone_sums(msgs, tone_chan):
    return pl.pallas_call(
        tone_kernel,
        out_shape=jax.ShapeDtypeStruct((tone_chan.shape[0], 2 * NTONE), f32),
        in_specs=[
            pl.BlockSpec(memory_space=pltpu.SMEM),
            pl.BlockSpec(memory_space=pltpu.VMEM),
        ],
        out_specs=pl.BlockSpec(memory_space=pltpu.VMEM),
        compiler_params=pltpu.CompilerParams(vmem_limit_bytes=8 << 20),
        name="tones",
    )(tone_chan, msgs)


PITCH = 136


def x_kernel(norm_scale, per_source, recv, vis, rs, ts, gs):
    sources, rows, _ = recv.shape
    local = per_source
    groups = S // local
    times = sources // groups * rows // local

    def widen(i, _):
        at = pl.multiple_of(i * rows, rows)
        rs[pl.ds(at, rows), :] = recv[i].astype(f32)
        return 0

    lax.fori_loop(0, sources, widen, 0, unroll=8)

    def turn(i, _):
        g = i // local
        s = i - g * local
        got = rs[pl.ds(g * times * local + s, times, stride=local), :]
        ts[pl.ds(pl.multiple_of(i * PITCH, 8), LANES), :] = got.T
        return 0

    lax.fori_loop(0, S, turn, 0, unroll=True)

    lane = lax.broadcasted_iota(jnp.int32, (8, LANES), 1)

    def eight(o, _):
        base = o * 8
        for c in range(8):
            re = ts[pl.ds(base + c, S, stride=PITCH), :]
            im = ts[pl.ds(base + c + LO, S, stride=PITCH), :]
            plus, quad, minus = re.astype(bf16), im.astype(bf16), (-re).astype(bf16)
            straight = jnp.concatenate([plus, quad], axis=1)
            turned = jnp.concatenate([quad, minus], axis=1)
            left = jnp.concatenate([straight, turned], axis=0)
            right = jnp.concatenate([straight, straight], axis=0)
            gram = lax.dot_general(
                left, right, (((1,), (1,)), ((), ())), preferred_element_type=f32
            )
            gs[pl.ds(c * PITCH, 2 * S), :] = gram * norm_scale
        top = pl.multiple_of(base, 8)
        for j in range(S):
            even = gs[pl.ds(2 * j, 8, stride=PITCH), :]
            odd = gs[pl.ds(2 * j + 1, 8, stride=PITCH), :]
            vis[pl.ds(top, 8), pl.ds(j * LANES, LANES)] = jnp.where(lane < S, even, odd)
        return 0

    lax.fori_loop(0, LO // 8, eight, 0, unroll=True)


def correlated(recv, per_source, norm_scale):
    vmem = pl.BlockSpec(memory_space=pltpu.VMEM)
    return pl.pallas_call(
        lambda *refs: x_kernel(norm_scale, per_source, *refs),
        out_shape=jax.ShapeDtypeStruct((LO, 2 * S * S), f32),
        in_specs=[vmem],
        out_specs=vmem,
        scratch_shapes=[
            pltpu.VMEM((recv.shape[0] * recv.shape[1], LANES), f32),
            pltpu.VMEM((S * PITCH, LANES), f32),
            pltpu.VMEM((8 * PITCH, LANES), f32),
        ],
        compiler_params=pltpu.CompilerParams(vmem_limit_bytes=24 << 20),
        name="correlate",
    )(on_chip(recv))


def passed_along(block, axis, distance):
    devices = range(lax.axis_size(axis))
    route = [(i - distance, i) for i in devices if i - distance in devices]
    return lax.ppermute(block, axis, route)


def routed(value, axis, dest):
    return lax.ppermute(value, axis, [(i, dest(i)) for i in range(lax.axis_size(axis))])


def gathered_sum(picks):
    value = picks + routed(picks, "cores", lambda i: i ^ 1)
    value = value + routed(value, "tm", lambda i: i ^ 1)
    size = lax.axis_size("tm")
    half = size // 4
    steps = [
        routed(value, "tm", lambda i, d=d: (i + 2 * (d + half * (i % 2))) % size)
        for d in range(half)
    ]
    value = sum(steps)
    return value + routed(value, "tm", lambda i: i ^ 1)


def shards(samples, delays, valid, tone_chan):
    stations, stretch = samples.shape
    whole = ("stn", "tm", "cores")
    here = stretch // (FA * FB)
    trailing = passed_along(samples[:, :MAXD], ("tm", "cores"), -1)
    own = (delays, valid, make_tables())
    msgs, tail = channelized(samples, *own)
    msgs = channelized(tail, *own, (msgs, trailing))
    spectra_all = here * lax.axis_size("tm") * lax.axis_size("cores")
    norm_scale = 1.0 / math.sqrt(spectra_all)
    recv = lax.all_to_all(msgs, whole, split_axis=0, concat_axis=0, tiled=True)
    phase_cal = gathered_sum(tone_sums(msgs, tone_chan)) * norm_scale
    return (correlated(recv, stations, norm_scale), phase_cal)


def solution(mesh):
    return jax.shard_map(
        shards,
        mesh=mesh,
        in_specs=(P("stn", ("tm", "cores")), P("stn"), P("stn"), P("stn", None)),
        out_specs=(P(("stn", "tm", "cores"), None), P("stn", None)),
        check_vma=False,
    )
```

time: 164 us -> 96.4 us (0.59)
  starting transfers between devices: 120 us -> 34.5 us
  waiting for transfers between devices: 3.27 us -> 29 us
  Pallas kernels: 34.2 us -> 25.2 us
    ppermute x31 -> x7, starting transfers between devices: 101 us -> 14.9 us  [routed(): lax.ppermute(value, axis, [(i, dest(i)) for i in range(lax.axis_size(axis...]
    ppermute x31 -> x7, waiting for transfers between devices: 3.26 us -> 28.9 us  [routed(): lax.ppermute(value, axis, [(i, dest(i)) for i in range(lax.axis_size(axis...]
    pallas_call x2 -> x3, Pallas kernels: 25.6 us -> 18.7 us  [the longest x2 11.7 us: channelized(): pl.pallas_call(lambda *refs: f_kernel(nt, at_row, bool(so_far), *refs), o...]
    unnamed x8 -> x18, local copies, waits for them, and re-layouts: 2.17 us -> 4.92 us
    pallas_call x1, Pallas kernels: 8.65 us -> 6.52 us  [correlated(): pl.pallas_call(lambda *refs: x_kernel(norm_scale, per_source, *refs), out...]
  transfers between devices with their start and end apart: 33 -> 9, of which waited for: 3 -> 6; matrix products, arithmetic and copies ran while one was open for 1% -> 1% of each run, Pallas kernels for 9% -> 16%
where the time goes in v4:
time: 96.4 us; the launch traced here: 96 us
  starting transfers between devices  34.5 us (36%)
  waiting for transfers between devices  29 us (30%)
  Pallas kernels  25.2 us (26%)
  local copies, waits for them, and re-layouts  6.04 us (6%)
    ppermute x7, waiting for transfers between devices, routed(): lax.ppermute(value, axis, [(i, dest(i)) for i in range(lax.axis_size(axis...  28.9 us
    all_to_all x1, starting transfers between devices, shards(): recv = lax.all_to_all(msgs, whole, split_axis=0, concat_axis=0, tiled=True)  15 us
    ppermute x7, starting transfers between devices, routed(): lax.ppermute(value, axis, [(i, dest(i)) for i in range(lax.axis_size(axis...  14.9 us
    pallas_call x2, Pallas kernels, channelized(): pl.pallas_call(lambda *refs: f_kernel(nt, at_row, bool(so_far), *refs), o...  11.7 us
    pallas_call x1, Pallas kernels, tone_sums(): pl.pallas_call(tone_kernel, out_shape=jax.ShapeDtypeStruct((tone_chan.sha...  6.98 us
    pallas_call x1, Pallas kernels, correlated(): pl.pallas_call(lambda *refs: x_kernel(norm_scale, per_source, *refs), out...  6.52 us
    unnamed x18, local copies, waits for them, and re-layouts  4.92 us
    ppermute x1, starting transfers between devices, passed_along(): return lax.ppermute(block, axis, route)  4.51 us
  transfers between devices with their start and end apart: 9, of which 6 were waited for; matrix products, arithmetic and copies ran while one was open for 1% of the time, Pallas kernels for 16%

profile of v4, /device:TPU:1, one launch (start us, length us, event | category | flops | bytes accessed | tf_op | source)
XLA Modules:
  0.0 96.0 jit_solution(11333158975222739829)
XLA Ops:
  0.6 1.1 %slice.3 = bf16[8,32768]{1,0:T(8,128)(2,1)S(1)} slice(bf16[8,131072]{1,0:T(8,128)(2,1)} %refs_2_.1), slice={[0:8], [0:32768]} | slice | bytes 1048576 | tf_op jit(solution)/shard_map/slice | solution.py:351
  1.8 4.5 %collective-permute-start = (bf16[8,32768]{1,0:T(8,128)(2,1)S(1)}, bf16[8,32768]{1,0:T(8,128)(2,1)S(1)}, u32[]{:S(2)}, u32[]{:S(2)}) collective-permute-start(bf16[8,32768]{1,0:T(8,128)(2,1)S(1)} %slice.3), channel_id=1, source_target_pairs={{1,0},{2,1},{3,2},{4,3},{5,4},{6,5},{7,6},{8,7},{9,8},{10,9},{11,1... | collective-permute-start | bytes 1572872 | tf_op jit(solution)/shard_map/ppermute | solution.py:327
  6.3 0.9 copy-done.1
  7.2 0.9 copy-done.3
  8.1 0.9 copy-done.4
  9.0 0.8 copy-done.5
  9.9 0.7 copy-done.7
  10.5 0.7 copy-done.8
  11.2 8.2 %channelize.2 = (bf16[256,32,128]{2,1,0:T(8,128)(2,1)}, bf16[8,32768]{1,0:T(8,128)(2,1)S(1)}) custom-call(s32[8]{0:T(128)S(1)} %copy-done.7, s32[8]{0:T(128)S(1)} %copy-done.8, bf16[8,131072]{1,0:T(8,128)(2,1)} %refs_2_.1, bf16[256,512]{1,0:T(8,128)(2,1)S(1)} %copy-done.1, f32[128,256]{1,0:T(8,128)S(1)} %copy-done.4, f32[128,256]{1,0:T(8,128)S(1)} %copy-done.3, ...), custom_call_target="tpu_custom_call" | custom-call | tf_op jit(solution)/shard_map/channelize/pallas_call | solution.py:203
  19.4 3.5 %channelize.3.msgs = bf16[256,32,128]{2,1,0:T(8,128)(2,1)} custom-call(s32[8]{0:T(128)S(1)} %copy-done.7, s32[8]{0:T(128)S(1)} %copy-done.8, bf16[8,32768]{1,0:T(8,128)(2,1)S(1)} %get-tuple-element.4.refs_2_, bf16[256,512]{1,0:T(8,128)(2,1)S(1)} %copy-done.2, f32[128,256]{1,0:T(8,128)S(1)} %copy-done.4, ...), custom_call_target="tpu_custom_call", output_to_operand_aliasing={{}: (8, {})} | custom-call | tf_op jit(solution)/shard_map/channelize/pallas_call | solution.py:203
  23.0 15.0 %all-to-all-start = ((bf16[256,32,128]{2,1,0:T(8,128)(2,1)}), bf16[256,32,128]{2,1,0:T(8,128)(2,1)}, u32[]{:S(2)}, u32[]{:S(2)}) async-start(bf16[256,32,128]{2,1,0:T(8,128)(2,1)} %channelize.3.msgs), calls=%async_computation | async-start | bytes 4194304 | tf_op jit(solution)/shard_map/all_to_all | solution.py:357
  38.0 7.0 %tones.2 = f32[8,128]{1,0:T(8,128)S(1)} custom-call(s32[8,64]{1,0:T(8,128)S(1)} %copy-done.6, bf16[256,32,128]{2,1,0:T(8,128)(2,1)S(1)} %copy-done), custom_call_target="tpu_custom_call" | custom-call | tf_op jit(solution)/shard_map/tones/pallas_call | solution.py:243
  45.0 1.4 %collective-permute-start.1 = (f32[8,128]{1,0:T(8,128)S(1)}, f32[8,128]{1,0:T(8,128)S(1)}, u32[]{:S(2)}, u32[]{:S(2)}) collective-permute-start(f32[8,128]{1,0:T(8,128)S(1)} %tones.2), channel_id=1, source_target_pairs={{0,1},{1,0},{2,3},{3,2},{4,5},{5,4},{6,7},{7,6},{8,9},{9,8},{10,11... | collective-permute-start | bytes 12296 | tf_op jit(solution)/shard_map/ppermute | solution.py:331
  46.4 1.6 %collective-permute-done.1 = f32[8,128]{1,0:T(8,128)S(1)} collective-permute-done((f32[8,128]{1,0:T(8,128)S(1)}, f32[8,128]{1,0:T(8,128)S(1)}, u32[]{:S(2)}, u32[]{:S(2)}) %collective-permute-start.1) | collective-permute-done | bytes 4128 | tf_op jit(solution)/shard_map/ppermute | solution.py:331
  48.1 2.9 %collective-permute-start.2 = (f32[8,128]{1,0:T(8,128)S(1)}, f32[8,128]{1,0:T(8,128)S(1)}, u32[]{:S(2)}, u32[]{:S(2)}) collective-permute-start(f32[8,128]{1,0:T(8,128)S(1)} %add.18), channel_id=1, source_target_pairs={{0,2},{2,0},{4,6},{6,4},{8,10},{10,8},{12,14},{14,12},{16,18},{18,... | collective-permute-start | bytes 12296 | tf_op jit(solution)/shard_map/ppermute | solution.py:331
  50.9 0.8 collective-permute-done.2
  51.8 2.4 %collective-permute-start.6 = (f32[8,128]{1,0:T(8,128)S(1)}, f32[8,128]{1,0:T(8,128)S(1)}, u32[]{:S(2)}, u32[]{:S(2)}) collective-permute-start(f32[8,128]{1,0:T(8,128)S(1)} %add.19), channel_id=1, source_target_pairs={{0,12},{2,30},{4,16},{6,2},{8,20},{10,6},{12,24},{14,10},{16,28},{... | collective-permute-start | bytes 12296 | tf_op jit(solution)/shard_map/ppermute | solution.py:331
  54.2 1.6 %collective-permute-start.5 = (f32[8,128]{1,0:T(8,128)S(1)}, f32[8,128]{1,0:T(8,128)S(1)}, u32[]{:S(2)}, u32[]{:S(2)}) collective-permute-start(f32[8,128]{1,0:T(8,128)S(1)} %add.19), channel_id=1, source_target_pairs={{0,8},{2,26},{4,12},{6,30},{8,16},{10,2},{12,20},{14,6},{16,24},{1... | collective-permute-start | bytes 12296 | tf_op jit(solution)/shard_map/ppermute | solution.py:331
  56.4 6.0 %collective-permute-start.3 = (f32[8,128]{1,0:T(8,128)S(1)}, f32[8,128]{1,0:T(8,128)S(1)}, u32[]{:S(2)}, u32[]{:S(2)}) collective-permute-start(f32[8,128]{1,0:T(8,128)S(1)} %add.19), channel_id=1, source_target_pairs={{0,0},{2,18},{4,4},{6,22},{8,8},{10,26},{12,12},{14,30},{16,16},{1... | collective-permute-start | bytes 12296 | tf_op jit(solution)/shard_map/ppermute | solution.py:331
  62.4 19.6 %collective-permute-done.6 = f32[8,128]{1,0:T(8,128)S(1)} collective-permute-done((f32[8,128]{1,0:T(8,128)S(1)}, f32[8,128]{1,0:T(8,128)S(1)}, u32[]{:S(2)}, u32[]{:S(2)}) %collective-permute-start.6) | collective-permute-done | bytes 4128 | tf_op jit(solution)/shard_map/ppermute | solution.py:331
  82.0 0.6 collective-permute-done.5
  82.6 5.1 %collective-permute-done.3 = f32[8,128]{1,0:T(8,128)S(1)} collective-permute-done((f32[8,128]{1,0:T(8,128)S(1)}, f32[8,128]{1,0:T(8,128)S(1)}, u32[]{:S(2)}, u32[]{:S(2)}) %collective-permute-start.3) | collective-permute-done | bytes 4128 | tf_op jit(solution)/shard_map/ppermute | solution.py:331
  87.8 1.2 %collective-permute-done.7 = f32[8,128]{1,0:T(8,128)S(1)} collective-permute-done((f32[8,128]{1,0:T(8,128)S(1)}, f32[8,128]{1,0:T(8,128)S(1)}, u32[]{:S(2)}, u32[]{:S(2)}) %collective-permute-start.7) | collective-permute-done | bytes 4128 | tf_op jit(solution)/shard_map/ppermute | solution.py:331
  89.5 6.5 %correlate.1 = f32[64,8192]{1,0:T(8,128)} custom-call(bf16[256,32,128]{2,1,0:T(8,128)(2,1)} %all-to-all-done.refs_0_), custom_call_target="tpu_custom_call" | custom-call | tf_op jit(solution)/shard_map/correlate/pallas_call | solution.py:309
  (21 shorter events, 1.2 us)
Async XLA Ops:
  0.6 18.8 %copy-start.2 = (bf16[256,512]{1,0:T(8,128)(2,1)S(1)}, bf16[256,512]{1,0:T(8,128)(2,1)}, u32[]{:S(2)}) copy-start(bf16[256,512]{1,0:T(8,128)(2,1)} %constant.10.clone.refs_3_) | copy-start | bytes 786436
  1.8 17.7 %collective-permute-start = (bf16[8,32768]{1,0:T(8,128)(2,1)S(1)}, bf16[8,32768]{1,0:T(8,128)(2,1)S(1)}, u32[]{:S(2)}, u32[]{:S(2)}) collective-permute-start(bf16[8,32768]{1,0:T(8,128)(2,1)S(1)} %slice.3), channel_id=1, source_target_pairs={{1,0},{2,1},{3,2},{4,3},{5,4},{6,5},{7,6},{8,7},{9,8},{10,9},{11,1... | collective-permute-start | bytes 1572872 | tf_op jit(solution)/shard_map/ppermute | solution.py:327
  6.3 1.0 copy-start.1
  7.2 0.9 copy-start.3
  8.1 0.9 copy-start.4
  9.0 0.8 copy-start.5
  9.9 0.7 copy-start.7
  10.5 0.7 copy-start.8
  23.0 15.0 %copy-start = (bf16[256,32,128]{2,1,0:T(8,128)(2,1)S(1)}, bf16[256,32,128]{2,1,0:T(8,128)(2,1)}, u32[]{:S(2)}) copy-start(bf16[256,32,128]{2,1,0:T(8,128)(2,1)} %channelize.3.msgs) | copy-start | bytes 6291460
  23.0 15.0 %copy-start.6 = (s32[8,64]{1,0:T(8,128)S(1)}, s32[8,64]{1,0:T(8,128)}, u32[]{:S(2)}) copy-start(s32[8,64]{1,0:T(8,128)} %tones.3) | copy-start | bytes 6148
  23.0 66.5 %all-to-all-start = ((bf16[256,32,128]{2,1,0:T(8,128)(2,1)}), bf16[256,32,128]{2,1,0:T(8,128)(2,1)}, u32[]{:S(2)}, u32[]{:S(2)}) async-start(bf16[256,32,128]{2,1,0:T(8,128)(2,1)} %channelize.3.msgs), calls=%async_computation | async-start | bytes 4194304 | tf_op jit(solution)/shard_map/all_to_all | solution.py:357
  45.0 3.1 %collective-permute-start.1 = (f32[8,128]{1,0:T(8,128)S(1)}, f32[8,128]{1,0:T(8,128)S(1)}, u32[]{:S(2)}, u32[]{:S(2)}) collective-permute-start(f32[8,128]{1,0:T(8,128)S(1)} %tones.2), channel_id=1, source_target_pairs={{0,1},{1,0},{2,3},{3,2},{4,5},{5,4},{6,7},{7,6},{8,9},{9,8},{10,11... | collective-permute-start | bytes 12296 | tf_op jit(solution)/shard_map/ppermute | solution.py:331
  48.1 3.7 %collective-permute-start.2 = (f32[8,128]{1,0:T(8,128)S(1)}, f32[8,128]{1,0:T(8,128)S(1)}, u32[]{:S(2)}, u32[]{:S(2)}) collective-permute-start(f32[8,128]{1,0:T(8,128)S(1)} %add.18), channel_id=1, source_target_pairs={{0,2},{2,0},{4,6},{6,4},{8,10},{10,8},{12,14},{14,12},{16,18},{18,... | collective-permute-start | bytes 12296 | tf_op jit(solution)/shard_map/ppermute | solution.py:331
  51.8 30.2 %collective-permute-start.6 = (f32[8,128]{1,0:T(8,128)S(1)}, f32[8,128]{1,0:T(8,128)S(1)}, u32[]{:S(2)}, u32[]{:S(2)}) collective-permute-start(f32[8,128]{1,0:T(8,128)S(1)} %add.19), channel_id=1, source_target_pairs={{0,12},{2,30},{4,16},{6,2},{8,20},{10,6},{12,24},{14,10},{16,28},{... | collective-permute-start | bytes 12296 | tf_op jit(solution)/shard_map/ppermute | solution.py:331
  54.2 28.4 %collective-permute-start.5 = (f32[8,128]{1,0:T(8,128)S(1)}, f32[8,128]{1,0:T(8,128)S(1)}, u32[]{:S(2)}, u32[]{:S(2)}) collective-permute-start(f32[8,128]{1,0:T(8,128)S(1)} %add.19), channel_id=1, source_target_pairs={{0,8},{2,26},{4,12},{6,30},{8,16},{10,2},{12,20},{14,6},{16,24},{1... | collective-permute-start | bytes 12296 | tf_op jit(solution)/shard_map/ppermute | solution.py:331
  55.8 26.8 %collective-permute-start.4 = (f32[8,128]{1,0:T(8,128)S(1)}, f32[8,128]{1,0:T(8,128)S(1)}, u32[]{:S(2)}, u32[]{:S(2)}) collective-permute-start(f32[8,128]{1,0:T(8,128)S(1)} %add.19), channel_id=1, source_target_pairs={{0,4},{2,22},{4,8},{6,26},{8,12},{10,30},{12,16},{14,2},{16,20},{1... | collective-permute-start | bytes 12296 | tf_op jit(solution)/shard_map/ppermute | solution.py:331
  56.4 31.4 %collective-permute-start.3 = (f32[8,128]{1,0:T(8,128)S(1)}, f32[8,128]{1,0:T(8,128)S(1)}, u32[]{:S(2)}, u32[]{:S(2)}) collective-permute-start(f32[8,128]{1,0:T(8,128)S(1)} %add.19), channel_id=1, source_target_pairs={{0,0},{2,18},{4,4},{6,22},{8,8},{10,26},{12,12},{14,30},{16,16},{1... | collective-permute-start | bytes 12296 | tf_op jit(solution)/shard_map/ppermute | solution.py:331
  87.7 1.2 %collective-permute-start.7 = (f32[8,128]{1,0:T(8,128)S(1)}, f32[8,128]{1,0:T(8,128)S(1)}, u32[]{:S(2)}, u32[]{:S(2)}) collective-permute-start(f32[8,128]{1,0:T(8,128)S(1)} %add_add_fusion), channel_id=1, source_target_pairs={{0,2},{2,0},{4,6},{6,4},{8,10},{10,8},{12,14},{14,12},{16,18},{18,... | collective-permute-start | bytes 12296 | tf_op jit(solution)/shard_map/ppermute | solution.py:331

commit v5 on v4

--- a/solution.py
+++ b/solution.py
@@ -49,44 +49,56 @@
 UNROLL = (1, 2)
 
 
-def f_kernel(nt, at_row, more, delays, valid, *refs):
-    stream, one, tcos, tsin, two = refs[:5]
-    xs, obuf, mbuf, out_sem = refs[-4:]
+def f_kernel(nt, skip, at_row, more, *refs):
+    sources, refs = refs[:7], refs[7:]
+    trail = refs[0] if more else None
+    msgs = refs[2 if more else 0]
+    delays, valid, one, tcos, tsin, two, xin, xs, obuf, mbuf, small_sem, in_sem, out_sem = refs[
+        -13:
+    ]
+    stream = sources[0]
+    small = [
+        pltpu.make_async_copy(source, target, small_sem.at[i])
+        for i, (source, target) in enumerate(
+            zip(sources[1:], (delays, valid, one, tcos, tsin, two))
+        )
+    ]
     stations = stream.shape[0]
     rows = nt * FA
     chunk = FA * LANES
     pitch = xs.shape[0] // stations
-
-    def spread(source, to):
+    copies = [
+        pltpu.make_async_copy(
+            stream.at[:, pl.ds(skip + i * chunk, chunk)],
+            xin.at[:, pl.ds(i * chunk, chunk)],
+            in_sem.at[i],
+        )
+        for i in range(xin.shape[1] // chunk)
+    ]
+    for copy in copies + small:
+        copy.start()
+
+    def spread(source, base, to):
         def one_row(j, _):
-            at = pl.multiple_of(j * LANES, LANES)
+            at = pl.multiple_of((base + j) * LANES, LANES)
             xs[pl.ds(to + j, stations, stride=pitch), :] = source[:, pl.ds(at, LANES)].astype(
                 f32
             )
             return 0
 
-        count = source.shape[1] // LANES
-        lax.fori_loop(0, count, one_row, 0, unroll=16)
-        return to + count
-
-    filled = 0
+        lax.fori_loop(0, FA, one_row, 0, unroll=16)
+
+    filled = len(copies) * FA
     if more:
-        trail, msgs = refs[5], refs[7]
-        for source in (stream, trail):
-            filled = spread(source, filled)
-    else:
-        msgs, tail, xin, in_sem = refs[5:9]
-        targets = [xin.at[:, pl.ds(i * chunk, chunk)] for i in range(nt)] + [tail]
-        copies = [
-            pltpu.make_async_copy(stream.at[:, pl.ds(i * chunk, chunk)], target, in_sem.at[i])
-            for i, target in enumerate(targets)
-        ]
-        for copy in copies:
-            copy.start()
-        for copy, target in zip(copies, targets):
-            copy.wait()
-            filled = spread(target, filled)
+        spread(trail, 0, filled)
+    for i, copy in enumerate(copies):
+        copy.wait()
+        spread(xin, i * FA, i * FA)
+    if more:
+        filled += FA
     xs[pl.ds(filled, stations, stride=pitch), :] = jnp.zeros((stations, LANES), f32)
+    for copy in small:
+        copy.wait()
     src = lax.broadcasted_iota(jnp.int32, (2 * LANES, LANES), 0)
     dst = lax.broadcasted_iota(jnp.int32, (2 * LANES, LANES), 1)
     low = lax.broadcasted_iota(jnp.int32, (NQ, LANES), 1) < LO
@@ -168,54 +180,46 @@
 
 def channelized(stream, delays, valid, tables, so_far=()):
     stations = stream.shape[0]
-    smem = pl.BlockSpec(memory_space=pltpu.SMEM)
+    hbm = pl.BlockSpec(memory_space=pl.ANY)
     vmem = pl.BlockSpec(memory_space=pltpu.VMEM)
-    hbm = pl.BlockSpec(memory_space=pltpu.HBM)
     chunk = FA * LANES
     here = stream.shape[1] // chunk
+    specs = [pl.BlockSpec(memory_space=pltpu.HBM)] * 7
     if so_far:
         msgs, trailing = so_far
-        nt, at_row = 1, msgs.shape[1] - stations
-        rows = (stream.shape[1] + trailing.shape[1]) // LANES
-        stream = on_chip(stream)
-        tables = [on_chip(jnp.asarray(table)) for table in tables]
-        extra = (on_chip(trailing), off_chip(msgs))
-        specs = [smem, smem] + [vmem] * 6 + [hbm]
-        outs, out_specs = pltpu.HBM(msgs.shape, bf16), hbm
+        nt, skip, at_row = 1, (here - 1) * chunk, (here - 1) * stations
+        extra = (on_chip(trailing), msgs)
+        specs += [vmem, hbm]
         aliases = {8: 0}
-        buffers = []
+        held = 1
     else:
-        nt, at_row, extra = here - 1, 0, ()
-        stream = off_chip(stream)
-        rows = here * FA
-        specs = [smem, smem, hbm] + [vmem] * 4
-        outs = (
-            pltpu.HBM((NQ * NHI, here * stations, LANES), bf16),
-            pltpu.VMEM((stations, chunk), bf16),
-        )
-        out_specs = (hbm, vmem)
+        nt, skip, at_row, extra = here - 1, 0, 0, ()
         aliases = {}
-        buffers = [
-            pltpu.VMEM((stations, nt * chunk), bf16),
-            pltpu.SemaphoreType.DMA((here,)),
+        held = here
+    pitch = ((held + len(aliases)) * FA // 16 + 1) * 16 + 8
+    return pl.pallas_call(
+        lambda *refs: f_kernel(nt, skip, at_row, bool(so_far), *refs),
+        out_shape=jax.ShapeDtypeStruct((NQ * NHI, here * stations, LANES), bf16),
+        in_specs=specs,
+        out_specs=hbm,
+        scratch_shapes=[
+            pltpu.SMEM(delays.shape, delays.dtype),
+            pltpu.SMEM(valid.shape, valid.dtype),
         ]
-    pitch = (rows // 16 + 1) * 16 + 8
-    return pl.pallas_call(
-        lambda *refs: f_kernel(nt, at_row, bool(so_far), *refs),
-        out_shape=outs,
-        in_specs=specs,
-        out_specs=out_specs,
-        scratch_shapes=buffers
+        + [pltpu.VMEM(table.shape, table.dtype) for table in tables]
         + [
+            pltpu.VMEM((stations, held * chunk), bf16),
             pltpu.VMEM((stations * pitch, LANES), f32),
             pltpu.VMEM((NHI * nt * stations * OPITCH, LANES), f32),
             pltpu.VMEM((NQ * NHI, nt * stations, LANES), bf16),
+            pltpu.SemaphoreType.DMA((2 + len(tables),)),
+            pltpu.SemaphoreType.DMA((held,)),
             pltpu.SemaphoreType.DMA((PIECES,)),
         ],
         input_output_aliases=aliases,
         compiler_params=pltpu.CompilerParams(vmem_limit_bytes=28 << 20),
         name="channelize",
-    )(delays, valid, stream, *tables, *extra)
+    )(*[off_chip(jnp.asarray(value)) for value in (stream, delays, valid, *tables)], *extra)
 
 
 def tone_kernel(tones, msgs, picks):
@@ -256,7 +260,7 @@
 PITCH = 136
 
 
-def x_kernel(norm_scale, per_source, recv, vis, rs, ts, gs):
+def x_kernel(norm_scale, per_source, recv, vis, rs, ts, gs, block, out_sem):
     sources, rows, _ = recv.shape
     local = per_source
     groups = S // local
@@ -279,6 +283,8 @@
     lax.fori_loop(0, S, turn, 0, unroll=True)
 
     lane = lax.broadcasted_iota(jnp.int32, (8, LANES), 1)
+
+    sent = []
 
     def eight(o, _):
         base = o * 8
@@ -294,14 +300,23 @@
                 left, right, (((1,), (1,)), ((), ())), preferred_element_type=f32
             )
             gs[pl.ds(c * PITCH, 2 * S), :] = gram * norm_scale
-        top = pl.multiple_of(base, 8)
+        top = base
         for j in range(S):
             even = gs[pl.ds(2 * j, 8, stride=PITCH), :]
             odd = gs[pl.ds(2 * j + 1, 8, stride=PITCH), :]
-            vis[pl.ds(top, 8), pl.ds(j * LANES, LANES)] = jnp.where(lane < S, even, odd)
+            block[pl.ds(top, 8), pl.ds(j * LANES, LANES)] = jnp.where(lane < S, even, odd)
         return 0
 
-    lax.fori_loop(0, LO // 8, eight, 0, unroll=True)
+    for o in range(LO // 8):
+        eight(o, 0)
+        sent.append(
+            pltpu.make_async_copy(
+                block.at[pl.ds(o * 8, 8), :], vis.at[pl.ds(o * 8, 8), :], out_sem.at[o]
+            )
+        )
+        sent[o].start()
+    for copy in sent:
+        copy.wait()
 
 
 def correlated(recv, per_source, norm_scale):
@@ -310,11 +325,13 @@
         lambda *refs: x_kernel(norm_scale, per_source, *refs),
         out_shape=jax.ShapeDtypeStruct((LO, 2 * S * S), f32),
         in_specs=[vmem],
-        out_specs=vmem,
+        out_specs=pl.BlockSpec(memory_space=pl.ANY),
         scratch_shapes=[
             pltpu.VMEM((recv.shape[0] * recv.shape[1], LANES), f32),
             pltpu.VMEM((S * PITCH, LANES), f32),
             pltpu.VMEM((8 * PITCH, LANES), f32),
+            pltpu.VMEM((LO, 2 * S * S), f32),
+            pltpu.SemaphoreType.DMA((LO // 8,)),
         ],
         compiler_params=pltpu.CompilerParams(vmem_limit_bytes=24 << 20),
         name="correlate",
@@ -349,9 +366,8 @@
     whole = ("stn", "tm", "cores")
     here = stretch // (FA * FB)
     trailing = passed_along(samples[:, :MAXD], ("tm", "cores"), -1)
-    own = (delays, valid, make_tables())
-    msgs, tail = channelized(samples, *own)
-    msgs = channelized(tail, *own, (msgs, trailing))
+    own = (samples, delays, valid, make_tables())
+    msgs = channelized(*own, (channelized(*own), trailing))
     spectra_all = here * lax.axis_size("tm") * lax.axis_size("cores")
     norm_scale = 1.0 / math.sqrt(spectra_all)
     recv = lax.all_to_all(msgs, whole, split_axis=0, concat_axis=0, tiled=True)

time: 96.4 us -> 94.2 us (0.977)
  local copies, waits for them, and re-layouts: 6.04 us -> 1.08 us
  waiting for transfers between devices: 29 us -> 32.5 us
  Pallas kernels: 25.2 us -> 24.2 us
    unnamed x18 -> x2, local copies, waits for them, and re-layouts: 4.92 us -> 0.01 us
    ppermute x1, waiting for transfers between devices: 0.01 us -> 3.76 us  [passed_along(): return lax.ppermute(block, axis, route)]
    pallas_call x1, Pallas kernels: 6.52 us -> 4.36 us  [correlated(): pl.pallas_call(lambda *refs: x_kernel(norm_scale, per_source, *refs), out...]
    pallas_call x1, Pallas kernels: 6.98 us -> 7.98 us  [tone_sums(): pl.pallas_call(tone_kernel, out_shape=jax.ShapeDtypeStruct((tone_chan.sha...]
  transfers between devices with their start and end apart: 9 -> 9, of which waited for: 6 -> 7; matrix products, arithmetic and copies ran while one was open for 1% -> 1% of each run, Pallas kernels for 16% -> 17%
where the time goes in v5:
time: 94.2 us; the launch traced here: 93.9 us
  starting transfers between devices  34.8 us (37%)
  waiting for transfers between devices  32.5 us (35%)
  Pallas kernels  24.2 us (26%)
  local copies, waits for them, and re-layouts  1.08 us (1%)
    ppermute x7, waiting for transfers between devices, routed(): lax.ppermute(value, axis, [(i, dest(i)) for i in range(lax.axis_size(axis...  28.7 us
    all_to_all x1, starting transfers between devices, shards(): recv = lax.all_to_all(msgs, whole, split_axis=0, concat_axis=0, tiled=True)  15.3 us
    ppermute x7, starting transfers between devices, routed(): lax.ppermute(value, axis, [(i, dest(i)) for i in range(lax.axis_size(axis...  15 us
    pallas_call x2, Pallas kernels, channelized(): pl.pallas_call(lambda *refs: f_kernel(nt, skip, at_row, bool(so_far), *re...  11.8 us
    pallas_call x1, Pallas kernels, tone_sums(): pl.pallas_call(tone_kernel, out_shape=jax.ShapeDtypeStruct((tone_chan.sha...  7.98 us
    ppermute x1, starting transfers between devices, passed_along(): return lax.ppermute(block, axis, route)  4.51 us
    pallas_call x1, Pallas kernels, correlated(): pl.pallas_call(lambda *refs: x_kernel(norm_scale, per_source, *refs), out...  4.36 us
    ppermute x1, waiting for transfers between devices, passed_along(): return lax.ppermute(block, axis, route)  3.76 us
  transfers between devices with their start and end apart: 9, of which 7 were waited for; matrix products, arithmetic and copies ran while one was open for 1% of the time, Pallas kernels for 17%

profile of v5, /device:TPU:1, one launch (start us, length us, event | category | flops | bytes accessed | tf_op | source)
XLA Modules:
  0.0 93.9 jit_solution(17416418480784074474)
XLA Ops:
  0.6 1.1 %slice.3 = bf16[8,32768]{1,0:T(8,128)(2,1)S(1)} slice(bf16[8,131072]{1,0:T(8,128)(2,1)} %refs_0_.3), slice={[0:8], [0:32768]} | slice | bytes 1048576 | tf_op jit(solution)/shard_map/slice | solution.py:368
  1.7 4.5 %collective-permute-start = (bf16[8,32768]{1,0:T(8,128)(2,1)S(1)}, bf16[8,32768]{1,0:T(8,128)(2,1)S(1)}, u32[]{:S(2)}, u32[]{:S(2)}) collective-permute-start(bf16[8,32768]{1,0:T(8,128)(2,1)S(1)} %slice.3), channel_id=1, source_target_pairs={{1,0},{2,1},{3,2},{4,3},{5,4},{6,5},{7,6},{8,7},{9,8},{10,9},{11,1... | collective-permute-start | bytes 1572872 | tf_op jit(solution)/shard_map/ppermute | solution.py:344
  6.2 8.0 %channelize.2.refs_8_ = bf16[256,32,128]{2,1,0:T(8,128)(2,1)} custom-call(bf16[8,131072]{1,0:T(8,128)(2,1)} %refs_0_.3, s32[8]{0:T(128)} %refs_1_.3, s32[8]{0:T(128)} %refs_2_.3, bf16[256,512]{1,0:T(8,128)(2,1)} %constant.10.clone.refs_3_, f32[128,256]{1,0:T(8,128)} %constant.11.clone.refs_4_, f32[128,256]{1,0:T(8,128)} %constant.12.clone.refs_5_, ...), custom_call_target="tpu_custom_call" | custom-call | tf_op jit(solution)/shard_map/channelize/pallas_call | solution.py:200
  14.2 3.8 %collective-permute-done.refs_7_ = bf16[8,32768]{1,0:T(8,128)(2,1)S(1)} collective-permute-done((bf16[8,32768]{1,0:T(8,128)(2,1)S(1)}, bf16[8,32768]{1,0:T(8,128)(2,1)S(1)}, u32[]{:S(2)}, u32[]{:S(2)}) %collective-permute-start) | collective-permute-done | bytes 524320 | tf_op jit(solution)/shard_map/ppermute | solution.py:344
  17.9 3.9 %channelize.3.msgs = bf16[256,32,128]{2,1,0:T(8,128)(2,1)} custom-call(bf16[8,131072]{1,0:T(8,128)(2,1)} %refs_0_.3, s32[8]{0:T(128)} %refs_1_.3, s32[8]{0:T(128)} %refs_2_.3, bf16[256,512]{1,0:T(8,128)(2,1)} %constant.10.clone.refs_3_, f32[128,256]{1,0:T(8,128)} %constant.11.clone.refs_4_, ...), custom_call_target="tpu_custom_call", output_to_operand_aliasing={{}: (8, {})} | custom-call | tf_op jit(solution)/shard_map/channelize/pallas_call | solution.py:200
  21.8 0.0 copy-start
  21.8 15.3 %all-to-all-start = ((bf16[256,32,128]{2,1,0:T(8,128)(2,1)}), bf16[256,32,128]{2,1,0:T(8,128)(2,1)S(1)}, u32[]{:S(2)}, u32[]{:S(2)}) async-start(bf16[256,32,128]{2,1,0:T(8,128)(2,1)} %channelize.3.msgs), calls=%async_computation | async-start | bytes 4194304 | tf_op jit(solution)/shard_map/all_to_all | solution.py:373
  37.1 8.0 %tones.2 = f32[8,128]{1,0:T(8,128)S(1)} custom-call(s32[8,64]{1,0:T(8,128)S(1)} %copy-done, bf16[256,32,128]{2,1,0:T(8,128)(2,1)} %channelize.3.msgs), custom_call_target="tpu_custom_call" | custom-call | tf_op jit(solution)/shard_map/tones/pallas_call | solution.py:247
  45.1 1.4 %collective-permute-start.1 = (f32[8,128]{1,0:T(8,128)S(1)}, f32[8,128]{1,0:T(8,128)S(1)}, u32[]{:S(2)}, u32[]{:S(2)}) collective-permute-start(f32[8,128]{1,0:T(8,128)S(1)} %tones.2), channel_id=1, source_target_pairs={{0,1},{1,0},{2,3},{3,2},{4,5},{5,4},{6,7},{7,6},{8,9},{9,8},{10,11... | collective-permute-start | bytes 12296 | tf_op jit(solution)/shard_map/ppermute | solution.py:348
  46.5 1.5 %collective-permute-done.1 = f32[8,128]{1,0:T(8,128)S(1)} collective-permute-done((f32[8,128]{1,0:T(8,128)S(1)}, f32[8,128]{1,0:T(8,128)S(1)}, u32[]{:S(2)}, u32[]{:S(2)}) %collective-permute-start.1) | collective-permute-done | bytes 4128 | tf_op jit(solution)/shard_map/ppermute | solution.py:348
  48.1 3.0 %collective-permute-start.2 = (f32[8,128]{1,0:T(8,128)S(1)}, f32[8,128]{1,0:T(8,128)S(1)}, u32[]{:S(2)}, u32[]{:S(2)}) collective-permute-start(f32[8,128]{1,0:T(8,128)S(1)} %add.18), channel_id=1, source_target_pairs={{0,2},{2,0},{4,6},{6,4},{8,10},{10,8},{12,14},{14,12},{16,18},{18,... | collective-permute-start | bytes 12296 | tf_op jit(solution)/shard_map/ppermute | solution.py:348
  51.0 0.8 collective-permute-done.2
  51.9 2.4 %collective-permute-start.6 = (f32[8,128]{1,0:T(8,128)S(1)}, f32[8,128]{1,0:T(8,128)S(1)}, u32[]{:S(2)}, u32[]{:S(2)}) collective-permute-start(f32[8,128]{1,0:T(8,128)S(1)} %add.19), channel_id=1, source_target_pairs={{0,12},{2,30},{4,16},{6,2},{8,20},{10,6},{12,24},{14,10},{16,28},{... | collective-permute-start | bytes 12296 | tf_op jit(solution)/shard_map/ppermute | solution.py:348
  54.3 1.6 %collective-permute-start.5 = (f32[8,128]{1,0:T(8,128)S(1)}, f32[8,128]{1,0:T(8,128)S(1)}, u32[]{:S(2)}, u32[]{:S(2)}) collective-permute-start(f32[8,128]{1,0:T(8,128)S(1)} %add.19), channel_id=1, source_target_pairs={{0,8},{2,26},{4,12},{6,30},{8,16},{10,2},{12,20},{14,6},{16,24},{1... | collective-permute-start | bytes 12296 | tf_op jit(solution)/shard_map/ppermute | solution.py:348
  55.9 0.6 collective-permute-start.4
  56.5 6.0 %collective-permute-start.3 = (f32[8,128]{1,0:T(8,128)S(1)}, f32[8,128]{1,0:T(8,128)S(1)}, u32[]{:S(2)}, u32[]{:S(2)}) collective-permute-start(f32[8,128]{1,0:T(8,128)S(1)} %add.19), channel_id=1, source_target_pairs={{0,0},{2,18},{4,4},{6,22},{8,8},{10,26},{12,12},{14,30},{16,16},{1... | collective-permute-start | bytes 12296 | tf_op jit(solution)/shard_map/ppermute | solution.py:348
  62.5 19.5 %collective-permute-done.6 = f32[8,128]{1,0:T(8,128)S(1)} collective-permute-done((f32[8,128]{1,0:T(8,128)S(1)}, f32[8,128]{1,0:T(8,128)S(1)}, u32[]{:S(2)}, u32[]{:S(2)}) %collective-permute-start.6) | collective-permute-done | bytes 4128 | tf_op jit(solution)/shard_map/ppermute | solution.py:348
  82.0 0.6 collective-permute-done.5
  82.6 0.0 collective-permute-done.4
  82.6 5.1 %collective-permute-done.3 = f32[8,128]{1,0:T(8,128)S(1)} collective-permute-done((f32[8,128]{1,0:T(8,128)S(1)}, f32[8,128]{1,0:T(8,128)S(1)}, u32[]{:S(2)}, u32[]{:S(2)}) %collective-permute-start.3) | collective-permute-done | bytes 4128 | tf_op jit(solution)/shard_map/ppermute | solution.py:348
  87.7 0.0 collective-permute-start.7
  87.8 1.2 %collective-permute-done.7 = f32[8,128]{1,0:T(8,128)S(1)} collective-permute-done((f32[8,128]{1,0:T(8,128)S(1)}, f32[8,128]{1,0:T(8,128)S(1)}, u32[]{:S(2)}, u32[]{:S(2)}) %collective-permute-start.7) | collective-permute-done | bytes 4128 | tf_op jit(solution)/shard_map/ppermute | solution.py:348
  88.9 0.6 add_multiply_fusion
  89.5 4.4 %correlate.1 = f32[64,8192]{1,0:T(8,128)} custom-call(bf16[256,32,128]{2,1,0:T(8,128)(2,1)S(1)} %all-to-all-done.refs_0_), custom_call_target="tpu_custom_call" | custom-call | tf_op jit(solution)/shard_map/correlate/pallas_call | solution.py:324
  (5 shorter events, 0.0 us)
Async XLA Ops:
  1.7 16.2 %collective-permute-start = (bf16[8,32768]{1,0:T(8,128)(2,1)S(1)}, bf16[8,32768]{1,0:T(8,128)(2,1)S(1)}, u32[]{:S(2)}, u32[]{:S(2)}) collective-permute-start(bf16[8,32768]{1,0:T(8,128)(2,1)S(1)} %slice.3), channel_id=1, source_target_pairs={{1,0},{2,1},{3,2},{4,3},{5,4},{6,5},{7,6},{8,7},{9,8},{10,9},{11,1... | collective-permute-start | bytes 1572872 | tf_op jit(solution)/shard_map/ppermute | solution.py:344
  21.8 15.3 %copy-start = (s32[8,64]{1,0:T(8,128)S(1)}, s32[8,64]{1,0:T(8,128)}, u32[]{:S(2)}) copy-start(s32[8,64]{1,0:T(8,128)} %tones.3) | copy-start | bytes 6148
  21.8 67.7 %all-to-all-start = ((bf16[256,32,128]{2,1,0:T(8,128)(2,1)}), bf16[256,32,128]{2,1,0:T(8,128)(2,1)S(1)}, u32[]{:S(2)}, u32[]{:S(2)}) async-start(bf16[256,32,128]{2,1,0:T(8,128)(2,1)} %channelize.3.msgs), calls=%async_computation | async-start | bytes 4194304 | tf_op jit(solution)/shard_map/all_to_all | solution.py:373
  45.1 3.0 %collective-permute-start.1 = (f32[8,128]{1,0:T(8,128)S(1)}, f32[8,128]{1,0:T(8,128)S(1)}, u32[]{:S(2)}, u32[]{:S(2)}) collective-permute-start(f32[8,128]{1,0:T(8,128)S(1)} %tones.2), channel_id=1, source_target_pairs={{0,1},{1,0},{2,3},{3,2},{4,5},{5,4},{6,7},{7,6},{8,9},{9,8},{10,11... | collective-permute-start | bytes 12296 | tf_op jit(solution)/shard_map/ppermute | solution.py:348
  48.1 3.8 %collective-permute-start.2 = (f32[8,128]{1,0:T(8,128)S(1)}, f32[8,128]{1,0:T(8,128)S(1)}, u32[]{:S(2)}, u32[]{:S(2)}) collective-permute-start(f32[8,128]{1,0:T(8,128)S(1)} %add.18), channel_id=1, source_target_pairs={{0,2},{2,0},{4,6},{6,4},{8,10},{10,8},{12,14},{14,12},{16,18},{18,... | collective-permute-start | bytes 12296 | tf_op jit(solution)/shard_map/ppermute | solution.py:348
  51.9 30.1 %collective-permute-start.6 = (f32[8,128]{1,0:T(8,128)S(1)}, f32[8,128]{1,0:T(8,128)S(1)}, u32[]{:S(2)}, u32[]{:S(2)}) collective-permute-start(f32[8,128]{1,0:T(8,128)S(1)} %add.19), channel_id=1, source_target_pairs={{0,12},{2,30},{4,16},{6,2},{8,20},{10,6},{12,24},{14,10},{16,28},{... | collective-permute-start | bytes 12296 | tf_op jit(solution)/shard_map/ppermute | solution.py:348
  54.3 28.3 %collective-permute-start.5 = (f32[8,128]{1,0:T(8,128)S(1)}, f32[8,128]{1,0:T(8,128)S(1)}, u32[]{:S(2)}, u32[]{:S(2)}) collective-permute-start(f32[8,128]{1,0:T(8,128)S(1)} %add.19), channel_id=1, source_target_pairs={{0,8},{2,26},{4,12},{6,30},{8,16},{10,2},{12,20},{14,6},{16,24},{1... | collective-permute-start | bytes 12296 | tf_op jit(solution)/shard_map/ppermute | solution.py:348
  55.9 26.7 %collective-permute-start.4 = (f32[8,128]{1,0:T(8,128)S(1)}, f32[8,128]{1,0:T(8,128)S(1)}, u32[]{:S(2)}, u32[]{:S(2)}) collective-permute-start(f32[8,128]{1,0:T(8,128)S(1)} %add.19), channel_id=1, source_target_pairs={{0,4},{2,22},{4,8},{6,26},{8,12},{10,30},{12,16},{14,2},{16,20},{1... | collective-permute-start | bytes 12296 | tf_op jit(solution)/shard_map/ppermute | solution.py:348
  56.5 31.3 %collective-permute-start.3 = (f32[8,128]{1,0:T(8,128)S(1)}, f32[8,128]{1,0:T(8,128)S(1)}, u32[]{:S(2)}, u32[]{:S(2)}) collective-permute-start(f32[8,128]{1,0:T(8,128)S(1)} %add.19), channel_id=1, source_target_pairs={{0,0},{2,18},{4,4},{6,22},{8,8},{10,26},{12,12},{14,30},{16,16},{1... | collective-permute-start | bytes 12296 | tf_op jit(solution)/shard_map/ppermute | solution.py:348
  87.7 1.2 %collective-permute-start.7 = (f32[8,128]{1,0:T(8,128)S(1)}, f32[8,128]{1,0:T(8,128)S(1)}, u32[]{:S(2)}, u32[]{:S(2)}) collective-permute-start(f32[8,128]{1,0:T(8,128)S(1)} %add_add_fusion), channel_id=1, source_target_pairs={{0,2},{2,0},{4,6},{6,4},{8,10},{10,8},{12,14},{14,12},{16,18},{18,... | collective-permute-start | bytes 12296 | tf_op jit(solution)/shard_map/ppermute | solution.py:348

commit v6 on v5

--- a/solution.py
+++ b/solution.py
@@ -50,18 +50,20 @@
 
 
 def f_kernel(nt, skip, at_row, more, *refs):
-    sources, refs = refs[:7], refs[7:]
+    stream, refs, given = refs[0], refs[7:], refs[1:7]
     trail = refs[0] if more else None
     msgs = refs[2 if more else 0]
-    delays, valid, one, tcos, tsin, two, xin, xs, obuf, mbuf, small_sem, in_sem, out_sem = refs[
-        -13:
-    ]
-    stream = sources[0]
+    xin, xs, obuf, mbuf, in_sem, out_sem, small_sem = refs[-13:-6]
+    held = refs[-6:]
+    if more:
+        given, held, tables = given[:2], held[:2], given[2:]
+    else:
+        tables = held[2:]
+    delays, valid = held[:2]
+    one, tcos, tsin, two = tables
     small = [
         pltpu.make_async_copy(source, target, small_sem.at[i])
-        for i, (source, target) in enumerate(
-            zip(sources[1:], (delays, valid, one, tcos, tsin, two))
-        )
+        for i, (source, target) in enumerate(zip(given, held))
     ]
     stations = stream.shape[0]
     rows = nt * FA
@@ -184,18 +186,22 @@
     vmem = pl.BlockSpec(memory_space=pltpu.VMEM)
     chunk = FA * LANES
     here = stream.shape[1] // chunk
-    specs = [pl.BlockSpec(memory_space=pltpu.HBM)] * 7
+    far = pl.BlockSpec(memory_space=pltpu.HBM)
+    tables = [jnp.asarray(table) for table in tables]
     if so_far:
         msgs, trailing = so_far
         nt, skip, at_row = 1, (here - 1) * chunk, (here - 1) * stations
         extra = (on_chip(trailing), msgs)
-        specs += [vmem, hbm]
+        specs = [far] * 3 + [vmem] * 5 + [hbm]
+        tables = [on_chip(table) for table in tables]
         aliases = {8: 0}
         held = 1
     else:
         nt, skip, at_row, extra = here - 1, 0, 0, ()
         aliases = {}
         held = here
+        specs = [far] * 7
+        tables = [off_chip(table) for table in tables]
     pitch = ((held + len(aliases)) * FA // 16 + 1) * 16 + 8
     return pl.pallas_call(
         lambda *refs: f_kernel(nt, skip, at_row, bool(so_far), *refs),
@@ -203,44 +209,51 @@
         in_specs=specs,
         out_specs=hbm,
         scratch_shapes=[
-            pltpu.SMEM(delays.shape, delays.dtype),
-            pltpu.SMEM(valid.shape, valid.dtype),
-        ]
-        + [pltpu.VMEM(table.shape, table.dtype) for table in tables]
-        + [
             pltpu.VMEM((stations, held * chunk), bf16),
             pltpu.VMEM((stations * pitch, LANES), f32),
             pltpu.VMEM((NHI * nt * stations * OPITCH, LANES), f32),
             pltpu.VMEM((NQ * NHI, nt * stations, LANES), bf16),
-            pltpu.SemaphoreType.DMA((2 + len(tables),)),
             pltpu.SemaphoreType.DMA((held,)),
             pltpu.SemaphoreType.DMA((PIECES,)),
-        ],
+            pltpu.SemaphoreType.DMA((2 + len(tables),)),
+            pltpu.SMEM(delays.shape, delays.dtype),
+            pltpu.SMEM(valid.shape, valid.dtype),
+        ]
+        + [pltpu.VMEM(table.shape, table.dtype) for table in tables],
         input_output_aliases=aliases,
         compiler_params=pltpu.CompilerParams(vmem_limit_bytes=28 << 20),
         name="channelize",
-    )(*[off_chip(jnp.asarray(value)) for value in (stream, delays, valid, *tables)], *extra)
-
-
-def tone_kernel(tones, msgs, picks):
+    )(*[off_chip(value) for value in (stream, delays, valid)], *tables, *extra)
+
+
+def tone_kernel(tones, msgs, picks, sums):
     stations, count = tones.shape
+    places, rows, _ = msgs.shape
+
+    def add_times(p, _):
+        tile = msgs[p].astype(f32)
+        total = tile[:stations]
+        for t in range(1, rows // stations):
+            total = total + tile[t * stations : (t + 1) * stations]
+        sums[pl.ds(pl.multiple_of(p * stations, stations), stations), :] = total
+        return 0
+
+    lax.fori_loop(0, places, add_times, 0, unroll=8)
     sub = lax.broadcasted_iota(jnp.int32, (stations, LANES), 0)
     slot = lax.broadcasted_iota(jnp.int32, (stations, LANES), 1) % NTONE
 
     def one_tone(k, acc):
+        here = jnp.where(slot == k, sub, -1)
         for s in range(stations):
             chan = tones[s, k]
-            place = chan // LO
-            within = chan - place * LO
-            tile = msgs[place].astype(f32)
-            total = tile[:stations]
-            for t in range(1, tile.shape[0] // stations):
-                total = total + tile[t * stations : (t + 1) * stations]
-            turned = pltpu.roll(total, (k - within + LANES) % LANES, 1)
-            acc = jnp.where((sub == s) & (slot == k), turned, acc)
+            place = lax.shift_right_logical(chan, LO.bit_length() - 1)
+            within = lax.bitwise_and(chan, LO - 1)
+            total = sums[pl.ds(pl.multiple_of(place * stations, stations), stations), :]
+            turned = pltpu.roll(total, lax.bitwise_and(k - within, LANES - 1), 1)
+            acc = jnp.where(here == s, turned, acc)
         return acc
 
-    picks[...] = lax.fori_loop(0, count, one_tone, jnp.zeros((stations, LANES), f32), unroll=2)
+    picks[...] = lax.fori_loop(0, count, one_tone, jnp.zeros((stations, LANES), f32), unroll=4)
 
 
 def tone_sums(msgs, tone_chan):
@@ -252,6 +265,7 @@
             pl.BlockSpec(memory_space=pltpu.VMEM),
         ],
         out_specs=pl.BlockSpec(memory_space=pltpu.VMEM),
+        scratch_shapes=[pltpu.VMEM((msgs.shape[0] * tone_chan.shape[0], LANES), f32)],
         compiler_params=pltpu.CompilerParams(vmem_limit_bytes=8 << 20),
         name="tones",
     )(tone_chan, msgs)

time: 94.2 us -> 94.2 us (level)
  Pallas kernels: 24.2 us -> 20.3 us
  waiting for transfers between devices: 32.5 us -> 36 us
    pallas_call x1, Pallas kernels: 7.98 us -> 4.37 us  [tone_sums(): pl.pallas_call(tone_kernel, out_shape=jax.ShapeDtypeStruct((tone_chan.sha...]
    ppermute x7, waiting for transfers between devices: 28.7 us -> 32.2 us  [routed(): lax.ppermute(value, axis, [(i, dest(i)) for i in range(lax.axis_size(axis...]
  transfers between devices with their start and end apart: 9 -> 9, of which waited for: 7 -> 7; matrix products, arithmetic and copies ran while one was open for 1% -> 1% of each run, Pallas kernels for 17% -> 13%
where the time goes in v6:
time: 94.2 us; the launch traced here: 93.9 us
  waiting for transfers between devices  36 us (38%)
  starting transfers between devices  35.1 us (37%)
  Pallas kernels  20.3 us (22%)
  local copies, waits for them, and re-layouts  1.11 us (1%)
    ppermute x7, waiting for transfers between devices, routed(): lax.ppermute(value, axis, [(i, dest(i)) for i in range(lax.axis_size(axis...  32.2 us
    all_to_all x1, starting transfers between devices, shards(): recv = lax.all_to_all(msgs, whole, split_axis=0, concat_axis=0, tiled=True)  15.3 us
    ppermute x7, starting transfers between devices, routed(): lax.ppermute(value, axis, [(i, dest(i)) for i in range(lax.axis_size(axis...  15.2 us
    pallas_call x2, Pallas kernels, channelized(): pl.pallas_call(lambda *refs: f_kernel(nt, skip, at_row, bool(so_far), *re...  11.6 us
    ppermute x1, starting transfers between devices, passed_along(): return lax.ppermute(block, axis, route)  4.64 us
    pallas_call x1, Pallas kernels, tone_sums(): pl.pallas_call(tone_kernel, out_shape=jax.ShapeDtypeStruct((tone_chan.sha...  4.37 us
    pallas_call x1, Pallas kernels, correlated(): pl.pallas_call(lambda *refs: x_kernel(norm_scale, per_source, *refs), out...  4.37 us
    ppermute x1, waiting for transfers between devices, passed_along(): return lax.ppermute(block, axis, route)  3.78 us
  transfers between devices with their start and end apart: 9, of which 7 were waited for; matrix products, arithmetic and copies ran while one was open for 1% of the time, Pallas kernels for 13%

profile of v6, /device:TPU:1, one launch (start us, length us, event | category | flops | bytes accessed | tf_op | source)
XLA Modules:
  0.0 93.9 jit_solution(51142634443098903)
XLA Ops:
  0.6 1.1 %slice.3 = bf16[8,32768]{1,0:T(8,128)(2,1)S(1)} slice(bf16[8,131072]{1,0:T(8,128)(2,1)} %refs_0_.3), slice={[0:8], [0:32768]} | slice | bytes 1048576 | tf_op jit(solution)/shard_map/slice | solution.py:382
  1.7 0.0 copy-start.1
  1.7 0.0 copy-start.2
  1.7 0.0 copy-start.3
  1.8 4.6 %collective-permute-start = (bf16[8,32768]{1,0:T(8,128)(2,1)S(1)}, bf16[8,32768]{1,0:T(8,128)(2,1)S(1)}, u32[]{:S(2)}, u32[]{:S(2)}) collective-permute-start(bf16[8,32768]{1,0:T(8,128)(2,1)S(1)} %slice.3), channel_id=1, source_target_pairs={{1,0},{2,1},{3,2},{4,3},{5,4},{6,5},{7,6},{8,7},{9,8},{10,9},{11,1... | collective-permute-start | bytes 1572872 | tf_op jit(solution)/shard_map/ppermute | solution.py:358
  6.4 7.9 %channelize.2.refs_8_ = bf16[256,32,128]{2,1,0:T(8,128)(2,1)} custom-call(bf16[8,131072]{1,0:T(8,128)(2,1)} %refs_0_.3, s32[8]{0:T(128)} %refs_1_.3, s32[8]{0:T(128)} %refs_2_.3, bf16[256,512]{1,0:T(8,128)(2,1)} %constant.10.clone.refs_3_, f32[128,256]{1,0:T(8,128)} %constant.11.clone.refs_4_, f32[128,256]{1,0:T(8,128)} %constant.12.clone.refs_5_, ...), custom_call_target="tpu_custom_call" | custom-call | tf_op jit(solution)/shard_map/channelize/pallas_call | solution.py:206
  14.4 3.8 %collective-permute-done.refs_7_ = bf16[8,32768]{1,0:T(8,128)(2,1)S(1)} collective-permute-done((bf16[8,32768]{1,0:T(8,128)(2,1)S(1)}, bf16[8,32768]{1,0:T(8,128)(2,1)S(1)}, u32[]{:S(2)}, u32[]{:S(2)}) %collective-permute-start) | collective-permute-done | bytes 524320 | tf_op jit(solution)/shard_map/ppermute | solution.py:358
  18.1 3.7 %channelize.3.msgs = bf16[256,32,128]{2,1,0:T(8,128)(2,1)} custom-call(bf16[8,131072]{1,0:T(8,128)(2,1)} %refs_0_.3, s32[8]{0:T(128)} %refs_1_.3, s32[8]{0:T(128)} %refs_2_.3, bf16[256,512]{1,0:T(8,128)(2,1)S(1)} %copy-done, f32[128,256]{1,0:T(8,128)S(1)} %copy-done.2, f32[128,256]{1,0:T(8,128)S(1)} %copy-done.1, ...), custom_call_target="tpu_custom_call", output_to_operand_aliasing={{}: (8, {})} | custom-call | tf_op jit(solution)/shard_map/channelize/pallas_call | solution.py:206
  21.8 15.3 %all-to-all-start = ((bf16[256,32,128]{2,1,0:T(8,128)(2,1)}), bf16[256,32,128]{2,1,0:T(8,128)(2,1)S(1)}, u32[]{:S(2)}, u32[]{:S(2)}) async-start(bf16[256,32,128]{2,1,0:T(8,128)(2,1)} %channelize.3.msgs), calls=%async_computation | async-start | bytes 4194304 | tf_op jit(solution)/shard_map/all_to_all | solution.py:387
  37.1 4.4 %tones.2 = f32[8,128]{1,0:T(8,128)S(1)} custom-call(s32[8,64]{1,0:T(8,128)S(1)} %copy-done.4, bf16[256,32,128]{2,1,0:T(8,128)(2,1)} %channelize.3.msgs), custom_call_target="tpu_custom_call" | custom-call | tf_op jit(solution)/shard_map/tones/pallas_call | solution.py:260
  41.5 1.5 %collective-permute-start.1 = (f32[8,128]{1,0:T(8,128)S(1)}, f32[8,128]{1,0:T(8,128)S(1)}, u32[]{:S(2)}, u32[]{:S(2)}) collective-permute-start(f32[8,128]{1,0:T(8,128)S(1)} %tones.2), channel_id=1, source_target_pairs={{0,1},{1,0},{2,3},{3,2},{4,5},{5,4},{6,7},{7,6},{8,9},{9,8},{10,11... | collective-permute-start | bytes 12296 | tf_op jit(solution)/shard_map/ppermute | solution.py:362
  43.0 1.4 %collective-permute-done.1 = f32[8,128]{1,0:T(8,128)S(1)} collective-permute-done((f32[8,128]{1,0:T(8,128)S(1)}, f32[8,128]{1,0:T(8,128)S(1)}, u32[]{:S(2)}, u32[]{:S(2)}) %collective-permute-start.1) | collective-permute-done | bytes 4128 | tf_op jit(solution)/shard_map/ppermute | solution.py:362
  44.4 3.0 %collective-permute-start.2 = (f32[8,128]{1,0:T(8,128)S(1)}, f32[8,128]{1,0:T(8,128)S(1)}, u32[]{:S(2)}, u32[]{:S(2)}) collective-permute-start(f32[8,128]{1,0:T(8,128)S(1)} %add.18), channel_id=1, source_target_pairs={{0,2},{2,0},{4,6},{6,4},{8,10},{10,8},{12,14},{14,12},{16,18},{18,... | collective-permute-start | bytes 12296 | tf_op jit(solution)/shard_map/ppermute | solution.py:362
  47.3 0.8 collective-permute-done.2
  48.2 2.5 %collective-permute-start.6 = (f32[8,128]{1,0:T(8,128)S(1)}, f32[8,128]{1,0:T(8,128)S(1)}, u32[]{:S(2)}, u32[]{:S(2)}) collective-permute-start(f32[8,128]{1,0:T(8,128)S(1)} %add.19), channel_id=1, source_target_pairs={{0,12},{2,30},{4,16},{6,2},{8,20},{10,6},{12,24},{14,10},{16,28},{... | collective-permute-start | bytes 12296 | tf_op jit(solution)/shard_map/ppermute | solution.py:362
  50.7 1.6 %collective-permute-start.5 = (f32[8,128]{1,0:T(8,128)S(1)}, f32[8,128]{1,0:T(8,128)S(1)}, u32[]{:S(2)}, u32[]{:S(2)}) collective-permute-start(f32[8,128]{1,0:T(8,128)S(1)} %add.19), channel_id=1, source_target_pairs={{0,8},{2,26},{4,12},{6,30},{8,16},{10,2},{12,20},{14,6},{16,24},{1... | collective-permute-start | bytes 12296 | tf_op jit(solution)/shard_map/ppermute | solution.py:362
  52.3 0.7 collective-permute-start.4
  53.0 5.9 %collective-permute-start.3 = (f32[8,128]{1,0:T(8,128)S(1)}, f32[8,128]{1,0:T(8,128)S(1)}, u32[]{:S(2)}, u32[]{:S(2)}) collective-permute-start(f32[8,128]{1,0:T(8,128)S(1)} %add.19), channel_id=1, source_target_pairs={{0,0},{2,18},{4,4},{6,22},{8,8},{10,26},{12,12},{14,30},{16,16},{1... | collective-permute-start | bytes 12296 | tf_op jit(solution)/shard_map/ppermute | solution.py:362
  58.9 23.1 %collective-permute-done.6 = f32[8,128]{1,0:T(8,128)S(1)} collective-permute-done((f32[8,128]{1,0:T(8,128)S(1)}, f32[8,128]{1,0:T(8,128)S(1)}, u32[]{:S(2)}, u32[]{:S(2)}) %collective-permute-start.6) | collective-permute-done | bytes 4128 | tf_op jit(solution)/shard_map/ppermute | solution.py:362
  82.0 0.6 collective-permute-done.5
  82.6 5.1 %collective-permute-done.3 = f32[8,128]{1,0:T(8,128)S(1)} collective-permute-done((f32[8,128]{1,0:T(8,128)S(1)}, f32[8,128]{1,0:T(8,128)S(1)}, u32[]{:S(2)}, u32[]{:S(2)}) %collective-permute-start.3) | collective-permute-done | bytes 4128 | tf_op jit(solution)/shard_map/ppermute | solution.py:362
  87.8 1.2 %collective-permute-done.7 = f32[8,128]{1,0:T(8,128)S(1)} collective-permute-done((f32[8,128]{1,0:T(8,128)S(1)}, f32[8,128]{1,0:T(8,128)S(1)}, u32[]{:S(2)}, u32[]{:S(2)}) %collective-permute-start.7) | collective-permute-done | bytes 4128 | tf_op jit(solution)/shard_map/ppermute | solution.py:362
  88.9 0.6 add_multiply_fusion
  89.5 4.4 %correlate.1 = f32[64,8192]{1,0:T(8,128)} custom-call(bf16[256,32,128]{2,1,0:T(8,128)(2,1)S(1)} %all-to-all-done.refs_0_), custom_call_target="tpu_custom_call" | custom-call | tf_op jit(solution)/shard_map/correlate/pallas_call | solution.py:338
  (13 shorter events, 0.0 us)
Async XLA Ops:
  1.7 16.4 %copy-start = (bf16[256,512]{1,0:T(8,128)(2,1)S(1)}, bf16[256,512]{1,0:T(8,128)(2,1)}, u32[]{:S(2)}) copy-start(bf16[256,512]{1,0:T(8,128)(2,1)} %constant.10.clone.refs_3_) | copy-start | bytes 786436
  1.7 16.4 %copy-start.1 = (f32[128,256]{1,0:T(8,128)S(1)}, f32[128,256]{1,0:T(8,128)}, u32[]{:S(2)}) copy-start(f32[128,256]{1,0:T(8,128)} %constant.12.clone.refs_5_) | copy-start | bytes 393220
  1.7 16.4 %copy-start.2 = (f32[128,256]{1,0:T(8,128)S(1)}, f32[128,256]{1,0:T(8,128)}, u32[]{:S(2)}) copy-start(f32[128,256]{1,0:T(8,128)} %constant.11.clone.refs_4_) | copy-start | bytes 393220
  1.7 16.4 %copy-start.3 = (bf16[128,256]{1,0:T(8,128)(2,1)S(1)}, bf16[128,256]{1,0:T(8,128)(2,1)}, u32[]{:S(2)}) copy-start(bf16[128,256]{1,0:T(8,128)(2,1)} %constant.13.clone.refs_6_) | copy-start | bytes 196612
  1.8 16.4 %collective-permute-start = (bf16[8,32768]{1,0:T(8,128)(2,1)S(1)}, bf16[8,32768]{1,0:T(8,128)(2,1)S(1)}, u32[]{:S(2)}, u32[]{:S(2)}) collective-permute-start(bf16[8,32768]{1,0:T(8,128)(2,1)S(1)} %slice.3), channel_id=1, source_target_pairs={{1,0},{2,1},{3,2},{4,3},{5,4},{6,5},{7,6},{8,7},{9,8},{10,9},{11,1... | collective-permute-start | bytes 1572872 | tf_op jit(solution)/shard_map/ppermute | solution.py:358
  21.8 15.3 %copy-start.4 = (s32[8,64]{1,0:T(8,128)S(1)}, s32[8,64]{1,0:T(8,128)}, u32[]{:S(2)}) copy-start(s32[8,64]{1,0:T(8,128)} %tones.3) | copy-start | bytes 6148
  21.8 67.7 %all-to-all-start = ((bf16[256,32,128]{2,1,0:T(8,128)(2,1)}), bf16[256,32,128]{2,1,0:T(8,128)(2,1)S(1)}, u32[]{:S(2)}, u32[]{:S(2)}) async-start(bf16[256,32,128]{2,1,0:T(8,128)(2,1)} %channelize.3.msgs), calls=%async_computation | async-start | bytes 4194304 | tf_op jit(solution)/shard_map/all_to_all | solution.py:387
  41.5 2.9 %collective-permute-start.1 = (f32[8,128]{1,0:T(8,128)S(1)}, f32[8,128]{1,0:T(8,128)S(1)}, u32[]{:S(2)}, u32[]{:S(2)}) collective-permute-start(f32[8,128]{1,0:T(8,128)S(1)} %tones.2), channel_id=1, source_target_pairs={{0,1},{1,0},{2,3},{3,2},{4,5},{5,4},{6,7},{7,6},{8,9},{9,8},{10,11... | collective-permute-start | bytes 12296 | tf_op jit(solution)/shard_map/ppermute | solution.py:362
  44.4 3.8 %collective-permute-start.2 = (f32[8,128]{1,0:T(8,128)S(1)}, f32[8,128]{1,0:T(8,128)S(1)}, u32[]{:S(2)}, u32[]{:S(2)}) collective-permute-start(f32[8,128]{1,0:T(8,128)S(1)} %add.18), channel_id=1, source_target_pairs={{0,2},{2,0},{4,6},{6,4},{8,10},{10,8},{12,14},{14,12},{16,18},{18,... | collective-permute-start | bytes 12296 | tf_op jit(solution)/shard_map/ppermute | solution.py:362
  48.2 33.8 %collective-permute-start.6 = (f32[8,128]{1,0:T(8,128)S(1)}, f32[8,128]{1,0:T(8,128)S(1)}, u32[]{:S(2)}, u32[]{:S(2)}) collective-permute-start(f32[8,128]{1,0:T(8,128)S(1)} %add.19), channel_id=1, source_target_pairs={{0,12},{2,30},{4,16},{6,2},{8,20},{10,6},{12,24},{14,10},{16,28},{... | collective-permute-start | bytes 12296 | tf_op jit(solution)/shard_map/ppermute | solution.py:362
  50.7 31.9 %collective-permute-start.5 = (f32[8,128]{1,0:T(8,128)S(1)}, f32[8,128]{1,0:T(8,128)S(1)}, u32[]{:S(2)}, u32[]{:S(2)}) collective-permute-start(f32[8,128]{1,0:T(8,128)S(1)} %add.19), channel_id=1, source_target_pairs={{0,8},{2,26},{4,12},{6,30},{8,16},{10,2},{12,20},{14,6},{16,24},{1... | collective-permute-start | bytes 12296 | tf_op jit(solution)/shard_map/ppermute | solution.py:362
  52.3 30.3 %collective-permute-start.4 = (f32[8,128]{1,0:T(8,128)S(1)}, f32[8,128]{1,0:T(8,128)S(1)}, u32[]{:S(2)}, u32[]{:S(2)}) collective-permute-start(f32[8,128]{1,0:T(8,128)S(1)} %add.19), channel_id=1, source_target_pairs={{0,4},{2,22},{4,8},{6,26},{8,12},{10,30},{12,16},{14,2},{16,20},{1... | collective-permute-start | bytes 12296 | tf_op jit(solution)/shard_map/ppermute | solution.py:362
  53.0 34.7 %collective-permute-start.3 = (f32[8,128]{1,0:T(8,128)S(1)}, f32[8,128]{1,0:T(8,128)S(1)}, u32[]{:S(2)}, u32[]{:S(2)}) collective-permute-start(f32[8,128]{1,0:T(8,128)S(1)} %add.19), channel_id=1, source_target_pairs={{0,0},{2,18},{4,4},{6,22},{8,8},{10,26},{12,12},{14,30},{16,16},{1... | collective-permute-start | bytes 12296 | tf_op jit(solution)/shard_map/ppermute | solution.py:362
  87.7 1.2 %collective-permute-start.7 = (f32[8,128]{1,0:T(8,128)S(1)}, f32[8,128]{1,0:T(8,128)S(1)}, u32[]{:S(2)}, u32[]{:S(2)}) collective-permute-start(f32[8,128]{1,0:T(8,128)S(1)} %add_add_fusion), channel_id=1, source_target_pairs={{0,2},{2,0},{4,6},{6,4},{8,10},{10,8},{12,14},{14,12},{16,18},{18,... | collective-permute-start | bytes 12296 | tf_op jit(solution)/shard_map/ppermute | solution.py:362

commit v7 on v6

--- a/solution.py
+++ b/solution.py
@@ -45,109 +45,73 @@
 
 OPITCH = NQ + 8
 PIECES = 4
-GROUP = (8, 2)
-UNROLL = (1, 2)
-
-
-def f_kernel(nt, skip, at_row, more, *refs):
-    stream, refs, given = refs[0], refs[7:], refs[1:7]
-    trail = refs[0] if more else None
-    msgs = refs[2 if more else 0]
-    xin, xs, obuf, mbuf, in_sem, out_sem, small_sem = refs[-13:-6]
-    held = refs[-6:]
-    if more:
-        given, held, tables = given[:2], held[:2], given[2:]
-    else:
-        tables = held[2:]
-    delays, valid = held[:2]
+HALVES = 2
+ROWS = MAXD // LANES
+
+
+def on_chip(value):
+    return pltpu.with_memory_space_constraint(value, pltpu.VMEM)
+
+
+def off_chip(value):
+    return pltpu.with_memory_space_constraint(value, pltpu.HBM)
+
+
+def spread(source, base, xs, first, stride):
+    def one_row(j, _):
+        at = pl.multiple_of((base + j) * LANES, LANES)
+        xs[pl.ds(first + j, source.shape[0], stride=stride), :] = source[
+            :, pl.ds(at, LANES)
+        ].astype(f32)
+        return 0
+
+    lax.fori_loop(0, FA, one_row, 0, unroll=16)
+
+
+def transform(chosen, nt, stations, delays, valid, tables, xs, obuf):
     one, tcos, tsin, two = tables
-    small = [
-        pltpu.make_async_copy(source, target, small_sem.at[i])
-        for i, (source, target) in enumerate(zip(given, held))
-    ]
-    stations = stream.shape[0]
     rows = nt * FA
-    chunk = FA * LANES
     pitch = xs.shape[0] // stations
-    copies = [
-        pltpu.make_async_copy(
-            stream.at[:, pl.ds(skip + i * chunk, chunk)],
-            xin.at[:, pl.ds(i * chunk, chunk)],
-            in_sem.at[i],
-        )
-        for i in range(xin.shape[1] // chunk)
-    ]
-    for copy in copies + small:
-        copy.start()
-
-    def spread(source, base, to):
-        def one_row(j, _):
-            at = pl.multiple_of((base + j) * LANES, LANES)
-            xs[pl.ds(to + j, stations, stride=pitch), :] = source[:, pl.ds(at, LANES)].astype(
-                f32
-            )
-            return 0
-
-        lax.fori_loop(0, FA, one_row, 0, unroll=16)
-
-    filled = len(copies) * FA
-    if more:
-        spread(trail, 0, filled)
-    for i, copy in enumerate(copies):
-        copy.wait()
-        spread(xin, i * FA, i * FA)
-    if more:
-        filled += FA
-    xs[pl.ds(filled, stations, stride=pitch), :] = jnp.zeros((stations, LANES), f32)
-    for copy in small:
-        copy.wait()
     src = lax.broadcasted_iota(jnp.int32, (2 * LANES, LANES), 0)
     dst = lax.broadcasted_iota(jnp.int32, (2 * LANES, LANES), 1)
     low = lax.broadcasted_iota(jnp.int32, (NQ, LANES), 1) < LO
-
-    def group(g, _):
-        blocks = []
-        for k in range(GROUP[nt > 1]):
-            s = g * GROUP[nt > 1] + k
-            shift = delays[s]
-            lead = shift // LANES
-            within = shift - lead * LANES
-            first = xs[pl.ds(s * pitch + lead, rows), :]
-            second = xs[pl.ds(s * pitch + lead + 1, rows), :]
-            pair = jnp.concatenate([first.astype(bf16), second.astype(bf16)], axis=1)
-            move = (src == dst + within).astype(f32).astype(bf16)
-            moved = jnp.dot(pair, move, preferred_element_type=f32).astype(bf16)
-            blocks += [moved[t * FA : (t + 1) * FA] for t in range(nt)]
-        sections = lax.dot_general(
-            jnp.concatenate(blocks, axis=1),
-            one[...],
-            (((0,), (0,)), ((), ())),
-            preferred_element_type=f32,
-        )
-        for k in range(GROUP[nt > 1]):
-            s = g * GROUP[nt > 1] + k
-            last = (two[...].astype(f32) * valid[s].astype(f32)).astype(bf16)
-            for t in range(nt):
-                at = (k * nt + t) * FB
-                re, im = sections[at : at + FB, :FA], sections[at : at + FB, FA:]
-                cosine, sine = tcos[...], tsin[...]
-                tr = (re * cosine + im * sine).astype(bf16)
-                ti = (im * cosine - re * sine).astype(bf16)
-                spec = jnp.dot(
-                    last, jnp.concatenate([tr, ti], axis=0), preferred_element_type=f32
-                )
-                for j in range(FA // LANES):
-                    a = spec[:NQ, j * LANES : (j + 1) * LANES]
-                    b = spec[NQ:, j * LANES : (j + 1) * LANES]
-                    even = jnp.where(low, a, pltpu.roll(b, LO, 1))
-                    odd = jnp.where(low, pltpu.roll(a, LO, 1), b)
-                    for h, piece in ((2 * j, even), (2 * j + 1, odd)):
-                        to = pl.multiple_of(((h * nt + t) * stations + s) * OPITCH, 8)
-                        obuf[pl.ds(to, NQ), :] = piece
-        return 0
-
-    lax.fori_loop(0, stations // GROUP[nt > 1], group, 0, unroll=UNROLL[nt > 1])
-
+    blocks = []
+    for s in chosen:
+        shift = delays[s]
+        lead = shift // LANES
+        within = shift - lead * LANES
+        first = xs[pl.ds(s * pitch + lead, rows), :]
+        second = xs[pl.ds(s * pitch + lead + 1, rows), :]
+        pair = jnp.concatenate([first.astype(bf16), second.astype(bf16)], axis=1)
+        move = (src == dst + within).astype(f32).astype(bf16)
+        moved = jnp.dot(pair, move, preferred_element_type=f32).astype(bf16)
+        blocks += [moved[t * FA : (t + 1) * FA] for t in range(nt)]
+    sections = lax.dot_general(
+        jnp.concatenate(blocks, axis=1),
+        one[...],
+        (((0,), (0,)), ((), ())),
+        preferred_element_type=f32,
+    )
+    for k, s in enumerate(chosen):
+        last = (two[...].astype(f32) * valid[s].astype(f32)).astype(bf16)
+        for t in range(nt):
+            at = (k * nt + t) * FB
+            re, im = sections[at : at + FB, :FA], sections[at : at + FB, FA:]
+            cosine, sine = tcos[...], tsin[...]
+            tr = (re * cosine + im * sine).astype(bf16)
+            ti = (im * cosine - re * sine).astype(bf16)
+            spec = jnp.dot(last, jnp.concatenate([tr, ti], axis=0), preferred_element_type=f32)
+            for j in range(FA // LANES):
+                a = spec[:NQ, j * LANES : (j + 1) * LANES]
+                b = spec[NQ:, j * LANES : (j + 1) * LANES]
+                even = jnp.where(low, a, pltpu.roll(b, LO, 1))
+                odd = jnp.where(low, pltpu.roll(a, LO, 1), b)
+                for h, piece in ((2 * j, even), (2 * j + 1, odd)):
+                    to = ((h * nt + t) * stations + s) * OPITCH
+                    obuf[pl.ds(pl.multiple_of(to, 8), NQ), :] = piece
+
+
+def write_messages(nt, at_row, stations, obuf, mbuf, msgs, out_sem):
     per = NQ // PIECES
     sent = []
     for i in range(PIECES):
@@ -172,58 +136,159 @@
         copy.wait()
 
 
-def on_chip(value):
-    return pltpu.with_memory_space_constraint(value, pltpu.VMEM)
-
-
-def off_chip(value):
-    return pltpu.with_memory_space_constraint(value, pltpu.HBM)
-
-
-def channelized(stream, delays, valid, tables, so_far=()):
+def early_kernel(nt, *refs):
+    stream, given, msgs = refs[0], refs[1:7], refs[7]
+    xin, xs, obuf, mbuf, in_sem, out_sem, small_sem = refs[8:15]
+    held = refs[15:]
     stations = stream.shape[0]
+    chunk = FA * LANES
+    pitch = xs.shape[0] // stations
+    copies = [
+        pltpu.make_async_copy(
+            stream.at[:, pl.ds(i * chunk, chunk)],
+            xin.at[:, pl.ds(i * chunk, chunk)],
+            in_sem.at[i],
+        )
+        for i in range(nt + 1)
+    ]
+    small = [
+        pltpu.make_async_copy(source, target, small_sem.at[i])
+        for i, (source, target) in enumerate(zip(given, held))
+    ]
+    for copy in copies + small:
+        copy.start()
+    for i, copy in enumerate(copies):
+        copy.wait()
+        spread(xin, i * FA, xs, i * FA, pitch)
+    xs[pl.ds((nt + 1) * FA, stations, stride=pitch), :] = jnp.zeros((stations, LANES), f32)
+    for copy in small:
+        copy.wait()
+
+    def group(g, _):
+        transform(
+            [2 * g, 2 * g + 1], nt, stations, held[0], held[1], held[2:], xs, obuf
+        )
+        return 0
+
+    lax.fori_loop(0, stations // 2, group, 0, unroll=2)
+    write_messages(nt, 0, stations, obuf, mbuf, msgs, out_sem)
+
+
+def late_kernel(half, skip, at_row, *refs):
+    stream, given, tables, trail = refs[0], refs[1:3], refs[3:7], refs[7]
+    final = half == HALVES - 1
+    outs = refs[10:] if final else refs[8:]
+    if half and not final:
+        outs = refs[9:]
+    obuf, rest = outs[0], outs[1:]
+    if final:
+        msgs, mbuf, out_sem = rest[:3]
+        rest = rest[3:]
+    xin, xs, in_sem, small_sem = rest[:4]
+    held = rest[4:]
+    stations = stream.shape[0]
+    some = trail.shape[0]
+    pitch = xs.shape[0] // stations
+    copy = pltpu.make_async_copy(stream.at[:, pl.ds(skip, FA * LANES)], xin, in_sem)
+    small = [
+        pltpu.make_async_copy(source, target, small_sem.at[i])
+        for i, (source, target) in enumerate(zip(given, held))
+    ]
+    for begun in [copy] + small:
+        begun.start()
+    spread(trail, 0, xs, half * some * pitch + FA, pitch)
+    copy.wait()
+    spread(xin, 0, xs, 0, pitch)
+    xs[pl.ds(FA + ROWS, stations, stride=pitch), :] = jnp.zeros((stations, LANES), f32)
+    for copy in small:
+        copy.wait()
+    chosen = [half * some + k for k in range(some)]
+    transform(chosen, 1, stations, held[0], held[1], tables, xs, obuf)
+    if final:
+        write_messages(1, at_row, stations, obuf, mbuf, msgs, out_sem)
+
+
+def odd_pitch(rows):
+    return (rows // 16 + 1) * 16 + 8
+
+
+def scalars(delays, valid):
+    return [pltpu.SMEM(delays.shape, delays.dtype), pltpu.SMEM(valid.shape, valid.dtype)]
+
+
+def early_messages(stream, delays, valid, tables):
+    stations = stream.shape[0]
+    far = pl.BlockSpec(memory_space=pltpu.HBM)
+    here = stream.shape[1] // (FA * LANES)
+    nt = here - 1
+    return pl.pallas_call(
+        lambda *refs: early_kernel(nt, *refs),
+        out_shape=jax.ShapeDtypeStruct((NQ * NHI, here * stations, LANES), bf16),
+        in_specs=[far] * 7,
+        out_specs=pl.BlockSpec(memory_space=pl.ANY),
+        scratch_shapes=[
+            pltpu.VMEM(stream.shape, bf16),
+            pltpu.VMEM((stations * odd_pitch(here * FA), LANES), f32),
+            pltpu.VMEM((NHI * nt * stations * OPITCH, LANES), f32),
+            pltpu.VMEM((NQ * NHI, nt * stations, LANES), bf16),
+            pltpu.SemaphoreType.DMA((here,)),
+            pltpu.SemaphoreType.DMA((PIECES,)),
+            pltpu.SemaphoreType.DMA((2 + len(tables),)),
+        ]
+        + scalars(delays, valid)
+        + [pltpu.VMEM(table.shape, table.dtype) for table in tables],
+        compiler_params=pltpu.CompilerParams(vmem_limit_bytes=28 << 20),
+        name="channelize",
+    )(*[off_chip(value) for value in (stream, delays, valid, *tables)])
+
+
+def late_messages(half, stream, delays, valid, tables, trail, so_far):
+    stations = stream.shape[0]
+    far = pl.BlockSpec(memory_space=pltpu.HBM)
+    vmem = pl.BlockSpec(memory_space=pltpu.VMEM)
     hbm = pl.BlockSpec(memory_space=pl.ANY)
-    vmem = pl.BlockSpec(memory_space=pltpu.VMEM)
     chunk = FA * LANES
     here = stream.shape[1] // chunk
-    far = pl.BlockSpec(memory_space=pltpu.HBM)
-    tables = [jnp.asarray(table) for table in tables]
-    if so_far:
-        msgs, trailing = so_far
-        nt, skip, at_row = 1, (here - 1) * chunk, (here - 1) * stations
-        extra = (on_chip(trailing), msgs)
-        specs = [far] * 3 + [vmem] * 5 + [hbm]
-        tables = [on_chip(table) for table in tables]
-        aliases = {8: 0}
-        held = 1
-    else:
-        nt, skip, at_row, extra = here - 1, 0, 0, ()
-        aliases = {}
-        held = here
-        specs = [far] * 7
-        tables = [off_chip(table) for table in tables]
-    pitch = ((held + len(aliases)) * FA // 16 + 1) * 16 + 8
+    final = half == HALVES - 1
+    args = [off_chip(value) for value in (stream, delays, valid)]
+    args += [on_chip(value) for value in (*tables, trail)]
+    specs = [far] * 3 + [vmem] * 5
+    outs = [pltpu.VMEM((NHI * stations * OPITCH, LANES), f32)]
+    out_specs = [vmem]
+    scratch = []
+    aliases = {}
+    if half:
+        aliases[8] = 0
+        args.append(on_chip(so_far[0]))
+        specs.append(vmem)
+    if final:
+        msgs = so_far[1]
+        aliases[9] = 1
+        args.append(msgs)
+        specs.append(hbm)
+        outs.append(jax.ShapeDtypeStruct(msgs.shape, bf16))
+        out_specs.append(hbm)
+        scratch = [
+            pltpu.VMEM((NQ * NHI, stations, LANES), bf16),
+            pltpu.SemaphoreType.DMA((PIECES,)),
+        ]
     return pl.pallas_call(
-        lambda *refs: f_kernel(nt, skip, at_row, bool(so_far), *refs),
-        out_shape=jax.ShapeDtypeStruct((NQ * NHI, here * stations, LANES), bf16),
+        lambda *refs: late_kernel(half, (here - 1) * chunk, (here - 1) * stations, *refs),
+        out_shape=outs,
         in_specs=specs,
-        out_specs=hbm,
-        scratch_shapes=[
-            pltpu.VMEM((stations, held * chunk), bf16),
-            pltpu.VMEM((stations * pitch, LANES), f32),
-            pltpu.VMEM((NHI * nt * stations * OPITCH, LANES), f32),
-            pltpu.VMEM((NQ * NHI, nt * stations, LANES), bf16),
-            pltpu.SemaphoreType.DMA((held,)),
-            pltpu.SemaphoreType.DMA((PIECES,)),
-            pltpu.SemaphoreType.DMA((2 + len(tables),)),
-            pltpu.SMEM(delays.shape, delays.dtype),
-            pltpu.SMEM(valid.shape, valid.dtype),
+        out_specs=out_specs,
+        scratch_shapes=scratch
+        + [
+            pltpu.VMEM((stations, chunk), bf16),
+            pltpu.VMEM((stations * odd_pitch(FA + ROWS), LANES), f32),
+            pltpu.SemaphoreType.DMA(()),
+            pltpu.SemaphoreType.DMA((2,)),
         ]
-        + [pltpu.VMEM(table.shape, table.dtype) for table in tables],
+        + scalars(delays, valid),
         input_output_aliases=aliases,
-        compiler_params=pltpu.CompilerParams(vmem_limit_bytes=28 << 20),
-        name="channelize",
-    )(*[off_chip(value) for value in (stream, delays, valid)], *tables, *extra)
+        compiler_params=pltpu.CompilerParams(vmem_limit_bytes=20 << 20),
+        name="channelize_late",
+    )(*args)
 
 
 def tone_kernel(tones, msgs, picks, sums):
@@ -379,9 +444,16 @@
     stations, stretch = samples.shape
     whole = ("stn", "tm", "cores")
     here = stretch // (FA * FB)
-    trailing = passed_along(samples[:, :MAXD], ("tm", "cores"), -1)
-    own = (samples, delays, valid, make_tables())
-    msgs = channelized(*own, (channelized(*own), trailing))
+    some = stations // HALVES
+    trailing = [
+        passed_along(samples[i * some : (i + 1) * some, :MAXD], ("tm", "cores"), -1)
+        for i in range(HALVES)
+    ]
+    tables = [jnp.asarray(table) for table in make_tables()]
+    own = (samples, delays, valid, tables)
+    early = early_messages(*own)
+    (held,) = late_messages(0, *own, trailing[0], ())
+    _, msgs = late_messages(1, *own, trailing[1], (held, early))
     spectra_all = here * lax.axis_size("tm") * lax.axis_size("cores")
     norm_scale = 1.0 / math.sqrt(spectra_all)
     recv = lax.all_to_all(msgs, whole, split_axis=0, concat_axis=0, tiled=True)

time: 94.2 us -> 94.4 us (level)
  waiting for transfers between devices: 36 us -> 32.2 us
  Pallas kernels: 20.3 us -> 22.3 us
  starting transfers between devices: 35.1 us -> 36.6 us
    ppermute x1 -> x2, starting transfers between devices: 4.64 us -> 8.82 us  [passed_along(): return lax.ppermute(block, axis, route)]
    ppermute x1 -> x2, waiting for transfers between devices: 3.78 us -> 0.01 us  [passed_along(): return lax.ppermute(block, axis, route)]
    all_to_all x1, starting transfers between devices: 15.3 us -> 12.6 us  [shards(): recv = lax.all_to_all(msgs, whole, split_axis=0, concat_axis=0, tiled=True)]
    pallas_call x2 -> x3, Pallas kernels: 11.6 us -> 13.5 us  [the longest x1 7.93 us: early_messages(): pl.pallas_call(lambda *refs: early_kernel(nt, *refs), out_shape=jax.Shape...]
  transfers between devices with their start and end apart: 9 -> 10, of which waited for: 7 -> 6; matrix products, arithmetic and copies ran while one was open for 1% -> 1% of each run, Pallas kernels for 13% -> 16%
where the time goes in v7:
time: 94.4 us; the launch traced here: 94.1 us
  starting transfers between devices  36.6 us (39%)
  waiting for transfers between devices  32.2 us (34%)
  Pallas kernels  22.3 us (24%)
  local copies, waits for them, and re-layouts  1.44 us (2%)
  between operations  0.95 us (1%)
    ppermute x7, waiting for transfers between devices, routed(): lax.ppermute(value, axis, [(i, dest(i)) for i in range(lax.axis_size(axis...  32.2 us
    ppermute x7, starting transfers between devices, routed(): lax.ppermute(value, axis, [(i, dest(i)) for i in range(lax.axis_size(axis...  15.2 us
    all_to_all x1, starting transfers between devices, shards(): recv = lax.all_to_all(msgs, whole, split_axis=0, concat_axis=0, tiled=True)  12.6 us
    ppermute x2, starting transfers between devices, passed_along(): return lax.ppermute(block, axis, route)  8.82 us
    pallas_call x1, Pallas kernels, early_messages(): pl.pallas_call(lambda *refs: early_kernel(nt, *refs), out_shape=jax.Shape...  7.93 us
    pallas_call x2, Pallas kernels, late_messages(): pl.pallas_call(lambda *refs: late_kernel(half, (here - 1) * chunk, (here...  5.61 us
    pallas_call x1, Pallas kernels, correlated(): pl.pallas_call(lambda *refs: x_kernel(norm_scale, per_source, *refs), out...  4.38 us
    pallas_call x1, Pallas kernels, tone_sums(): pl.pallas_call(tone_kernel, out_shape=jax.ShapeDtypeStruct((tone_chan.sha...  4.37 us
  transfers between devices with their start and end apart: 10, of which 6 were waited for; matrix products, arithmetic and copies ran while one was open for 1% of the time, Pallas kernels for 16%

profile of v7, /device:TPU:1, one launch (start us, length us, event | category | flops | bytes accessed | tf_op | source)
XLA Modules:
  0.0 94.1 jit_solution(4379509648492201204)
XLA Ops:
  0.6 1.4 %fusion = (bf16[4,32768]{1,0:T(4,128)(2,1)S(1)}, bf16[4,32768]{1,0:T(4,128)(2,1)S(1)}) fusion(bf16[8,131072]{1,0:T(8,128)(2,1)} %refs_0_.5), kind=kLoop, calls=%fused_computation.2 | loop fusion | bytes 1048576 | tf_op jit(solution)/shard_map/slice | solution.py:449
  2.0 4.5 %collective-permute-start.1 = (bf16[4,32768]{1,0:T(4,128)(2,1)S(1)}, bf16[4,32768]{1,0:T(4,128)(2,1)S(1)}, u32[]{:S(2)}, u32[]{:S(2)}) collective-permute-start(bf16[4,32768]{1,0:T(4,128)(2,1)S(1)} %get-tuple-element.4), channel_id=1, source_target_pairs={{1,0},{2,1},{3,2},{4,3},{5,4},{6,5},{7,6},{8,7},{9,8},{10,9},{11,1... | collective-permute-start | bytes 786440 | tf_op jit(solution)/shard_map/ppermute | solution.py:423
  6.6 0.0 copy-start
  6.6 0.0 copy-start.2
  6.6 4.3 %collective-permute-start = (bf16[4,32768]{1,0:T(4,128)(2,1)S(1)}, bf16[4,32768]{1,0:T(4,128)(2,1)S(1)}, u32[]{:S(2)}, u32[]{:S(2)}) collective-permute-start(bf16[4,32768]{1,0:T(4,128)(2,1)S(1)} %get-tuple-element.5), channel_id=1, source_target_pairs={{1,0},{2,1},{3,2},{4,3},{5,4},{6,5},{7,6},{8,7},{9,8},{10,9},{11,1... | collective-permute-start | bytes 786440 | tf_op jit(solution)/shard_map/ppermute | solution.py:423
  10.9 7.9 %channelize.1.refs_9_ = bf16[256,32,128]{2,1,0:T(8,128)(2,1)} custom-call(bf16[8,131072]{1,0:T(8,128)(2,1)} %refs_0_.5, s32[8]{0:T(128)} %refs_1_.5, s32[8]{0:T(128)} %refs_2_.5, bf16[256,512]{1,0:T(8,128)(2,1)} %constant.10.clone.refs_3_, f32[128,256]{1,0:T(8,128)} %constant.11.clone.refs_4_, f32[128,256]{1,0:T(8,128)} %constant.12.clone.refs_5_, ...), custom_call_target="tpu_custom_call" | custom-call | tf_op jit(solution)/shard_map/channelize/pallas_call | solution.py:224
  18.9 2.3 %channelize_late.2.refs_8_ = f32[2304,128]{1,0:T(8,128)S(1)} custom-call(bf16[8,131072]{1,0:T(8,128)(2,1)} %refs_0_.5, s32[8]{0:T(128)} %refs_1_.5, s32[8]{0:T(128)} %refs_2_.5, bf16[256,512]{1,0:T(8,128)(2,1)S(1)} %copy-done, f32[128,256]{1,0:T(8,128)S(1)} %copy-done.2, f32[128,256]{1,0:T(8,128)S(1)} %copy-done.1, bf16[128,256]{1,0:T(8,128)(2,1)S(1)} %copy-done.3, ...), custom_call_target="tpu_custom_call" | custom-call | tf_op jit(solution)/shard_map/channelize_late/pallas_call | solution.py:275
  21.3 3.3 %channelize_late.3 = (f32[2304,128]{1,0:T(8,128)S(1)}, bf16[256,32,128]{2,1,0:T(8,128)(2,1)}) custom-call(bf16[8,131072]{1,0:T(8,128)(2,1)} %refs_0_.5, s32[8]{0:T(128)} %refs_1_.5, s32[8]{0:T(128)} %refs_2_.5, bf16[256,512]{1,0:T(8,128)(2,1)S(1)} %copy-done, f32[128,256]{1,0:T(8,128)S(1)} %copy-done.2, ...), custom_call_target="tpu_custom_call", output_to_operand_aliasing={{0}: (8, {}), {1}: (9, {})} | custom-call | tf_op jit(solution)/shard_map/channelize_late/pallas_call | solution.py:275
  24.6 12.6 %all-to-all-start = ((bf16[256,32,128]{2,1,0:T(8,128)(2,1)}), bf16[256,32,128]{2,1,0:T(8,128)(2,1)S(1)}, u32[]{:S(2)}, u32[]{:S(2)}) async-start(bf16[256,32,128]{2,1,0:T(8,128)(2,1)} %get-tuple-element.3.msgs), calls=%async_computation | async-start | bytes 4194304 | tf_op jit(solution)/shard_map/all_to_all | solution.py:459
  37.1 4.4 %tones.2 = f32[8,128]{1,0:T(8,128)S(1)} custom-call(s32[8,64]{1,0:T(8,128)S(1)} %copy-done.4, bf16[256,32,128]{2,1,0:T(8,128)(2,1)} %get-tuple-element.3.msgs), custom_call_target="tpu_custom_call" | custom-call | tf_op jit(solution)/shard_map/tones/pallas_call | solution.py:325
  41.5 1.5 %collective-permute-start.2 = (f32[8,128]{1,0:T(8,128)S(1)}, f32[8,128]{1,0:T(8,128)S(1)}, u32[]{:S(2)}, u32[]{:S(2)}) collective-permute-start(f32[8,128]{1,0:T(8,128)S(1)} %tones.2), channel_id=1, source_target_pairs={{0,1},{1,0},{2,3},{3,2},{4,5},{5,4},{6,7},{7,6},{8,9},{9,8},{10,11... | collective-permute-start | bytes 12296 | tf_op jit(solution)/shard_map/ppermute | solution.py:427
  43.0 1.4 %collective-permute-done.2 = f32[8,128]{1,0:T(8,128)S(1)} collective-permute-done((f32[8,128]{1,0:T(8,128)S(1)}, f32[8,128]{1,0:T(8,128)S(1)}, u32[]{:S(2)}, u32[]{:S(2)}) %collective-permute-start.2) | collective-permute-done | bytes 4128 | tf_op jit(solution)/shard_map/ppermute | solution.py:427
  44.4 3.0 %collective-permute-start.3 = (f32[8,128]{1,0:T(8,128)S(1)}, f32[8,128]{1,0:T(8,128)S(1)}, u32[]{:S(2)}, u32[]{:S(2)}) collective-permute-start(f32[8,128]{1,0:T(8,128)S(1)} %add.18), channel_id=1, source_target_pairs={{0,2},{2,0},{4,6},{6,4},{8,10},{10,8},{12,14},{14,12},{16,18},{18,... | collective-permute-start | bytes 12296 | tf_op jit(solution)/shard_map/ppermute | solution.py:427
  47.4 0.8 collective-permute-done.3
  48.2 2.5 %collective-permute-start.7 = (f32[8,128]{1,0:T(8,128)S(1)}, f32[8,128]{1,0:T(8,128)S(1)}, u32[]{:S(2)}, u32[]{:S(2)}) collective-permute-start(f32[8,128]{1,0:T(8,128)S(1)} %add.19), channel_id=1, source_target_pairs={{0,12},{2,30},{4,16},{6,2},{8,20},{10,6},{12,24},{14,10},{16,28},{... | collective-permute-start | bytes 12296 | tf_op jit(solution)/shard_map/ppermute | solution.py:427
  50.8 1.6 %collective-permute-start.6 = (f32[8,128]{1,0:T(8,128)S(1)}, f32[8,128]{1,0:T(8,128)S(1)}, u32[]{:S(2)}, u32[]{:S(2)}) collective-permute-start(f32[8,128]{1,0:T(8,128)S(1)} %add.19), channel_id=1, source_target_pairs={{0,8},{2,26},{4,12},{6,30},{8,16},{10,2},{12,20},{14,6},{16,24},{1... | collective-permute-start | bytes 12296 | tf_op jit(solution)/shard_map/ppermute | solution.py:427
  52.3 0.7 collective-permute-start.5
  53.0 5.9 %collective-permute-start.4 = (f32[8,128]{1,0:T(8,128)S(1)}, f32[8,128]{1,0:T(8,128)S(1)}, u32[]{:S(2)}, u32[]{:S(2)}) collective-permute-start(f32[8,128]{1,0:T(8,128)S(1)} %add.19), channel_id=1, source_target_pairs={{0,0},{2,18},{4,4},{6,22},{8,8},{10,26},{12,12},{14,30},{16,16},{1... | collective-permute-start | bytes 12296 | tf_op jit(solution)/shard_map/ppermute | solution.py:427
  58.9 23.1 %collective-permute-done.7 = f32[8,128]{1,0:T(8,128)S(1)} collective-permute-done((f32[8,128]{1,0:T(8,128)S(1)}, f32[8,128]{1,0:T(8,128)S(1)}, u32[]{:S(2)}, u32[]{:S(2)}) %collective-permute-start.7) | collective-permute-done | bytes 4128 | tf_op jit(solution)/shard_map/ppermute | solution.py:427
  82.0 0.6 collective-permute-done.6
  82.6 5.1 %collective-permute-done.4 = f32[8,128]{1,0:T(8,128)S(1)} collective-permute-done((f32[8,128]{1,0:T(8,128)S(1)}, f32[8,128]{1,0:T(8,128)S(1)}, u32[]{:S(2)}, u32[]{:S(2)}) %collective-permute-start.4) | collective-permute-done | bytes 4128 | tf_op jit(solution)/shard_map/ppermute | solution.py:427
  87.8 1.2 %collective-permute-done.8 = f32[8,128]{1,0:T(8,128)S(1)} collective-permute-done((f32[8,128]{1,0:T(8,128)S(1)}, f32[8,128]{1,0:T(8,128)S(1)}, u32[]{:S(2)}, u32[]{:S(2)}) %collective-permute-start.8) | collective-permute-done | bytes 4128 | tf_op jit(solution)/shard_map/ppermute | solution.py:427
  88.9 0.6 add_multiply_fusion
  89.5 4.4 %correlate.1 = f32[64,8192]{1,0:T(8,128)} custom-call(bf16[256,32,128]{2,1,0:T(8,128)(2,1)S(1)} %all-to-all-done.refs_0_), custom_call_target="tpu_custom_call" | custom-call | tf_op jit(solution)/shard_map/correlate/pallas_call | solution.py:403
  (16 shorter events, 0.0 us)
Async XLA Ops:
  2.0 16.8 %collective-permute-start.1 = (bf16[4,32768]{1,0:T(4,128)(2,1)S(1)}, bf16[4,32768]{1,0:T(4,128)(2,1)S(1)}, u32[]{:S(2)}, u32[]{:S(2)}) collective-permute-start(bf16[4,32768]{1,0:T(4,128)(2,1)S(1)} %get-tuple-element.4), channel_id=1, source_target_pairs={{1,0},{2,1},{3,2},{4,3},{5,4},{6,5},{7,6},{8,7},{9,8},{10,9},{11,1... | collective-permute-start | bytes 786440 | tf_op jit(solution)/shard_map/ppermute | solution.py:423
  6.6 12.3 %copy-start = (bf16[256,512]{1,0:T(8,128)(2,1)S(1)}, bf16[256,512]{1,0:T(8,128)(2,1)}, u32[]{:S(2)}) copy-start(bf16[256,512]{1,0:T(8,128)(2,1)} %constant.10.clone.refs_3_) | copy-start | bytes 786436
  6.6 12.3 %copy-start.1 = (f32[128,256]{1,0:T(8,128)S(1)}, f32[128,256]{1,0:T(8,128)}, u32[]{:S(2)}) copy-start(f32[128,256]{1,0:T(8,128)} %constant.12.clone.refs_5_) | copy-start | bytes 393220
  6.6 12.3 %copy-start.2 = (f32[128,256]{1,0:T(8,128)S(1)}, f32[128,256]{1,0:T(8,128)}, u32[]{:S(2)}) copy-start(f32[128,256]{1,0:T(8,128)} %constant.11.clone.refs_4_) | copy-start | bytes 393220
  6.6 12.3 %copy-start.3 = (bf16[128,256]{1,0:T(8,128)(2,1)S(1)}, bf16[128,256]{1,0:T(8,128)(2,1)}, u32[]{:S(2)}) copy-start(bf16[128,256]{1,0:T(8,128)(2,1)} %constant.13.clone.refs_6_) | copy-start | bytes 196612
  6.6 14.6 %collective-permute-start = (bf16[4,32768]{1,0:T(4,128)(2,1)S(1)}, bf16[4,32768]{1,0:T(4,128)(2,1)S(1)}, u32[]{:S(2)}, u32[]{:S(2)}) collective-permute-start(bf16[4,32768]{1,0:T(4,128)(2,1)S(1)} %get-tuple-element.5), channel_id=1, source_target_pairs={{1,0},{2,1},{3,2},{4,3},{5,4},{6,5},{7,6},{8,7},{9,8},{10,9},{11,1... | collective-permute-start | bytes 786440 | tf_op jit(solution)/shard_map/ppermute | solution.py:423
  24.6 12.6 %copy-start.4 = (s32[8,64]{1,0:T(8,128)S(1)}, s32[8,64]{1,0:T(8,128)}, u32[]{:S(2)}) copy-start(s32[8,64]{1,0:T(8,128)} %tones.3) | copy-start | bytes 6148
  24.6 65.0 %all-to-all-start = ((bf16[256,32,128]{2,1,0:T(8,128)(2,1)}), bf16[256,32,128]{2,1,0:T(8,128)(2,1)S(1)}, u32[]{:S(2)}, u32[]{:S(2)}) async-start(bf16[256,32,128]{2,1,0:T(8,128)(2,1)} %get-tuple-element.3.msgs), calls=%async_computation | async-start | bytes 4194304 | tf_op jit(solution)/shard_map/all_to_all | solution.py:459
  41.5 2.9 %collective-permute-start.2 = (f32[8,128]{1,0:T(8,128)S(1)}, f32[8,128]{1,0:T(8,128)S(1)}, u32[]{:S(2)}, u32[]{:S(2)}) collective-permute-start(f32[8,128]{1,0:T(8,128)S(1)} %tones.2), channel_id=1, source_target_pairs={{0,1},{1,0},{2,3},{3,2},{4,5},{5,4},{6,7},{7,6},{8,9},{9,8},{10,11... | collective-permute-start | bytes 12296 | tf_op jit(solution)/shard_map/ppermute | solution.py:427
  44.4 3.8 %collective-permute-start.3 = (f32[8,128]{1,0:T(8,128)S(1)}, f32[8,128]{1,0:T(8,128)S(1)}, u32[]{:S(2)}, u32[]{:S(2)}) collective-permute-start(f32[8,128]{1,0:T(8,128)S(1)} %add.18), channel_id=1, source_target_pairs={{0,2},{2,0},{4,6},{6,4},{8,10},{10,8},{12,14},{14,12},{16,18},{18,... | collective-permute-start | bytes 12296 | tf_op jit(solution)/shard_map/ppermute | solution.py:427
  48.2 33.8 %collective-permute-start.7 = (f32[8,128]{1,0:T(8,128)S(1)}, f32[8,128]{1,0:T(8,128)S(1)}, u32[]{:S(2)}, u32[]{:S(2)}) collective-permute-start(f32[8,128]{1,0:T(8,128)S(1)} %add.19), channel_id=1, source_target_pairs={{0,12},{2,30},{4,16},{6,2},{8,20},{10,6},{12,24},{14,10},{16,28},{... | collective-permute-start | bytes 12296 | tf_op jit(solution)/shard_map/ppermute | solution.py:427
  50.8 31.9 %collective-permute-start.6 = (f32[8,128]{1,0:T(8,128)S(1)}, f32[8,128]{1,0:T(8,128)S(1)}, u32[]{:S(2)}, u32[]{:S(2)}) collective-permute-start(f32[8,128]{1,0:T(8,128)S(1)} %add.19), channel_id=1, source_target_pairs={{0,8},{2,26},{4,12},{6,30},{8,16},{10,2},{12,20},{14,6},{16,24},{1... | collective-permute-start | bytes 12296 | tf_op jit(solution)/shard_map/ppermute | solution.py:427
  52.3 30.3 %collective-permute-start.5 = (f32[8,128]{1,0:T(8,128)S(1)}, f32[8,128]{1,0:T(8,128)S(1)}, u32[]{:S(2)}, u32[]{:S(2)}) collective-permute-start(f32[8,128]{1,0:T(8,128)S(1)} %add.19), channel_id=1, source_target_pairs={{0,4},{2,22},{4,8},{6,26},{8,12},{10,30},{12,16},{14,2},{16,20},{1... | collective-permute-start | bytes 12296 | tf_op jit(solution)/shard_map/ppermute | solution.py:427
  53.0 34.7 %collective-permute-start.4 = (f32[8,128]{1,0:T(8,128)S(1)}, f32[8,128]{1,0:T(8,128)S(1)}, u32[]{:S(2)}, u32[]{:S(2)}) collective-permute-start(f32[8,128]{1,0:T(8,128)S(1)} %add.19), channel_id=1, source_target_pairs={{0,0},{2,18},{4,4},{6,22},{8,8},{10,26},{12,12},{14,30},{16,16},{1... | collective-permute-start | bytes 12296 | tf_op jit(solution)/shard_map/ppermute | solution.py:427
  87.8 1.2 %collective-permute-start.8 = (f32[8,128]{1,0:T(8,128)S(1)}, f32[8,128]{1,0:T(8,128)S(1)}, u32[]{:S(2)}, u32[]{:S(2)}) collective-permute-start(f32[8,128]{1,0:T(8,128)S(1)} %add_add_fusion), channel_id=1, source_target_pairs={{0,2},{2,0},{4,6},{6,4},{8,10},{10,8},{12,14},{14,12},{16,18},{18,... | collective-permute-start | bytes 12296 | tf_op jit(solution)/shard_map/ppermute | solution.py:427

commit v8 on v6

--- a/solution.py
+++ b/solution.py
@@ -291,7 +291,7 @@
         g = i // local
         s = i - g * local
         got = rs[pl.ds(g * times * local + s, times, stride=local), :]
-        ts[pl.ds(pl.multiple_of(i * PITCH, 8), LANES), :] = got.T
+        ts[pl.ds(pl.multiple_of(i * PITCH, 8), LANES), :] = got.astype(bf16).T.astype(f32)
         return 0
 
     lax.fori_loop(0, S, turn, 0, unroll=True)
@@ -362,7 +362,7 @@
     return lax.ppermute(value, axis, [(i, dest(i)) for i in range(lax.axis_size(axis))])
 
 
-def gathered_sum(picks):
+def over_z(picks):
     value = picks + routed(picks, "cores", lambda i: i ^ 1)
     value = value + routed(value, "tm", lambda i: i ^ 1)
     size = lax.axis_size("tm")
@@ -371,8 +371,7 @@
         routed(value, "tm", lambda i, d=d: (i + 2 * (d + half * (i % 2))) % size)
         for d in range(half)
     ]
-    value = sum(steps)
-    return value + routed(value, "tm", lambda i: i ^ 1)
+    return sum(steps)
 
 
 def shards(samples, delays, valid, tone_chan):
@@ -385,7 +384,9 @@
     spectra_all = here * lax.axis_size("tm") * lax.axis_size("cores")
     norm_scale = 1.0 / math.sqrt(spectra_all)
     recv = lax.all_to_all(msgs, whole, split_axis=0, concat_axis=0, tiled=True)
-    phase_cal = gathered_sum(tone_sums(msgs, tone_chan)) * norm_scale
+    half = over_z(tone_sums(msgs, tone_chan)) * norm_scale
+    recv, half = lax.optimization_barrier((recv, half))
+    phase_cal = half + routed(half, "tm", lambda i: i ^ 1)
     return (correlated(recv, stations, norm_scale), phase_cal)
 
 

time: 94.2 us -> 95.1 us (level)
    all_to_all x1, waiting for transfers between devices: 0.01 us -> 1.4 us  [shards(): recv = lax.all_to_all(msgs, whole, split_axis=0, concat_axis=0, tiled=True)]
    ppermute x7, waiting for transfers between devices: 32.2 us -> 31 us  [routed(): lax.ppermute(value, axis, [(i, dest(i)) for i in range(lax.axis_size(axis...]
  transfers between devices with their start and end apart: 9 -> 9, of which waited for: 7 -> 7; matrix products, arithmetic and copies ran while one was open for 1% -> 0% of each run, Pallas kernels for 13% -> 17%
where the time goes in v8:
time: 95.1 us; the launch traced here: 94.7 us
  waiting for transfers between devices  36.2 us (38%)
  starting transfers between devices  36 us (38%)
  Pallas kernels  20 us (21%)
  local copies, waits for them, and re-layouts  1.11 us (1%)
    ppermute x7, waiting for transfers between devices, routed(): lax.ppermute(value, axis, [(i, dest(i)) for i in range(lax.axis_size(axis...  31 us
    ppermute x7, starting transfers between devices, routed(): lax.ppermute(value, axis, [(i, dest(i)) for i in range(lax.axis_size(axis...  16.1 us
    all_to_all x1, starting transfers between devices, shards(): recv = lax.all_to_all(msgs, whole, split_axis=0, concat_axis=0, tiled=True)  15.3 us
    pallas_call x2, Pallas kernels, channelized(): pl.pallas_call(lambda *refs: f_kernel(nt, skip, at_row, bool(so_far), *re...  11.6 us
    ppermute x1, starting transfers between devices, passed_along(): return lax.ppermute(block, axis, route)  4.64 us
    pallas_call x1, Pallas kernels, tone_sums(): pl.pallas_call(tone_kernel, out_shape=jax.ShapeDtypeStruct((tone_chan.sha...  4.37 us
    pallas_call x1, Pallas kernels, correlated(): pl.pallas_call(lambda *refs: x_kernel(norm_scale, per_source, *refs), out...  4.05 us
    ppermute x1, waiting for transfers between devices, passed_along(): return lax.ppermute(block, axis, route)  3.77 us
  transfers between devices with their start and end apart: 9, of which 7 were waited for; matrix products, arithmetic and copies ran while one was open for 0% of the time, Pallas kernels for 17%

profile of v8, /device:TPU:1, one launch (start us, length us, event | category | flops | bytes accessed | tf_op | source)
XLA Modules:
  0.0 94.7 jit_solution(14472527949390116634)
XLA Ops:
  0.6 1.1 %slice.3 = bf16[8,32768]{1,0:T(8,128)(2,1)S(1)} slice(bf16[8,131072]{1,0:T(8,128)(2,1)} %refs_0_.3), slice={[0:8], [0:32768]} | slice | bytes 1048576 | tf_op jit(solution)/shard_map/slice | solution.py:381
  1.7 0.0 copy-start.1
  1.7 0.0 copy-start.2
  1.8 4.6 %collective-permute-start = (bf16[8,32768]{1,0:T(8,128)(2,1)S(1)}, bf16[8,32768]{1,0:T(8,128)(2,1)S(1)}, u32[]{:S(2)}, u32[]{:S(2)}) collective-permute-start(bf16[8,32768]{1,0:T(8,128)(2,1)S(1)} %slice.3), channel_id=1, source_target_pairs={{1,0},{2,1},{3,2},{4,3},{5,4},{6,5},{7,6},{8,7},{9,8},{10,9},{11,1... | collective-permute-start | bytes 1572872 | tf_op jit(solution)/shard_map/ppermute | solution.py:358
  6.4 7.9 %channelize.2.refs_8_ = bf16[256,32,128]{2,1,0:T(8,128)(2,1)} custom-call(bf16[8,131072]{1,0:T(8,128)(2,1)} %refs_0_.3, s32[8]{0:T(128)} %refs_1_.3, s32[8]{0:T(128)} %refs_2_.3, bf16[256,512]{1,0:T(8,128)(2,1)} %constant.10.clone.refs_3_, f32[128,256]{1,0:T(8,128)} %constant.11.clone.refs_4_, f32[128,256]{1,0:T(8,128)} %constant.12.clone.refs_5_, ...), custom_call_target="tpu_custom_call" | custom-call | tf_op jit(solution)/shard_map/channelize/pallas_call | solution.py:206
  14.4 3.8 %collective-permute-done.refs_7_ = bf16[8,32768]{1,0:T(8,128)(2,1)S(1)} collective-permute-done((bf16[8,32768]{1,0:T(8,128)(2,1)S(1)}, bf16[8,32768]{1,0:T(8,128)(2,1)S(1)}, u32[]{:S(2)}, u32[]{:S(2)}) %collective-permute-start) | collective-permute-done | bytes 524320 | tf_op jit(solution)/shard_map/ppermute | solution.py:358
  18.1 3.7 %channelize.3.msgs = bf16[256,32,128]{2,1,0:T(8,128)(2,1)} custom-call(bf16[8,131072]{1,0:T(8,128)(2,1)} %refs_0_.3, s32[8]{0:T(128)} %refs_1_.3, s32[8]{0:T(128)} %refs_2_.3, bf16[256,512]{1,0:T(8,128)(2,1)S(1)} %copy-done, f32[128,256]{1,0:T(8,128)S(1)} %copy-done.2, f32[128,256]{1,0:T(8,128)S(1)} %copy-done.1, ...), custom_call_target="tpu_custom_call", output_to_operand_aliasing={{}: (8, {})} | custom-call | tf_op jit(solution)/shard_map/channelize/pallas_call | solution.py:206
  21.8 15.3 %all-to-all-start = ((bf16[256,32,128]{2,1,0:T(8,128)(2,1)}), bf16[256,32,128]{2,1,0:T(8,128)(2,1)S(1)}, u32[]{:S(2)}, u32[]{:S(2)}) async-start(bf16[256,32,128]{2,1,0:T(8,128)(2,1)} %channelize.3.msgs), calls=%async_computation | async-start | bytes 4194304 | tf_op jit(solution)/shard_map/all_to_all | solution.py:386
  37.1 4.4 %tones.2 = f32[8,128]{1,0:T(8,128)S(1)} custom-call(s32[8,64]{1,0:T(8,128)S(1)} %copy-done.4, bf16[256,32,128]{2,1,0:T(8,128)(2,1)} %channelize.3.msgs), custom_call_target="tpu_custom_call" | custom-call | tf_op jit(solution)/shard_map/tones/pallas_call | solution.py:260
  41.5 1.5 %collective-permute-start.1 = (f32[8,128]{1,0:T(8,128)S(1)}, f32[8,128]{1,0:T(8,128)S(1)}, u32[]{:S(2)}, u32[]{:S(2)}) collective-permute-start(f32[8,128]{1,0:T(8,128)S(1)} %tones.2), channel_id=1, source_target_pairs={{0,1},{1,0},{2,3},{3,2},{4,5},{5,4},{6,7},{7,6},{8,9},{9,8},{10,11... | collective-permute-start | bytes 12296 | tf_op jit(solution)/shard_map/ppermute | solution.py:362
  43.0 1.4 %collective-permute-done.1 = f32[8,128]{1,0:T(8,128)S(1)} collective-permute-done((f32[8,128]{1,0:T(8,128)S(1)}, f32[8,128]{1,0:T(8,128)S(1)}, u32[]{:S(2)}, u32[]{:S(2)}) %collective-permute-start.1) | collective-permute-done | bytes 4128 | tf_op jit(solution)/shard_map/ppermute | solution.py:362
  44.4 3.0 %collective-permute-start.2 = (f32[8,128]{1,0:T(8,128)S(1)}, f32[8,128]{1,0:T(8,128)S(1)}, u32[]{:S(2)}, u32[]{:S(2)}) collective-permute-start(f32[8,128]{1,0:T(8,128)S(1)} %add.18), channel_id=1, source_target_pairs={{0,2},{2,0},{4,6},{6,4},{8,10},{10,8},{12,14},{14,12},{16,18},{18,... | collective-permute-start | bytes 12296 | tf_op jit(solution)/shard_map/ppermute | solution.py:362
  47.3 0.8 collective-permute-done.2
  48.2 2.5 %collective-permute-start.6 = (f32[8,128]{1,0:T(8,128)S(1)}, f32[8,128]{1,0:T(8,128)S(1)}, u32[]{:S(2)}, u32[]{:S(2)}) collective-permute-start(f32[8,128]{1,0:T(8,128)S(1)} %add.19), channel_id=1, source_target_pairs={{0,12},{2,30},{4,16},{6,2},{8,20},{10,6},{12,24},{14,10},{16,28},{... | collective-permute-start | bytes 12296 | tf_op jit(solution)/shard_map/ppermute | solution.py:362
  50.7 1.6 %collective-permute-start.5 = (f32[8,128]{1,0:T(8,128)S(1)}, f32[8,128]{1,0:T(8,128)S(1)}, u32[]{:S(2)}, u32[]{:S(2)}) collective-permute-start(f32[8,128]{1,0:T(8,128)S(1)} %add.19), channel_id=1, source_target_pairs={{0,8},{2,26},{4,12},{6,30},{8,16},{10,2},{12,20},{14,6},{16,24},{1... | collective-permute-start | bytes 12296 | tf_op jit(solution)/shard_map/ppermute | solution.py:362
  52.3 0.7 collective-permute-start.4
  53.0 5.9 %collective-permute-start.3 = (f32[8,128]{1,0:T(8,128)S(1)}, f32[8,128]{1,0:T(8,128)S(1)}, u32[]{:S(2)}, u32[]{:S(2)}) collective-permute-start(f32[8,128]{1,0:T(8,128)S(1)} %add.19), channel_id=1, source_target_pairs={{0,0},{2,18},{4,4},{6,22},{8,8},{10,26},{12,12},{14,30},{16,16},{1... | collective-permute-start | bytes 12296 | tf_op jit(solution)/shard_map/ppermute | solution.py:362
  58.9 23.1 %collective-permute-done.6 = f32[8,128]{1,0:T(8,128)S(1)} collective-permute-done((f32[8,128]{1,0:T(8,128)S(1)}, f32[8,128]{1,0:T(8,128)S(1)}, u32[]{:S(2)}, u32[]{:S(2)}) %collective-permute-start.6) | collective-permute-done | bytes 4128 | tf_op jit(solution)/shard_map/ppermute | solution.py:362
  82.0 0.6 collective-permute-done.5
  82.6 5.1 %collective-permute-done.3 = f32[8,128]{1,0:T(8,128)S(1)} collective-permute-done((f32[8,128]{1,0:T(8,128)S(1)}, f32[8,128]{1,0:T(8,128)S(1)}, u32[]{:S(2)}, u32[]{:S(2)}) %collective-permute-start.3) | collective-permute-done | bytes 4128 | tf_op jit(solution)/shard_map/ppermute | solution.py:362
  87.7 1.4 %all-to-all-done.refs_0_ = bf16[256,32,128]{2,1,0:T(8,128)(2,1)S(1)} async-done(((bf16[256,32,128]{2,1,0:T(8,128)(2,1)}), bf16[256,32,128]{2,1,0:T(8,128)(2,1)S(1)}, u32[]{:S(2)}, u32[]{:S(2)}) %all-to-all-start) | async-done | bytes 2097184 | tf_op jit(solution)/shard_map/all_to_all | solution.py:386
  89.2 0.9 collective-permute-start.7
  90.1 4.0 %correlate.1 = f32[64,8192]{1,0:T(8,128)} custom-call(bf16[256,32,128]{2,1,0:T(8,128)(2,1)S(1)} %all-to-all-done.refs_0_), custom_call_target="tpu_custom_call" | custom-call | tf_op jit(solution)/shard_map/correlate/pallas_call | solution.py:338
  94.1 0.6 add.23
  (13 shorter events, 0.0 us)
Async XLA Ops:
  1.7 16.4 %copy-start = (bf16[256,512]{1,0:T(8,128)(2,1)S(1)}, bf16[256,512]{1,0:T(8,128)(2,1)}, u32[]{:S(2)}) copy-start(bf16[256,512]{1,0:T(8,128)(2,1)} %constant.10.clone.refs_3_) | copy-start | bytes 786436
  1.7 16.4 %copy-start.1 = (f32[128,256]{1,0:T(8,128)S(1)}, f32[128,256]{1,0:T(8,128)}, u32[]{:S(2)}) copy-start(f32[128,256]{1,0:T(8,128)} %constant.12.clone.refs_5_) | copy-start | bytes 393220
  1.7 16.4 %copy-start.2 = (f32[128,256]{1,0:T(8,128)S(1)}, f32[128,256]{1,0:T(8,128)}, u32[]{:S(2)}) copy-start(f32[128,256]{1,0:T(8,128)} %constant.11.clone.refs_4_) | copy-start | bytes 393220
  1.7 16.4 %copy-start.3 = (bf16[128,256]{1,0:T(8,128)(2,1)S(1)}, bf16[128,256]{1,0:T(8,128)(2,1)}, u32[]{:S(2)}) copy-start(bf16[128,256]{1,0:T(8,128)(2,1)} %constant.13.clone.refs_6_) | copy-start | bytes 196612
  1.8 16.4 %collective-permute-start = (bf16[8,32768]{1,0:T(8,128)(2,1)S(1)}, bf16[8,32768]{1,0:T(8,128)(2,1)S(1)}, u32[]{:S(2)}, u32[]{:S(2)}) collective-permute-start(bf16[8,32768]{1,0:T(8,128)(2,1)S(1)} %slice.3), channel_id=1, source_target_pairs={{1,0},{2,1},{3,2},{4,3},{5,4},{6,5},{7,6},{8,7},{9,8},{10,9},{11,1... | collective-permute-start | bytes 1572872 | tf_op jit(solution)/shard_map/ppermute | solution.py:358
  21.8 15.3 %copy-start.4 = (s32[8,64]{1,0:T(8,128)S(1)}, s32[8,64]{1,0:T(8,128)}, u32[]{:S(2)}) copy-start(s32[8,64]{1,0:T(8,128)} %tones.3) | copy-start | bytes 6148
  21.8 67.3 %all-to-all-start = ((bf16[256,32,128]{2,1,0:T(8,128)(2,1)}), bf16[256,32,128]{2,1,0:T(8,128)(2,1)S(1)}, u32[]{:S(2)}, u32[]{:S(2)}) async-start(bf16[256,32,128]{2,1,0:T(8,128)(2,1)} %channelize.3.msgs), calls=%async_computation | async-start | bytes 4194304 | tf_op jit(solution)/shard_map/all_to_all | solution.py:386
  41.5 2.9 %collective-permute-start.1 = (f32[8,128]{1,0:T(8,128)S(1)}, f32[8,128]{1,0:T(8,128)S(1)}, u32[]{:S(2)}, u32[]{:S(2)}) collective-permute-start(f32[8,128]{1,0:T(8,128)S(1)} %tones.2), channel_id=1, source_target_pairs={{0,1},{1,0},{2,3},{3,2},{4,5},{5,4},{6,7},{7,6},{8,9},{9,8},{10,11... | collective-permute-start | bytes 12296 | tf_op jit(solution)/shard_map/ppermute | solution.py:362
  44.4 3.8 %collective-permute-start.2 = (f32[8,128]{1,0:T(8,128)S(1)}, f32[8,128]{1,0:T(8,128)S(1)}, u32[]{:S(2)}, u32[]{:S(2)}) collective-permute-start(f32[8,128]{1,0:T(8,128)S(1)} %add.18), channel_id=1, source_target_pairs={{0,2},{2,0},{4,6},{6,4},{8,10},{10,8},{12,14},{14,12},{16,18},{18,... | collective-permute-start | bytes 12296 | tf_op jit(solution)/shard_map/ppermute | solution.py:362
  48.2 33.8 %collective-permute-start.6 = (f32[8,128]{1,0:T(8,128)S(1)}, f32[8,128]{1,0:T(8,128)S(1)}, u32[]{:S(2)}, u32[]{:S(2)}) collective-permute-start(f32[8,128]{1,0:T(8,128)S(1)} %add.19), channel_id=1, source_target_pairs={{0,12},{2,30},{4,16},{6,2},{8,20},{10,6},{12,24},{14,10},{16,28},{... | collective-permute-start | bytes 12296 | tf_op jit(solution)/shard_map/ppermute | solution.py:362
  50.7 31.9 %collective-permute-start.5 = (f32[8,128]{1,0:T(8,128)S(1)}, f32[8,128]{1,0:T(8,128)S(1)}, u32[]{:S(2)}, u32[]{:S(2)}) collective-permute-start(f32[8,128]{1,0:T(8,128)S(1)} %add.19), channel_id=1, source_target_pairs={{0,8},{2,26},{4,12},{6,30},{8,16},{10,2},{12,20},{14,6},{16,24},{1... | collective-permute-start | bytes 12296 | tf_op jit(solution)/shard_map/ppermute | solution.py:362
  52.3 30.3 %collective-permute-start.4 = (f32[8,128]{1,0:T(8,128)S(1)}, f32[8,128]{1,0:T(8,128)S(1)}, u32[]{:S(2)}, u32[]{:S(2)}) collective-permute-start(f32[8,128]{1,0:T(8,128)S(1)} %add.19), channel_id=1, source_target_pairs={{0,4},{2,22},{4,8},{6,26},{8,12},{10,30},{12,16},{14,2},{16,20},{1... | collective-permute-start | bytes 12296 | tf_op jit(solution)/shard_map/ppermute | solution.py:362
  53.0 34.7 %collective-permute-start.3 = (f32[8,128]{1,0:T(8,128)S(1)}, f32[8,128]{1,0:T(8,128)S(1)}, u32[]{:S(2)}, u32[]{:S(2)}) collective-permute-start(f32[8,128]{1,0:T(8,128)S(1)} %add.19), channel_id=1, source_target_pairs={{0,0},{2,18},{4,4},{6,22},{8,8},{10,26},{12,12},{14,30},{16,16},{1... | collective-permute-start | bytes 12296 | tf_op jit(solution)/shard_map/ppermute | solution.py:362
  89.2 5.0 %collective-permute-start.7 = (f32[8,128]{1,0:T(8,128)S(1)}, f32[8,128]{1,0:T(8,128)S(1)}, u32[]{:S(2)}, u32[]{:S(2)}) collective-permute-start(f32[8,128]{1,0:T(8,128)S(1)} %add_multiply_fusion), channel_id=1, source_target_pairs={{0,2},{2,0},{4,6},{6,4},{8,10},{10,8},{12,14},{14,12},{16,18},{18,... | collective-permute-start | bytes 12296 | tf_op jit(solution)/shard_map/ppermute | solution.py:362

commit v9 on v7

--- a/solution.py
+++ b/solution.py
@@ -45,7 +45,6 @@
 
 OPITCH = NQ + 8
 PIECES = 4
-HALVES = 2
 ROWS = MAXD // LANES
 
 
@@ -137,9 +136,9 @@
 
 
 def early_kernel(nt, *refs):
-    stream, given, msgs = refs[0], refs[1:7], refs[7]
-    xin, xs, obuf, mbuf, in_sem, out_sem, small_sem = refs[8:15]
-    held = refs[15:]
+    stream, given, msgs, handed = refs[0], refs[1:7], refs[7], refs[8]
+    xin, xs, obuf, mbuf, in_sem, out_sem, small_sem = refs[9:16]
+    held = refs[16:]
     stations = stream.shape[0]
     chunk = FA * LANES
     pitch = xs.shape[0] // stations
@@ -160,6 +159,7 @@
     for i, copy in enumerate(copies):
         copy.wait()
         spread(xin, i * FA, xs, i * FA, pitch)
+    spread(xin, nt * FA, handed, 0, handed.shape[0] // stations)
     xs[pl.ds((nt + 1) * FA, stations, stride=pitch), :] = jnp.zeros((stations, LANES), f32)
     for copy in small:
         copy.wait()
@@ -174,38 +174,24 @@
     write_messages(nt, 0, stations, obuf, mbuf, msgs, out_sem)
 
 
-def late_kernel(half, skip, at_row, *refs):
-    stream, given, tables, trail = refs[0], refs[1:3], refs[3:7], refs[7]
-    final = half == HALVES - 1
-    outs = refs[10:] if final else refs[8:]
-    if half and not final:
-        outs = refs[9:]
-    obuf, rest = outs[0], outs[1:]
-    if final:
-        msgs, mbuf, out_sem = rest[:3]
-        rest = rest[3:]
-    xin, xs, in_sem, small_sem = rest[:4]
-    held = rest[4:]
-    stations = stream.shape[0]
-    some = trail.shape[0]
+def late_kernel(at_row, *refs):
+    given, tables, trail = refs[:2], refs[2:6], refs[6]
+    xs, msgs, obuf, mbuf, out_sem, small_sem = refs[9:15]
+    held = refs[15:]
+    stations = trail.shape[0]
     pitch = xs.shape[0] // stations
-    copy = pltpu.make_async_copy(stream.at[:, pl.ds(skip, FA * LANES)], xin, in_sem)
     small = [
         pltpu.make_async_copy(source, target, small_sem.at[i])
         for i, (source, target) in enumerate(zip(given, held))
     ]
-    for begun in [copy] + small:
-        begun.start()
-    spread(trail, 0, xs, half * some * pitch + FA, pitch)
-    copy.wait()
-    spread(xin, 0, xs, 0, pitch)
+    for copy in small:
+        copy.start()
+    spread(trail, 0, xs, FA, pitch)
     xs[pl.ds(FA + ROWS, stations, stride=pitch), :] = jnp.zeros((stations, LANES), f32)
     for copy in small:
         copy.wait()
-    chosen = [half * some + k for k in range(some)]
-    transform(chosen, 1, stations, held[0], held[1], tables, xs, obuf)
-    if final:
-        write_messages(1, at_row, stations, obuf, mbuf, msgs, out_sem)
+    transform(range(stations), 1, stations, held[0], held[1], tables, xs, obuf)
+    write_messages(1, at_row, stations, obuf, mbuf, msgs, out_sem)
 
 
 def odd_pitch(rows):
@@ -223,9 +209,12 @@
     nt = here - 1
     return pl.pallas_call(
         lambda *refs: early_kernel(nt, *refs),
-        out_shape=jax.ShapeDtypeStruct((NQ * NHI, here * stations, LANES), bf16),
+        out_shape=(
+            jax.ShapeDtypeStruct((NQ * NHI, here * stations, LANES), bf16),
+            pltpu.VMEM((stations * odd_pitch(FA + ROWS), LANES), f32),
+        ),
         in_specs=[far] * 7,
-        out_specs=pl.BlockSpec(memory_space=pl.ANY),
+        out_specs=(pl.BlockSpec(memory_space=pl.ANY), pl.BlockSpec(memory_space=pltpu.VMEM)),
         scratch_shapes=[
             pltpu.VMEM(stream.shape, bf16),
             pltpu.VMEM((stations * odd_pitch(here * FA), LANES), f32),
@@ -242,53 +231,33 @@
     )(*[off_chip(value) for value in (stream, delays, valid, *tables)])
 
 
-def late_messages(half, stream, delays, valid, tables, trail, so_far):
-    stations = stream.shape[0]
+def late_messages(delays, valid, tables, trail, msgs, handed):
+    stations = trail.shape[0]
     far = pl.BlockSpec(memory_space=pltpu.HBM)
     vmem = pl.BlockSpec(memory_space=pltpu.VMEM)
     hbm = pl.BlockSpec(memory_space=pl.ANY)
-    chunk = FA * LANES
-    here = stream.shape[1] // chunk
-    final = half == HALVES - 1
-    args = [off_chip(value) for value in (stream, delays, valid)]
-    args += [on_chip(value) for value in (*tables, trail)]
-    specs = [far] * 3 + [vmem] * 5
-    outs = [pltpu.VMEM((NHI * stations * OPITCH, LANES), f32)]
-    out_specs = [vmem]
-    scratch = []
-    aliases = {}
-    if half:
-        aliases[8] = 0
-        args.append(on_chip(so_far[0]))
-        specs.append(vmem)
-    if final:
-        msgs = so_far[1]
-        aliases[9] = 1
-        args.append(msgs)
-        specs.append(hbm)
-        outs.append(jax.ShapeDtypeStruct(msgs.shape, bf16))
-        out_specs.append(hbm)
-        scratch = [
+    at_row = msgs.shape[1] - stations
+    args = [off_chip(value) for value in (delays, valid)]
+    args += [on_chip(value) for value in (*tables, trail, handed)]
+    return pl.pallas_call(
+        lambda *refs: late_kernel(at_row, *refs),
+        out_shape=(
+            pltpu.VMEM(handed.shape, f32),
+            jax.ShapeDtypeStruct(msgs.shape, bf16),
+        ),
+        in_specs=[far] * 2 + [vmem] * 6 + [hbm],
+        out_specs=(vmem, hbm),
+        scratch_shapes=[
+            pltpu.VMEM((NHI * stations * OPITCH, LANES), f32),
             pltpu.VMEM((NQ * NHI, stations, LANES), bf16),
             pltpu.SemaphoreType.DMA((PIECES,)),
-        ]
-    return pl.pallas_call(
-        lambda *refs: late_kernel(half, (here - 1) * chunk, (here - 1) * stations, *refs),
-        out_shape=outs,
-        in_specs=specs,
-        out_specs=out_specs,
-        scratch_shapes=scratch
-        + [
-            pltpu.VMEM((stations, chunk), bf16),
-            pltpu.VMEM((stations * odd_pitch(FA + ROWS), LANES), f32),
-            pltpu.SemaphoreType.DMA(()),
             pltpu.SemaphoreType.DMA((2,)),
         ]
         + scalars(delays, valid),
-        input_output_aliases=aliases,
+        input_output_aliases={7: 0, 8: 1},
         compiler_params=pltpu.CompilerParams(vmem_limit_bytes=20 << 20),
         name="channelize_late",
-    )(*args)
+    )(*args, msgs)
 
 
 def tone_kernel(tones, msgs, picks, sums):
@@ -356,7 +325,7 @@
         g = i // local
         s = i - g * local
         got = rs[pl.ds(g * times * local + s, times, stride=local), :]
-        ts[pl.ds(pl.multiple_of(i * PITCH, 8), LANES), :] = got.T
+        ts[pl.ds(pl.multiple_of(i * PITCH, 8), LANES), :] = got.astype(bf16).T.astype(f32)
         return 0
 
     lax.fori_loop(0, S, turn, 0, unroll=True)
@@ -444,16 +413,10 @@
     stations, stretch = samples.shape
     whole = ("stn", "tm", "cores")
     here = stretch // (FA * FB)
-    some = stations // HALVES
-    trailing = [
-        passed_along(samples[i * some : (i + 1) * some, :MAXD], ("tm", "cores"), -1)
-        for i in range(HALVES)
-    ]
+    trailing = passed_along(samples[:, :MAXD], ("tm", "cores"), -1)
     tables = [jnp.asarray(table) for table in make_tables()]
-    own = (samples, delays, valid, tables)
-    early = early_messages(*own)
-    (held,) = late_messages(0, *own, trailing[0], ())
-    _, msgs = late_messages(1, *own, trailing[1], (held, early))
+    early = early_messages(samples, delays, valid, tables)
+    _, msgs = late_messages(delays, valid, tables, trailing, *early)
     spectra_all = here * lax.axis_size("tm") * lax.axis_size("cores")
     norm_scale = 1.0 / math.sqrt(spectra_all)
     recv = lax.all_to_all(msgs, whole, split_axis=0, concat_axis=0, tiled=True)

time: 94.4 us -> 92.9 us (0.984)
  waiting for transfers between devices: 32.2 us -> 35.5 us
  Pallas kernels: 22.3 us -> 19.6 us
  starting transfers between devices: 36.6 us -> 35 us
    ppermute x2 -> x1, starting transfers between devices: 8.82 us -> 4.51 us  [passed_along(): return lax.ppermute(block, axis, route)]
    ppermute x2 -> x1, waiting for transfers between devices: 0.01 us -> 3.28 us  [passed_along(): return lax.ppermute(block, axis, route)]
    all_to_all x1, starting transfers between devices: 12.6 us -> 15.3 us  [shards(): recv = lax.all_to_all(msgs, whole, split_axis=0, concat_axis=0, tiled=True)]
    pallas_call x3 -> x2, Pallas kernels: 13.5 us -> 11.2 us  [the longest x1 8.43 us: early_messages(): pl.pallas_call(lambda *refs: early_kernel(nt, *refs), out_shape=(jax.Shap...]
  transfers between devices with their start and end apart: 10 -> 9, of which waited for: 6 -> 7; matrix products, arithmetic and copies ran while one was open for 1% -> 1% of each run, Pallas kernels for 16% -> 14%
where the time goes in v9:
time: 92.9 us; the launch traced here: 92.6 us
  waiting for transfers between devices  35.5 us (38%)
  starting transfers between devices  35 us (38%)
  Pallas kernels  19.6 us (21%)
  local copies, waits for them, and re-layouts  1.18 us (1%)
    ppermute x7, waiting for transfers between devices, routed(): lax.ppermute(value, axis, [(i, dest(i)) for i in range(lax.axis_size(axis...  32.2 us
    all_to_all x1, starting transfers between devices, shards(): recv = lax.all_to_all(msgs, whole, split_axis=0, concat_axis=0, tiled=True)  15.3 us
    ppermute x7, starting transfers between devices, routed(): lax.ppermute(value, axis, [(i, dest(i)) for i in range(lax.axis_size(axis...  15.2 us
    pallas_call x1, Pallas kernels, early_messages(): pl.pallas_call(lambda *refs: early_kernel(nt, *refs), out_shape=(jax.Shap...  8.43 us
    ppermute x1, starting transfers between devices, passed_along(): return lax.ppermute(block, axis, route)  4.51 us
    pallas_call x1, Pallas kernels, tone_sums(): pl.pallas_call(tone_kernel, out_shape=jax.ShapeDtypeStruct((tone_chan.sha...  4.37 us
    pallas_call x1, Pallas kernels, correlated(): pl.pallas_call(lambda *refs: x_kernel(norm_scale, per_source, *refs), out...  4.04 us
    ppermute x1, waiting for transfers between devices, passed_along(): return lax.ppermute(block, axis, route)  3.28 us
  transfers between devices with their start and end apart: 9, of which 7 were waited for; matrix products, arithmetic and copies ran while one was open for 1% of the time, Pallas kernels for 14%

profile of v9, /device:TPU:1, one launch (start us, length us, event | category | flops | bytes accessed | tf_op | source)
XLA Modules:
  0.0 92.6 jit_solution(3828284895371004251)
XLA Ops:
  0.6 0.0 copy-start.3
  0.6 0.0 copy-start.1
  0.7 0.0 copy-start.2
  0.7 1.1 %slice.3 = bf16[8,32768]{1,0:T(8,128)(2,1)S(1)} slice(bf16[8,131072]{1,0:T(8,128)(2,1)} %refs_0_.2), slice={[0:8], [0:32768]} | slice | bytes 1048576 | tf_op jit(solution)/shard_map/slice | solution.py:416
  1.8 4.5 %collective-permute-start = (bf16[8,32768]{1,0:T(8,128)(2,1)S(1)}, bf16[8,32768]{1,0:T(8,128)(2,1)S(1)}, u32[]{:S(2)}, u32[]{:S(2)}) collective-permute-start(bf16[8,32768]{1,0:T(8,128)(2,1)S(1)} %slice.3), channel_id=1, source_target_pairs={{1,0},{2,1},{3,2},{4,3},{5,4},{6,5},{7,6},{8,7},{9,8},{10,9},{11,1... | collective-permute-start | bytes 1572872 | tf_op jit(solution)/shard_map/ppermute | solution.py:392
  6.3 8.4 %channelize.1 = (bf16[256,32,128]{2,1,0:T(8,128)(2,1)}, f32[4288,128]{1,0:T(8,128)S(1)}) custom-call(bf16[8,131072]{1,0:T(8,128)(2,1)} %refs_0_.2, s32[8]{0:T(128)} %refs_0_.3, s32[8]{0:T(128)} %refs_1_.3, bf16[256,512]{1,0:T(8,128)(2,1)} %constant.10.clone.refs_3_.refs_2_, f32[128,256]{1,0:T(8,128)} %constant.11.clone.refs_4_.refs_3_, ...), custom_call_target="tpu_custom_call" | custom-call | tf_op jit(solution)/shard_map/channelize/pallas_call | solution.py:210
  14.8 3.3 %collective-permute-done.refs_6_ = bf16[8,32768]{1,0:T(8,128)(2,1)S(1)} collective-permute-done((bf16[8,32768]{1,0:T(8,128)(2,1)S(1)}, bf16[8,32768]{1,0:T(8,128)(2,1)S(1)}, u32[]{:S(2)}, u32[]{:S(2)}) %collective-permute-start) | collective-permute-done | bytes 524320 | tf_op jit(solution)/shard_map/ppermute | solution.py:392
  18.1 2.8 %channelize_late.1 = (f32[4288,128]{1,0:T(8,128)S(1)}, bf16[256,32,128]{2,1,0:T(8,128)(2,1)}) custom-call(s32[8]{0:T(128)} %refs_0_.3, s32[8]{0:T(128)} %refs_1_.3, bf16[256,512]{1,0:T(8,128)(2,1)S(1)} %copy-done, f32[128,256]{1,0:T(8,128)S(1)} %copy-done.2, f32[128,256]{1,0:T(8,128)S(1)} %copy-done.1, ...), custom_call_target="tpu_custom_call", output_to_operand_aliasing={{0}: (7, {}), {1}: (8, {})} | custom-call | tf_op jit(solution)/shard_map/channelize_late/pallas_call | solution.py:242
  20.9 15.3 %all-to-all-start = ((bf16[256,32,128]{2,1,0:T(8,128)(2,1)}), bf16[256,32,128]{2,1,0:T(8,128)(2,1)S(1)}, u32[]{:S(2)}, u32[]{:S(2)}) async-start(bf16[256,32,128]{2,1,0:T(8,128)(2,1)} %get-tuple-element.7.msgs), calls=%async_computation | async-start | bytes 4194304 | tf_op jit(solution)/shard_map/all_to_all | solution.py:422
  36.2 4.4 %tones.2 = f32[8,128]{1,0:T(8,128)S(1)} custom-call(s32[8,64]{1,0:T(8,128)S(1)} %copy-done.4, bf16[256,32,128]{2,1,0:T(8,128)(2,1)} %get-tuple-element.7.msgs), custom_call_target="tpu_custom_call" | custom-call | tf_op jit(solution)/shard_map/tones/pallas_call | solution.py:294
  40.6 1.5 %collective-permute-start.1 = (f32[8,128]{1,0:T(8,128)S(1)}, f32[8,128]{1,0:T(8,128)S(1)}, u32[]{:S(2)}, u32[]{:S(2)}) collective-permute-start(f32[8,128]{1,0:T(8,128)S(1)} %tones.2), channel_id=1, source_target_pairs={{0,1},{1,0},{2,3},{3,2},{4,5},{5,4},{6,7},{7,6},{8,9},{9,8},{10,11... | collective-permute-start | bytes 12296 | tf_op jit(solution)/shard_map/ppermute | solution.py:396
  42.0 1.4 %collective-permute-done.1 = f32[8,128]{1,0:T(8,128)S(1)} collective-permute-done((f32[8,128]{1,0:T(8,128)S(1)}, f32[8,128]{1,0:T(8,128)S(1)}, u32[]{:S(2)}, u32[]{:S(2)}) %collective-permute-start.1) | collective-permute-done | bytes 4128 | tf_op jit(solution)/shard_map/ppermute | solution.py:396
  43.4 3.0 %collective-permute-start.2 = (f32[8,128]{1,0:T(8,128)S(1)}, f32[8,128]{1,0:T(8,128)S(1)}, u32[]{:S(2)}, u32[]{:S(2)}) collective-permute-start(f32[8,128]{1,0:T(8,128)S(1)} %add.18), channel_id=1, source_target_pairs={{0,2},{2,0},{4,6},{6,4},{8,10},{10,8},{12,14},{14,12},{16,18},{18,... | collective-permute-start | bytes 12296 | tf_op jit(solution)/shard_map/ppermute | solution.py:396
  46.4 0.8 collective-permute-done.2
  47.2 2.5 %collective-permute-start.6 = (f32[8,128]{1,0:T(8,128)S(1)}, f32[8,128]{1,0:T(8,128)S(1)}, u32[]{:S(2)}, u32[]{:S(2)}) collective-permute-start(f32[8,128]{1,0:T(8,128)S(1)} %add.19), channel_id=1, source_target_pairs={{0,12},{2,30},{4,16},{6,2},{8,20},{10,6},{12,24},{14,10},{16,28},{... | collective-permute-start | bytes 12296 | tf_op jit(solution)/shard_map/ppermute | solution.py:396
  49.8 1.6 %collective-permute-start.5 = (f32[8,128]{1,0:T(8,128)S(1)}, f32[8,128]{1,0:T(8,128)S(1)}, u32[]{:S(2)}, u32[]{:S(2)}) collective-permute-start(f32[8,128]{1,0:T(8,128)S(1)} %add.19), channel_id=1, source_target_pairs={{0,8},{2,26},{4,12},{6,30},{8,16},{10,2},{12,20},{14,6},{16,24},{1... | collective-permute-start | bytes 12296 | tf_op jit(solution)/shard_map/ppermute | solution.py:396
  51.4 0.7 collective-permute-start.4
  52.1 5.9 %collective-permute-start.3 = (f32[8,128]{1,0:T(8,128)S(1)}, f32[8,128]{1,0:T(8,128)S(1)}, u32[]{:S(2)}, u32[]{:S(2)}) collective-permute-start(f32[8,128]{1,0:T(8,128)S(1)} %add.19), channel_id=1, source_target_pairs={{0,0},{2,18},{4,4},{6,22},{8,8},{10,26},{12,12},{14,30},{16,16},{1... | collective-permute-start | bytes 12296 | tf_op jit(solution)/shard_map/ppermute | solution.py:396
  58.0 23.1 %collective-permute-done.6 = f32[8,128]{1,0:T(8,128)S(1)} collective-permute-done((f32[8,128]{1,0:T(8,128)S(1)}, f32[8,128]{1,0:T(8,128)S(1)}, u32[]{:S(2)}, u32[]{:S(2)}) %collective-permute-start.6) | collective-permute-done | bytes 4128 | tf_op jit(solution)/shard_map/ppermute | solution.py:396
  81.1 0.6 collective-permute-done.5
  81.7 5.1 %collective-permute-done.3 = f32[8,128]{1,0:T(8,128)S(1)} collective-permute-done((f32[8,128]{1,0:T(8,128)S(1)}, f32[8,128]{1,0:T(8,128)S(1)}, u32[]{:S(2)}, u32[]{:S(2)}) %collective-permute-start.3) | collective-permute-done | bytes 4128 | tf_op jit(solution)/shard_map/ppermute | solution.py:396
  86.8 1.2 %collective-permute-done.7 = f32[8,128]{1,0:T(8,128)S(1)} collective-permute-done((f32[8,128]{1,0:T(8,128)S(1)}, f32[8,128]{1,0:T(8,128)S(1)}, u32[]{:S(2)}, u32[]{:S(2)}) %collective-permute-start.7) | collective-permute-done | bytes 4128 | tf_op jit(solution)/shard_map/ppermute | solution.py:396
  88.0 0.6 add_multiply_fusion
  88.6 4.0 %correlate.1 = f32[64,8192]{1,0:T(8,128)} custom-call(bf16[256,32,128]{2,1,0:T(8,128)(2,1)S(1)} %all-to-all-done.refs_0_), custom_call_target="tpu_custom_call" | custom-call | tf_op jit(solution)/shard_map/correlate/pallas_call | solution.py:372
  (13 shorter events, 0.0 us)
Async XLA Ops:
  0.6 17.4 %copy-start.3 = (bf16[128,256]{1,0:T(8,128)(2,1)S(1)}, bf16[128,256]{1,0:T(8,128)(2,1)}, u32[]{:S(2)}) copy-start(bf16[128,256]{1,0:T(8,128)(2,1)} %constant.13.clone.refs_6_.refs_5_) | copy-start | bytes 196612
  0.6 17.4 %copy-start.1 = (f32[128,256]{1,0:T(8,128)S(1)}, f32[128,256]{1,0:T(8,128)}, u32[]{:S(2)}) copy-start(f32[128,256]{1,0:T(8,128)} %constant.12.clone.refs_5_.refs_4_) | copy-start | bytes 393220
  0.7 17.4 %copy-start.2 = (f32[128,256]{1,0:T(8,128)S(1)}, f32[128,256]{1,0:T(8,128)}, u32[]{:S(2)}) copy-start(f32[128,256]{1,0:T(8,128)} %constant.11.clone.refs_4_.refs_3_) | copy-start | bytes 393220
  0.7 17.4 %copy-start = (bf16[256,512]{1,0:T(8,128)(2,1)S(1)}, bf16[256,512]{1,0:T(8,128)(2,1)}, u32[]{:S(2)}) copy-start(bf16[256,512]{1,0:T(8,128)(2,1)} %constant.10.clone.refs_3_.refs_2_) | copy-start | bytes 786436
  1.8 16.2 %collective-permute-start = (bf16[8,32768]{1,0:T(8,128)(2,1)S(1)}, bf16[8,32768]{1,0:T(8,128)(2,1)S(1)}, u32[]{:S(2)}, u32[]{:S(2)}) collective-permute-start(bf16[8,32768]{1,0:T(8,128)(2,1)S(1)} %slice.3), channel_id=1, source_target_pairs={{1,0},{2,1},{3,2},{4,3},{5,4},{6,5},{7,6},{8,7},{9,8},{10,9},{11,1... | collective-permute-start | bytes 1572872 | tf_op jit(solution)/shard_map/ppermute | solution.py:392
  20.9 15.3 %copy-start.4 = (s32[8,64]{1,0:T(8,128)S(1)}, s32[8,64]{1,0:T(8,128)}, u32[]{:S(2)}) copy-start(s32[8,64]{1,0:T(8,128)} %tones.3) | copy-start | bytes 6148
  20.9 67.7 %all-to-all-start = ((bf16[256,32,128]{2,1,0:T(8,128)(2,1)}), bf16[256,32,128]{2,1,0:T(8,128)(2,1)S(1)}, u32[]{:S(2)}, u32[]{:S(2)}) async-start(bf16[256,32,128]{2,1,0:T(8,128)(2,1)} %get-tuple-element.7.msgs), calls=%async_computation | async-start | bytes 4194304 | tf_op jit(solution)/shard_map/all_to_all | solution.py:422
  40.6 2.9 %collective-permute-start.1 = (f32[8,128]{1,0:T(8,128)S(1)}, f32[8,128]{1,0:T(8,128)S(1)}, u32[]{:S(2)}, u32[]{:S(2)}) collective-permute-start(f32[8,128]{1,0:T(8,128)S(1)} %tones.2), channel_id=1, source_target_pairs={{0,1},{1,0},{2,3},{3,2},{4,5},{5,4},{6,7},{7,6},{8,9},{9,8},{10,11... | collective-permute-start | bytes 12296 | tf_op jit(solution)/shard_map/ppermute | solution.py:396
  43.4 3.8 %collective-permute-start.2 = (f32[8,128]{1,0:T(8,128)S(1)}, f32[8,128]{1,0:T(8,128)S(1)}, u32[]{:S(2)}, u32[]{:S(2)}) collective-permute-start(f32[8,128]{1,0:T(8,128)S(1)} %add.18), channel_id=1, source_target_pairs={{0,2},{2,0},{4,6},{6,4},{8,10},{10,8},{12,14},{14,12},{16,18},{18,... | collective-permute-start | bytes 12296 | tf_op jit(solution)/shard_map/ppermute | solution.py:396
  47.2 33.8 %collective-permute-start.6 = (f32[8,128]{1,0:T(8,128)S(1)}, f32[8,128]{1,0:T(8,128)S(1)}, u32[]{:S(2)}, u32[]{:S(2)}) collective-permute-start(f32[8,128]{1,0:T(8,128)S(1)} %add.19), channel_id=1, source_target_pairs={{0,12},{2,30},{4,16},{6,2},{8,20},{10,6},{12,24},{14,10},{16,28},{... | collective-permute-start | bytes 12296 | tf_op jit(solution)/shard_map/ppermute | solution.py:396
  49.8 31.9 %collective-permute-start.5 = (f32[8,128]{1,0:T(8,128)S(1)}, f32[8,128]{1,0:T(8,128)S(1)}, u32[]{:S(2)}, u32[]{:S(2)}) collective-permute-start(f32[8,128]{1,0:T(8,128)S(1)} %add.19), channel_id=1, source_target_pairs={{0,8},{2,26},{4,12},{6,30},{8,16},{10,2},{12,20},{14,6},{16,24},{1... | collective-permute-start | bytes 12296 | tf_op jit(solution)/shard_map/ppermute | solution.py:396
  51.4 30.3 %collective-permute-start.4 = (f32[8,128]{1,0:T(8,128)S(1)}, f32[8,128]{1,0:T(8,128)S(1)}, u32[]{:S(2)}, u32[]{:S(2)}) collective-permute-start(f32[8,128]{1,0:T(8,128)S(1)} %add.19), channel_id=1, source_target_pairs={{0,4},{2,22},{4,8},{6,26},{8,12},{10,30},{12,16},{14,2},{16,20},{1... | collective-permute-start | bytes 12296 | tf_op jit(solution)/shard_map/ppermute | solution.py:396
  52.1 34.7 %collective-permute-start.3 = (f32[8,128]{1,0:T(8,128)S(1)}, f32[8,128]{1,0:T(8,128)S(1)}, u32[]{:S(2)}, u32[]{:S(2)}) collective-permute-start(f32[8,128]{1,0:T(8,128)S(1)} %add.19), channel_id=1, source_target_pairs={{0,0},{2,18},{4,4},{6,22},{8,8},{10,26},{12,12},{14,30},{16,16},{1... | collective-permute-start | bytes 12296 | tf_op jit(solution)/shard_map/ppermute | solution.py:396
  86.8 1.2 %collective-permute-start.7 = (f32[8,128]{1,0:T(8,128)S(1)}, f32[8,128]{1,0:T(8,128)S(1)}, u32[]{:S(2)}, u32[]{:S(2)}) collective-permute-start(f32[8,128]{1,0:T(8,128)S(1)} %add_add_fusion), channel_id=1, source_target_pairs={{0,2},{2,0},{4,6},{6,4},{8,10},{10,8},{12,14},{14,12},{16,18},{18,... | collective-permute-start | bytes 12296 | tf_op jit(solution)/shard_map/ppermute | solution.py:396

commit v10 on v9

--- a/solution.py
+++ b/solution.py
@@ -64,7 +64,7 @@
         ].astype(f32)
         return 0
 
-    lax.fori_loop(0, FA, one_row, 0, unroll=16)
+    lax.fori_loop(0, FA, one_row, 0, unroll=32)
 
 
 def transform(chosen, nt, stations, delays, valid, tables, xs, obuf):
@@ -123,7 +123,7 @@
                 mbuf[q * NHI + h] = got.astype(bf16)
             return 0
 
-        lax.fori_loop(i * per, (i + 1) * per, gather, 0, unroll=4)
+        lax.fori_loop(i * per, (i + 1) * per, gather, 0, unroll=True)
         span = pl.ds(i * per * NHI, per * NHI)
         sent.append(
             pltpu.make_async_copy(
@@ -233,19 +233,17 @@
 
 def late_messages(delays, valid, tables, trail, msgs, handed):
     stations = trail.shape[0]
-    far = pl.BlockSpec(memory_space=pltpu.HBM)
     vmem = pl.BlockSpec(memory_space=pltpu.VMEM)
     hbm = pl.BlockSpec(memory_space=pl.ANY)
     at_row = msgs.shape[1] - stations
-    args = [off_chip(value) for value in (delays, valid)]
-    args += [on_chip(value) for value in (*tables, trail, handed)]
+    args = [on_chip(value) for value in (delays, valid, *tables, trail, handed)]
     return pl.pallas_call(
         lambda *refs: late_kernel(at_row, *refs),
         out_shape=(
             pltpu.VMEM(handed.shape, f32),
             jax.ShapeDtypeStruct(msgs.shape, bf16),
         ),
-        in_specs=[far] * 2 + [vmem] * 6 + [hbm],
+        in_specs=[vmem] * 8 + [hbm],
         out_specs=(vmem, hbm),
         scratch_shapes=[
             pltpu.VMEM((NHI * stations * OPITCH, LANES), f32),
@@ -314,21 +312,14 @@
     groups = S // local
     times = sources // groups * rows // local
 
-    def widen(i, _):
-        at = pl.multiple_of(i * rows, rows)
-        rs[pl.ds(at, rows), :] = recv[i].astype(f32)
-        return 0
-
-    lax.fori_loop(0, sources, widen, 0, unroll=8)
-
-    def turn(i, _):
-        g = i // local
-        s = i - g * local
-        got = rs[pl.ds(g * times * local + s, times, stride=local), :]
-        ts[pl.ds(pl.multiple_of(i * PITCH, 8), LANES), :] = got.astype(bf16).T.astype(f32)
-        return 0
-
-    lax.fori_loop(0, S, turn, 0, unroll=True)
+    per_group = sources // groups
+    for g in range(groups):
+        for i in range(g * per_group, (g + 1) * per_group):
+            rs[pl.ds(i * rows, rows), :] = recv[i].astype(f32)
+        for s in range(local):
+            got = rs[pl.ds(g * times * local + s, times, stride=local), :]
+            at = (g * local + s) * PITCH
+            ts[pl.ds(at, LANES), :] = got.astype(bf16).T.astype(f32)
 
     lane = lax.broadcasted_iota(jnp.int32, (8, LANES), 1)
 
@@ -343,16 +334,16 @@
             straight = jnp.concatenate([plus, quad], axis=1)
             turned = jnp.concatenate([quad, minus], axis=1)
             left = jnp.concatenate([straight, turned], axis=0)
-            right = jnp.concatenate([straight, straight], axis=0)
+            right = straight
             gram = lax.dot_general(
                 left, right, (((1,), (1,)), ((), ())), preferred_element_type=f32
             )
-            gs[pl.ds(c * PITCH, 2 * S), :] = gram * norm_scale
+            gs[pl.ds(c * PITCH, 2 * S), :S] = gram * norm_scale
         top = base
         for j in range(S):
             even = gs[pl.ds(2 * j, 8, stride=PITCH), :]
             odd = gs[pl.ds(2 * j + 1, 8, stride=PITCH), :]
-            block[pl.ds(top, 8), pl.ds(j * LANES, LANES)] = jnp.where(lane < S, even, odd)
+            block[pl.ds(top, 8), pl.ds(j * LANES, LANES)] = jnp.where(lane < S, even, pltpu.roll(odd, S, 1))
         return 0
 
     for o in range(LO // 8):

time: 92.9 us -> 92.8 us (level)
  no operation moved by 1% of the time
where the time goes in v10:
time: 92.8 us; the launch traced here: 92.5 us
  waiting for transfers between devices  35.7 us (38%)
  starting transfers between devices  35 us (38%)
  Pallas kernels  19 us (20%)
  local copies, waits for them, and re-layouts  1.22 us (1%)
  between operations  0.93 us (1%)
    ppermute x7, waiting for transfers between devices, routed(): lax.ppermute(value, axis, [(i, dest(i)) for i in range(lax.axis_size(axis...  32.2 us
    all_to_all x1, starting transfers between devices, shards(): recv = lax.all_to_all(msgs, whole, split_axis=0, concat_axis=0, tiled=True)  15.3 us
    ppermute x7, starting transfers between devices, routed(): lax.ppermute(value, axis, [(i, dest(i)) for i in range(lax.axis_size(axis...  15.2 us
    pallas_call x1, Pallas kernels, early_messages(): pl.pallas_call(lambda *refs: early_kernel(nt, *refs), out_shape=(jax.Shap...  8.17 us
    ppermute x1, starting transfers between devices, passed_along(): return lax.ppermute(block, axis, route)  4.51 us
    pallas_call x1, Pallas kernels, tone_sums(): pl.pallas_call(tone_kernel, out_shape=jax.ShapeDtypeStruct((tone_chan.sha...  4.37 us
    pallas_call x1, Pallas kernels, correlated(): pl.pallas_call(lambda *refs: x_kernel(norm_scale, per_source, *refs), out...  3.85 us
    ppermute x1, waiting for transfers between devices, passed_along(): return lax.ppermute(block, axis, route)  3.54 us
  transfers between devices with their start and end apart: 9, of which 7 were waited for; matrix products, arithmetic and copies ran while one was open for 1% of the time, Pallas kernels for 14%

profile of v10, /device:TPU:1, one launch (start us, length us, event | category | flops | bytes accessed | tf_op | source)
XLA Modules:
  0.0 92.5 jit_solution(12767810793704638170)
XLA Ops:
  0.6 0.0 copy-start.3
  0.6 0.0 copy-start.1
  0.7 0.0 copy-start.2
  0.7 1.2 %slice.3 = bf16[8,32768]{1,0:T(8,128)(2,1)S(1)} slice(bf16[8,131072]{1,0:T(8,128)(2,1)} %refs_0_.2), slice={[0:8], [0:32768]} | slice | bytes 1048576 | tf_op jit(solution)/shard_map/slice | solution.py:407
  1.9 4.5 %collective-permute-start = (bf16[8,32768]{1,0:T(8,128)(2,1)S(1)}, bf16[8,32768]{1,0:T(8,128)(2,1)S(1)}, u32[]{:S(2)}, u32[]{:S(2)}) collective-permute-start(bf16[8,32768]{1,0:T(8,128)(2,1)S(1)} %slice.3), channel_id=1, source_target_pairs={{1,0},{2,1},{3,2},{4,3},{5,4},{6,5},{7,6},{8,7},{9,8},{10,9},{11,1... | collective-permute-start | bytes 1572872 | tf_op jit(solution)/shard_map/ppermute | solution.py:383
  6.4 8.2 %channelize.1 = (bf16[256,32,128]{2,1,0:T(8,128)(2,1)}, f32[4288,128]{1,0:T(8,128)S(1)}) custom-call(bf16[8,131072]{1,0:T(8,128)(2,1)} %refs_0_.2, s32[8]{0:T(128)} %refs_0_.3, s32[8]{0:T(128)} %refs_1_.3, bf16[256,512]{1,0:T(8,128)(2,1)} %constant.10.clone.refs_3_.refs_2_, f32[128,256]{1,0:T(8,128)} %constant.11.clone.refs_4_.refs_3_, ...), custom_call_target="tpu_custom_call" | custom-call | tf_op jit(solution)/shard_map/channelize/pallas_call | solution.py:210
  14.6 3.5 %collective-permute-done.refs_6_ = bf16[8,32768]{1,0:T(8,128)(2,1)S(1)} collective-permute-done((bf16[8,32768]{1,0:T(8,128)(2,1)S(1)}, bf16[8,32768]{1,0:T(8,128)(2,1)S(1)}, u32[]{:S(2)}, u32[]{:S(2)}) %collective-permute-start) | collective-permute-done | bytes 524320 | tf_op jit(solution)/shard_map/ppermute | solution.py:383
  18.2 2.6 %channelize_late.1 = (f32[4288,128]{1,0:T(8,128)S(1)}, bf16[256,32,128]{2,1,0:T(8,128)(2,1)}) custom-call(s32[8]{0:T(128)S(1)} %copy-done.5, s32[8]{0:T(128)S(1)} %copy-done.6, bf16[256,512]{1,0:T(8,128)(2,1)S(1)} %copy-done, f32[128,256]{1,0:T(8,128)S(1)} %copy-done.2, f32[128,256]{1,0:T(8,128)S(1)} %copy-done.1, ...), custom_call_target="tpu_custom_call", output_to_operand_aliasing={{0}: (7, {}), {1}: (8, {})} | custom-call | tf_op jit(solution)/shard_map/channelize_late/pallas_call | solution.py:240
  20.8 15.3 %all-to-all-start = ((bf16[256,32,128]{2,1,0:T(8,128)(2,1)}), bf16[256,32,128]{2,1,0:T(8,128)(2,1)S(1)}, u32[]{:S(2)}, u32[]{:S(2)}) async-start(bf16[256,32,128]{2,1,0:T(8,128)(2,1)} %get-tuple-element.7.msgs), calls=%async_computation | async-start | bytes 4194304 | tf_op jit(solution)/shard_map/all_to_all | solution.py:413
  36.1 4.4 %tones.2 = f32[8,128]{1,0:T(8,128)S(1)} custom-call(s32[8,64]{1,0:T(8,128)S(1)} %copy-done.4, bf16[256,32,128]{2,1,0:T(8,128)(2,1)} %get-tuple-element.7.msgs), custom_call_target="tpu_custom_call" | custom-call | tf_op jit(solution)/shard_map/tones/pallas_call | solution.py:292
  40.5 1.5 %collective-permute-start.1 = (f32[8,128]{1,0:T(8,128)S(1)}, f32[8,128]{1,0:T(8,128)S(1)}, u32[]{:S(2)}, u32[]{:S(2)}) collective-permute-start(f32[8,128]{1,0:T(8,128)S(1)} %tones.2), channel_id=1, source_target_pairs={{0,1},{1,0},{2,3},{3,2},{4,5},{5,4},{6,7},{7,6},{8,9},{9,8},{10,11... | collective-permute-start | bytes 12296 | tf_op jit(solution)/shard_map/ppermute | solution.py:387
  41.9 1.4 %collective-permute-done.1 = f32[8,128]{1,0:T(8,128)S(1)} collective-permute-done((f32[8,128]{1,0:T(8,128)S(1)}, f32[8,128]{1,0:T(8,128)S(1)}, u32[]{:S(2)}, u32[]{:S(2)}) %collective-permute-start.1) | collective-permute-done | bytes 4128 | tf_op jit(solution)/shard_map/ppermute | solution.py:387
  43.3 3.0 %collective-permute-start.2 = (f32[8,128]{1,0:T(8,128)S(1)}, f32[8,128]{1,0:T(8,128)S(1)}, u32[]{:S(2)}, u32[]{:S(2)}) collective-permute-start(f32[8,128]{1,0:T(8,128)S(1)} %add.18), channel_id=1, source_target_pairs={{0,2},{2,0},{4,6},{6,4},{8,10},{10,8},{12,14},{14,12},{16,18},{18,... | collective-permute-start | bytes 12296 | tf_op jit(solution)/shard_map/ppermute | solution.py:387
  46.3 0.8 collective-permute-done.2
  47.1 2.5 %collective-permute-start.6 = (f32[8,128]{1,0:T(8,128)S(1)}, f32[8,128]{1,0:T(8,128)S(1)}, u32[]{:S(2)}, u32[]{:S(2)}) collective-permute-start(f32[8,128]{1,0:T(8,128)S(1)} %add.19), channel_id=1, source_target_pairs={{0,12},{2,30},{4,16},{6,2},{8,20},{10,6},{12,24},{14,10},{16,28},{... | collective-permute-start | bytes 12296 | tf_op jit(solution)/shard_map/ppermute | solution.py:387
  49.7 1.6 %collective-permute-start.5 = (f32[8,128]{1,0:T(8,128)S(1)}, f32[8,128]{1,0:T(8,128)S(1)}, u32[]{:S(2)}, u32[]{:S(2)}) collective-permute-start(f32[8,128]{1,0:T(8,128)S(1)} %add.19), channel_id=1, source_target_pairs={{0,8},{2,26},{4,12},{6,30},{8,16},{10,2},{12,20},{14,6},{16,24},{1... | collective-permute-start | bytes 12296 | tf_op jit(solution)/shard_map/ppermute | solution.py:387
  51.2 0.7 collective-permute-start.4
  52.0 5.9 %collective-permute-start.3 = (f32[8,128]{1,0:T(8,128)S(1)}, f32[8,128]{1,0:T(8,128)S(1)}, u32[]{:S(2)}, u32[]{:S(2)}) collective-permute-start(f32[8,128]{1,0:T(8,128)S(1)} %add.19), channel_id=1, source_target_pairs={{0,0},{2,18},{4,4},{6,22},{8,8},{10,26},{12,12},{14,30},{16,16},{1... | collective-permute-start | bytes 12296 | tf_op jit(solution)/shard_map/ppermute | solution.py:387
  57.9 23.1 %collective-permute-done.6 = f32[8,128]{1,0:T(8,128)S(1)} collective-permute-done((f32[8,128]{1,0:T(8,128)S(1)}, f32[8,128]{1,0:T(8,128)S(1)}, u32[]{:S(2)}, u32[]{:S(2)}) %collective-permute-start.6) | collective-permute-done | bytes 4128 | tf_op jit(solution)/shard_map/ppermute | solution.py:387
  81.0 0.6 collective-permute-done.5
  81.6 5.1 %collective-permute-done.3 = f32[8,128]{1,0:T(8,128)S(1)} collective-permute-done((f32[8,128]{1,0:T(8,128)S(1)}, f32[8,128]{1,0:T(8,128)S(1)}, u32[]{:S(2)}, u32[]{:S(2)}) %collective-permute-start.3) | collective-permute-done | bytes 4128 | tf_op jit(solution)/shard_map/ppermute | solution.py:387
  86.7 1.2 %collective-permute-done.7 = f32[8,128]{1,0:T(8,128)S(1)} collective-permute-done((f32[8,128]{1,0:T(8,128)S(1)}, f32[8,128]{1,0:T(8,128)S(1)}, u32[]{:S(2)}, u32[]{:S(2)}) %collective-permute-start.7) | collective-permute-done | bytes 4128 | tf_op jit(solution)/shard_map/ppermute | solution.py:387
  87.9 0.6 add_multiply_fusion
  88.5 3.9 %correlate.1 = f32[64,8192]{1,0:T(8,128)} custom-call(bf16[256,32,128]{2,1,0:T(8,128)(2,1)S(1)} %all-to-all-done.refs_0_), custom_call_target="tpu_custom_call" | custom-call | tf_op jit(solution)/shard_map/correlate/pallas_call | solution.py:363
  (17 shorter events, 0.1 us)
Async XLA Ops:
  0.6 17.5 %copy-start.3 = (bf16[128,256]{1,0:T(8,128)(2,1)S(1)}, bf16[128,256]{1,0:T(8,128)(2,1)}, u32[]{:S(2)}) copy-start(bf16[128,256]{1,0:T(8,128)(2,1)} %constant.13.clone.refs_6_.refs_5_) | copy-start | bytes 196612
  0.6 17.5 %copy-start.1 = (f32[128,256]{1,0:T(8,128)S(1)}, f32[128,256]{1,0:T(8,128)}, u32[]{:S(2)}) copy-start(f32[128,256]{1,0:T(8,128)} %constant.12.clone.refs_5_.refs_4_) | copy-start | bytes 393220
  0.7 17.5 %copy-start.2 = (f32[128,256]{1,0:T(8,128)S(1)}, f32[128,256]{1,0:T(8,128)}, u32[]{:S(2)}) copy-start(f32[128,256]{1,0:T(8,128)} %constant.11.clone.refs_4_.refs_3_) | copy-start | bytes 393220
  0.7 17.5 %copy-start = (bf16[256,512]{1,0:T(8,128)(2,1)S(1)}, bf16[256,512]{1,0:T(8,128)(2,1)}, u32[]{:S(2)}) copy-start(bf16[256,512]{1,0:T(8,128)(2,1)} %constant.10.clone.refs_3_.refs_2_) | copy-start | bytes 786436
  0.7 17.5 %copy-start.6 = (s32[8]{0:T(128)S(1)}, s32[8]{0:T(128)}, u32[]{:S(2)}) copy-start(s32[8]{0:T(128)} %refs_1_.3) | copy-start | bytes 100
  0.7 17.5 %copy-start.5 = (s32[8]{0:T(128)S(1)}, s32[8]{0:T(128)}, u32[]{:S(2)}) copy-start(s32[8]{0:T(128)} %refs_0_.3) | copy-start | bytes 100
  1.9 16.2 %collective-permute-start = (bf16[8,32768]{1,0:T(8,128)(2,1)S(1)}, bf16[8,32768]{1,0:T(8,128)(2,1)S(1)}, u32[]{:S(2)}, u32[]{:S(2)}) collective-permute-start(bf16[8,32768]{1,0:T(8,128)(2,1)S(1)} %slice.3), channel_id=1, source_target_pairs={{1,0},{2,1},{3,2},{4,3},{5,4},{6,5},{7,6},{8,7},{9,8},{10,9},{11,1... | collective-permute-start | bytes 1572872 | tf_op jit(solution)/shard_map/ppermute | solution.py:383
  20.8 15.3 %copy-start.4 = (s32[8,64]{1,0:T(8,128)S(1)}, s32[8,64]{1,0:T(8,128)}, u32[]{:S(2)}) copy-start(s32[8,64]{1,0:T(8,128)} %tones.3) | copy-start | bytes 6148
  20.8 67.7 %all-to-all-start = ((bf16[256,32,128]{2,1,0:T(8,128)(2,1)}), bf16[256,32,128]{2,1,0:T(8,128)(2,1)S(1)}, u32[]{:S(2)}, u32[]{:S(2)}) async-start(bf16[256,32,128]{2,1,0:T(8,128)(2,1)} %get-tuple-element.7.msgs), calls=%async_computation | async-start | bytes 4194304 | tf_op jit(solution)/shard_map/all_to_all | solution.py:413
  40.5 2.9 %collective-permute-start.1 = (f32[8,128]{1,0:T(8,128)S(1)}, f32[8,128]{1,0:T(8,128)S(1)}, u32[]{:S(2)}, u32[]{:S(2)}) collective-permute-start(f32[8,128]{1,0:T(8,128)S(1)} %tones.2), channel_id=1, source_target_pairs={{0,1},{1,0},{2,3},{3,2},{4,5},{5,4},{6,7},{7,6},{8,9},{9,8},{10,11... | collective-permute-start | bytes 12296 | tf_op jit(solution)/shard_map/ppermute | solution.py:387
  43.3 3.8 %collective-permute-start.2 = (f32[8,128]{1,0:T(8,128)S(1)}, f32[8,128]{1,0:T(8,128)S(1)}, u32[]{:S(2)}, u32[]{:S(2)}) collective-permute-start(f32[8,128]{1,0:T(8,128)S(1)} %add.18), channel_id=1, source_target_pairs={{0,2},{2,0},{4,6},{6,4},{8,10},{10,8},{12,14},{14,12},{16,18},{18,... | collective-permute-start | bytes 12296 | tf_op jit(solution)/shard_map/ppermute | solution.py:387
  47.1 33.8 %collective-permute-start.6 = (f32[8,128]{1,0:T(8,128)S(1)}, f32[8,128]{1,0:T(8,128)S(1)}, u32[]{:S(2)}, u32[]{:S(2)}) collective-permute-start(f32[8,128]{1,0:T(8,128)S(1)} %add.19), channel_id=1, source_target_pairs={{0,12},{2,30},{4,16},{6,2},{8,20},{10,6},{12,24},{14,10},{16,28},{... | collective-permute-start | bytes 12296 | tf_op jit(solution)/shard_map/ppermute | solution.py:387
  49.7 31.9 %collective-permute-start.5 = (f32[8,128]{1,0:T(8,128)S(1)}, f32[8,128]{1,0:T(8,128)S(1)}, u32[]{:S(2)}, u32[]{:S(2)}) collective-permute-start(f32[8,128]{1,0:T(8,128)S(1)} %add.19), channel_id=1, source_target_pairs={{0,8},{2,26},{4,12},{6,30},{8,16},{10,2},{12,20},{14,6},{16,24},{1... | collective-permute-start | bytes 12296 | tf_op jit(solution)/shard_map/ppermute | solution.py:387
  51.2 30.3 %collective-permute-start.4 = (f32[8,128]{1,0:T(8,128)S(1)}, f32[8,128]{1,0:T(8,128)S(1)}, u32[]{:S(2)}, u32[]{:S(2)}) collective-permute-start(f32[8,128]{1,0:T(8,128)S(1)} %add.19), channel_id=1, source_target_pairs={{0,4},{2,22},{4,8},{6,26},{8,12},{10,30},{12,16},{14,2},{16,20},{1... | collective-permute-start | bytes 12296 | tf_op jit(solution)/shard_map/ppermute | solution.py:387
  52.0 34.7 %collective-permute-start.3 = (f32[8,128]{1,0:T(8,128)S(1)}, f32[8,128]{1,0:T(8,128)S(1)}, u32[]{:S(2)}, u32[]{:S(2)}) collective-permute-start(f32[8,128]{1,0:T(8,128)S(1)} %add.19), channel_id=1, source_target_pairs={{0,0},{2,18},{4,4},{6,22},{8,8},{10,26},{12,12},{14,30},{16,16},{1... | collective-permute-start | bytes 12296 | tf_op jit(solution)/shard_map/ppermute | solution.py:387
  86.7 1.2 %collective-permute-start.7 = (f32[8,128]{1,0:T(8,128)S(1)}, f32[8,128]{1,0:T(8,128)S(1)}, u32[]{:S(2)}, u32[]{:S(2)}) collective-permute-start(f32[8,128]{1,0:T(8,128)S(1)} %add_add_fusion), channel_id=1, source_target_pairs={{0,2},{2,0},{4,6},{6,4},{8,10},{10,8},{12,14},{14,12},{16,18},{18,... | collective-permute-start | bytes 12296 | tf_op jit(solution)/shard_map/ppermute | solution.py:387

commit v11 on v10

--- a/solution.py
+++ b/solution.py
@@ -78,7 +78,7 @@
     for s in chosen:
         shift = delays[s]
         lead = shift // LANES
-        within = shift - lead * LANES
+        within = jnp.where(valid[s] == 0, 2 * LANES, shift - lead * LANES)
         first = xs[pl.ds(s * pitch + lead, rows), :]
         second = xs[pl.ds(s * pitch + lead + 1, rows), :]
         pair = jnp.concatenate([first.astype(bf16), second.astype(bf16)], axis=1)
@@ -92,14 +92,15 @@
         preferred_element_type=f32,
     )
     for k, s in enumerate(chosen):
-        last = (two[...].astype(f32) * valid[s].astype(f32)).astype(bf16)
         for t in range(nt):
             at = (k * nt + t) * FB
             re, im = sections[at : at + FB, :FA], sections[at : at + FB, FA:]
             cosine, sine = tcos[...], tsin[...]
             tr = (re * cosine + im * sine).astype(bf16)
             ti = (im * cosine - re * sine).astype(bf16)
-            spec = jnp.dot(last, jnp.concatenate([tr, ti], axis=0), preferred_element_type=f32)
+            spec = jnp.dot(
+                two[...], jnp.concatenate([tr, ti], axis=0), preferred_element_type=f32
+            )
             for j in range(FA // LANES):
                 a = spec[:NQ, j * LANES : (j + 1) * LANES]
                 b = spec[NQ:, j * LANES : (j + 1) * LANES]

time: 92.8 us -> 92.7 us (level)
  transfers between devices with their start and end apart: 9 -> 9, of which waited for: 7 -> 7; matrix products, arithmetic and copies ran while one was open for 1% -> 1% of each run, Pallas kernels for 14% -> 13%
where the time goes in v11:
time: 92.7 us; the launch traced here: 92.4 us
  waiting for transfers between devices  35.9 us (39%)
  starting transfers between devices  35 us (38%)
  Pallas kernels  18.8 us (20%)
  local copies, waits for them, and re-layouts  1.22 us (1%)
  between operations  0.93 us (1%)
    ppermute x7, waiting for transfers between devices, routed(): lax.ppermute(value, axis, [(i, dest(i)) for i in range(lax.axis_size(axis...  32.2 us
    all_to_all x1, starting transfers between devices, shards(): recv = lax.all_to_all(msgs, whole, split_axis=0, concat_axis=0, tiled=True)  15.3 us
    ppermute x7, starting transfers between devices, routed(): lax.ppermute(value, axis, [(i, dest(i)) for i in range(lax.axis_size(axis...  15.2 us
    pallas_call x1, Pallas kernels, early_messages(): pl.pallas_call(lambda *refs: early_kernel(nt, *refs), out_shape=(jax.Shap...  8.06 us
    ppermute x1, starting transfers between devices, passed_along(): return lax.ppermute(block, axis, route)  4.51 us
    pallas_call x1, Pallas kernels, tone_sums(): pl.pallas_call(tone_kernel, out_shape=jax.ShapeDtypeStruct((tone_chan.sha...  4.37 us
    pallas_call x1, Pallas kernels, correlated(): pl.pallas_call(lambda *refs: x_kernel(norm_scale, per_source, *refs), out...  3.85 us
    ppermute x1, waiting for transfers between devices, passed_along(): return lax.ppermute(block, axis, route)  3.65 us
  transfers between devices with their start and end apart: 9, of which 7 were waited for; matrix products, arithmetic and copies ran while one was open for 1% of the time, Pallas kernels for 13%

profile of v11, /device:TPU:1, one launch (start us, length us, event | category | flops | bytes accessed | tf_op | source)
XLA Modules:
  0.0 92.4 jit_solution(1662669282153149880)
XLA Ops:
  0.6 0.0 copy-start.1
  0.7 0.0 copy-start.2
  0.7 0.0 copy-start
  0.7 1.2 %slice.3 = bf16[8,32768]{1,0:T(8,128)(2,1)S(1)} slice(bf16[8,131072]{1,0:T(8,128)(2,1)} %refs_0_.2), slice={[0:8], [0:32768]} | slice | bytes 1048576 | tf_op jit(solution)/shard_map/slice | solution.py:408
  1.9 4.5 %collective-permute-start = (bf16[8,32768]{1,0:T(8,128)(2,1)S(1)}, bf16[8,32768]{1,0:T(8,128)(2,1)S(1)}, u32[]{:S(2)}, u32[]{:S(2)}) collective-permute-start(bf16[8,32768]{1,0:T(8,128)(2,1)S(1)} %slice.3), channel_id=1, source_target_pairs={{1,0},{2,1},{3,2},{4,3},{5,4},{6,5},{7,6},{8,7},{9,8},{10,9},{11,1... | collective-permute-start | bytes 1572872 | tf_op jit(solution)/shard_map/ppermute | solution.py:384
  6.4 8.1 %channelize.1 = (bf16[256,32,128]{2,1,0:T(8,128)(2,1)}, f32[4288,128]{1,0:T(8,128)S(1)}) custom-call(bf16[8,131072]{1,0:T(8,128)(2,1)} %refs_0_.2, s32[8]{0:T(128)} %refs_0_.3, s32[8]{0:T(128)} %refs_1_.3, bf16[256,512]{1,0:T(8,128)(2,1)} %constant.10.clone.refs_3_.refs_2_, f32[128,256]{1,0:T(8,128)} %constant.11.clone.refs_4_.refs_3_, ...), custom_call_target="tpu_custom_call" | custom-call | tf_op jit(solution)/shard_map/channelize/pallas_call | solution.py:211
  14.5 3.6 %collective-permute-done.refs_6_ = bf16[8,32768]{1,0:T(8,128)(2,1)S(1)} collective-permute-done((bf16[8,32768]{1,0:T(8,128)(2,1)S(1)}, bf16[8,32768]{1,0:T(8,128)(2,1)S(1)}, u32[]{:S(2)}, u32[]{:S(2)}) %collective-permute-start) | collective-permute-done | bytes 524320 | tf_op jit(solution)/shard_map/ppermute | solution.py:384
  18.2 2.5 %channelize_late.1 = (f32[4288,128]{1,0:T(8,128)S(1)}, bf16[256,32,128]{2,1,0:T(8,128)(2,1)}) custom-call(s32[8]{0:T(128)S(1)} %copy-done.5, s32[8]{0:T(128)S(1)} %copy-done.6, bf16[256,512]{1,0:T(8,128)(2,1)S(1)} %copy-done, f32[128,256]{1,0:T(8,128)S(1)} %copy-done.2, f32[128,256]{1,0:T(8,128)S(1)} %copy-done.1, ...), custom_call_target="tpu_custom_call", output_to_operand_aliasing={{0}: (7, {}), {1}: (8, {})} | custom-call | tf_op jit(solution)/shard_map/channelize_late/pallas_call | solution.py:241
  20.7 15.3 %all-to-all-start = ((bf16[256,32,128]{2,1,0:T(8,128)(2,1)}), bf16[256,32,128]{2,1,0:T(8,128)(2,1)S(1)}, u32[]{:S(2)}, u32[]{:S(2)}) async-start(bf16[256,32,128]{2,1,0:T(8,128)(2,1)} %get-tuple-element.7.msgs), calls=%async_computation | async-start | bytes 4194304 | tf_op jit(solution)/shard_map/all_to_all | solution.py:414
  36.0 4.4 %tones.2 = f32[8,128]{1,0:T(8,128)S(1)} custom-call(s32[8,64]{1,0:T(8,128)S(1)} %copy-done.4, bf16[256,32,128]{2,1,0:T(8,128)(2,1)} %get-tuple-element.7.msgs), custom_call_target="tpu_custom_call" | custom-call | tf_op jit(solution)/shard_map/tones/pallas_call | solution.py:293
  40.4 1.5 %collective-permute-start.1 = (f32[8,128]{1,0:T(8,128)S(1)}, f32[8,128]{1,0:T(8,128)S(1)}, u32[]{:S(2)}, u32[]{:S(2)}) collective-permute-start(f32[8,128]{1,0:T(8,128)S(1)} %tones.2), channel_id=1, source_target_pairs={{0,1},{1,0},{2,3},{3,2},{4,5},{5,4},{6,7},{7,6},{8,9},{9,8},{10,11... | collective-permute-start | bytes 12296 | tf_op jit(solution)/shard_map/ppermute | solution.py:388
  41.9 1.4 %collective-permute-done.1 = f32[8,128]{1,0:T(8,128)S(1)} collective-permute-done((f32[8,128]{1,0:T(8,128)S(1)}, f32[8,128]{1,0:T(8,128)S(1)}, u32[]{:S(2)}, u32[]{:S(2)}) %collective-permute-start.1) | collective-permute-done | bytes 4128 | tf_op jit(solution)/shard_map/ppermute | solution.py:388
  43.3 3.0 %collective-permute-start.2 = (f32[8,128]{1,0:T(8,128)S(1)}, f32[8,128]{1,0:T(8,128)S(1)}, u32[]{:S(2)}, u32[]{:S(2)}) collective-permute-start(f32[8,128]{1,0:T(8,128)S(1)} %add.18), channel_id=1, source_target_pairs={{0,2},{2,0},{4,6},{6,4},{8,10},{10,8},{12,14},{14,12},{16,18},{18,... | collective-permute-start | bytes 12296 | tf_op jit(solution)/shard_map/ppermute | solution.py:388
  46.3 0.8 collective-permute-done.2
  47.1 2.5 %collective-permute-start.6 = (f32[8,128]{1,0:T(8,128)S(1)}, f32[8,128]{1,0:T(8,128)S(1)}, u32[]{:S(2)}, u32[]{:S(2)}) collective-permute-start(f32[8,128]{1,0:T(8,128)S(1)} %add.19), channel_id=1, source_target_pairs={{0,12},{2,30},{4,16},{6,2},{8,20},{10,6},{12,24},{14,10},{16,28},{... | collective-permute-start | bytes 12296 | tf_op jit(solution)/shard_map/ppermute | solution.py:388
  49.6 1.6 %collective-permute-start.5 = (f32[8,128]{1,0:T(8,128)S(1)}, f32[8,128]{1,0:T(8,128)S(1)}, u32[]{:S(2)}, u32[]{:S(2)}) collective-permute-start(f32[8,128]{1,0:T(8,128)S(1)} %add.19), channel_id=1, source_target_pairs={{0,8},{2,26},{4,12},{6,30},{8,16},{10,2},{12,20},{14,6},{16,24},{1... | collective-permute-start | bytes 12296 | tf_op jit(solution)/shard_map/ppermute | solution.py:388
  51.2 0.7 collective-permute-start.4
  51.9 5.9 %collective-permute-start.3 = (f32[8,128]{1,0:T(8,128)S(1)}, f32[8,128]{1,0:T(8,128)S(1)}, u32[]{:S(2)}, u32[]{:S(2)}) collective-permute-start(f32[8,128]{1,0:T(8,128)S(1)} %add.19), channel_id=1, source_target_pairs={{0,0},{2,18},{4,4},{6,22},{8,8},{10,26},{12,12},{14,30},{16,16},{1... | collective-permute-start | bytes 12296 | tf_op jit(solution)/shard_map/ppermute | solution.py:388
  57.8 23.1 %collective-permute-done.6 = f32[8,128]{1,0:T(8,128)S(1)} collective-permute-done((f32[8,128]{1,0:T(8,128)S(1)}, f32[8,128]{1,0:T(8,128)S(1)}, u32[]{:S(2)}, u32[]{:S(2)}) %collective-permute-start.6) | collective-permute-done | bytes 4128 | tf_op jit(solution)/shard_map/ppermute | solution.py:388
  80.9 0.6 collective-permute-done.5
  81.5 5.1 %collective-permute-done.3 = f32[8,128]{1,0:T(8,128)S(1)} collective-permute-done((f32[8,128]{1,0:T(8,128)S(1)}, f32[8,128]{1,0:T(8,128)S(1)}, u32[]{:S(2)}, u32[]{:S(2)}) %collective-permute-start.3) | collective-permute-done | bytes 4128 | tf_op jit(solution)/shard_map/ppermute | solution.py:388
  86.7 1.2 %collective-permute-done.7 = f32[8,128]{1,0:T(8,128)S(1)} collective-permute-done((f32[8,128]{1,0:T(8,128)S(1)}, f32[8,128]{1,0:T(8,128)S(1)}, u32[]{:S(2)}, u32[]{:S(2)}) %collective-permute-start.7) | collective-permute-done | bytes 4128 | tf_op jit(solution)/shard_map/ppermute | solution.py:388
  87.8 0.6 add_multiply_fusion
  88.4 3.9 %correlate.1 = f32[64,8192]{1,0:T(8,128)} custom-call(bf16[256,32,128]{2,1,0:T(8,128)(2,1)S(1)} %all-to-all-done.refs_0_), custom_call_target="tpu_custom_call" | custom-call | tf_op jit(solution)/shard_map/correlate/pallas_call | solution.py:364
  (17 shorter events, 0.1 us)
Async XLA Ops:
  0.6 17.5 %copy-start.3 = (bf16[128,256]{1,0:T(8,128)(2,1)S(1)}, bf16[128,256]{1,0:T(8,128)(2,1)}, u32[]{:S(2)}) copy-start(bf16[128,256]{1,0:T(8,128)(2,1)} %constant.13.clone.refs_6_.refs_5_) | copy-start | bytes 196612
  0.6 17.5 %copy-start.1 = (f32[128,256]{1,0:T(8,128)S(1)}, f32[128,256]{1,0:T(8,128)}, u32[]{:S(2)}) copy-start(f32[128,256]{1,0:T(8,128)} %constant.12.clone.refs_5_.refs_4_) | copy-start | bytes 393220
  0.7 17.5 %copy-start.2 = (f32[128,256]{1,0:T(8,128)S(1)}, f32[128,256]{1,0:T(8,128)}, u32[]{:S(2)}) copy-start(f32[128,256]{1,0:T(8,128)} %constant.11.clone.refs_4_.refs_3_) | copy-start | bytes 393220
  0.7 17.5 %copy-start = (bf16[256,512]{1,0:T(8,128)(2,1)S(1)}, bf16[256,512]{1,0:T(8,128)(2,1)}, u32[]{:S(2)}) copy-start(bf16[256,512]{1,0:T(8,128)(2,1)} %constant.10.clone.refs_3_.refs_2_) | copy-start | bytes 786436
  0.7 17.5 %copy-start.6 = (s32[8]{0:T(128)S(1)}, s32[8]{0:T(128)}, u32[]{:S(2)}) copy-start(s32[8]{0:T(128)} %refs_1_.3) | copy-start | bytes 100
  0.7 17.5 %copy-start.5 = (s32[8]{0:T(128)S(1)}, s32[8]{0:T(128)}, u32[]{:S(2)}) copy-start(s32[8]{0:T(128)} %refs_0_.3) | copy-start | bytes 100
  1.9 16.2 %collective-permute-start = (bf16[8,32768]{1,0:T(8,128)(2,1)S(1)}, bf16[8,32768]{1,0:T(8,128)(2,1)S(1)}, u32[]{:S(2)}, u32[]{:S(2)}) collective-permute-start(bf16[8,32768]{1,0:T(8,128)(2,1)S(1)} %slice.3), channel_id=1, source_target_pairs={{1,0},{2,1},{3,2},{4,3},{5,4},{6,5},{7,6},{8,7},{9,8},{10,9},{11,1... | collective-permute-start | bytes 1572872 | tf_op jit(solution)/shard_map/ppermute | solution.py:384
  20.7 15.3 %copy-start.4 = (s32[8,64]{1,0:T(8,128)S(1)}, s32[8,64]{1,0:T(8,128)}, u32[]{:S(2)}) copy-start(s32[8,64]{1,0:T(8,128)} %tones.3) | copy-start | bytes 6148
  20.7 67.7 %all-to-all-start = ((bf16[256,32,128]{2,1,0:T(8,128)(2,1)}), bf16[256,32,128]{2,1,0:T(8,128)(2,1)S(1)}, u32[]{:S(2)}, u32[]{:S(2)}) async-start(bf16[256,32,128]{2,1,0:T(8,128)(2,1)} %get-tuple-element.7.msgs), calls=%async_computation | async-start | bytes 4194304 | tf_op jit(solution)/shard_map/all_to_all | solution.py:414
  40.4 2.9 %collective-permute-start.1 = (f32[8,128]{1,0:T(8,128)S(1)}, f32[8,128]{1,0:T(8,128)S(1)}, u32[]{:S(2)}, u32[]{:S(2)}) collective-permute-start(f32[8,128]{1,0:T(8,128)S(1)} %tones.2), channel_id=1, source_target_pairs={{0,1},{1,0},{2,3},{3,2},{4,5},{5,4},{6,7},{7,6},{8,9},{9,8},{10,11... | collective-permute-start | bytes 12296 | tf_op jit(solution)/shard_map/ppermute | solution.py:388
  43.3 3.8 %collective-permute-start.2 = (f32[8,128]{1,0:T(8,128)S(1)}, f32[8,128]{1,0:T(8,128)S(1)}, u32[]{:S(2)}, u32[]{:S(2)}) collective-permute-start(f32[8,128]{1,0:T(8,128)S(1)} %add.18), channel_id=1, source_target_pairs={{0,2},{2,0},{4,6},{6,4},{8,10},{10,8},{12,14},{14,12},{16,18},{18,... | collective-permute-start | bytes 12296 | tf_op jit(solution)/shard_map/ppermute | solution.py:388
  47.1 33.8 %collective-permute-start.6 = (f32[8,128]{1,0:T(8,128)S(1)}, f32[8,128]{1,0:T(8,128)S(1)}, u32[]{:S(2)}, u32[]{:S(2)}) collective-permute-start(f32[8,128]{1,0:T(8,128)S(1)} %add.19), channel_id=1, source_target_pairs={{0,12},{2,30},{4,16},{6,2},{8,20},{10,6},{12,24},{14,10},{16,28},{... | collective-permute-start | bytes 12296 | tf_op jit(solution)/shard_map/ppermute | solution.py:388
  49.6 31.9 %collective-permute-start.5 = (f32[8,128]{1,0:T(8,128)S(1)}, f32[8,128]{1,0:T(8,128)S(1)}, u32[]{:S(2)}, u32[]{:S(2)}) collective-permute-start(f32[8,128]{1,0:T(8,128)S(1)} %add.19), channel_id=1, source_target_pairs={{0,8},{2,26},{4,12},{6,30},{8,16},{10,2},{12,20},{14,6},{16,24},{1... | collective-permute-start | bytes 12296 | tf_op jit(solution)/shard_map/ppermute | solution.py:388
  51.2 30.3 %collective-permute-start.4 = (f32[8,128]{1,0:T(8,128)S(1)}, f32[8,128]{1,0:T(8,128)S(1)}, u32[]{:S(2)}, u32[]{:S(2)}) collective-permute-start(f32[8,128]{1,0:T(8,128)S(1)} %add.19), channel_id=1, source_target_pairs={{0,4},{2,22},{4,8},{6,26},{8,12},{10,30},{12,16},{14,2},{16,20},{1... | collective-permute-start | bytes 12296 | tf_op jit(solution)/shard_map/ppermute | solution.py:388
  51.9 34.7 %collective-permute-start.3 = (f32[8,128]{1,0:T(8,128)S(1)}, f32[8,128]{1,0:T(8,128)S(1)}, u32[]{:S(2)}, u32[]{:S(2)}) collective-permute-start(f32[8,128]{1,0:T(8,128)S(1)} %add.19), channel_id=1, source_target_pairs={{0,0},{2,18},{4,4},{6,22},{8,8},{10,26},{12,12},{14,30},{16,16},{1... | collective-permute-start | bytes 12296 | tf_op jit(solution)/shard_map/ppermute | solution.py:388
  86.7 1.2 %collective-permute-start.7 = (f32[8,128]{1,0:T(8,128)S(1)}, f32[8,128]{1,0:T(8,128)S(1)}, u32[]{:S(2)}, u32[]{:S(2)}) collective-permute-start(f32[8,128]{1,0:T(8,128)S(1)} %add_add_fusion), channel_id=1, source_target_pairs={{0,2},{2,0},{4,6},{6,4},{8,10},{10,8},{12,14},{14,12},{16,18},{18,... | collective-permute-start | bytes 12296 | tf_op jit(solution)/shard_map/ppermute | solution.py:388

commit v12 on v11

--- a/solution.py
+++ b/solution.py
@@ -349,12 +349,12 @@
 
     for o in range(LO // 8):
         eight(o, 0)
-        sent.append(
-            pltpu.make_async_copy(
-                block.at[pl.ds(o * 8, 8), :], vis.at[pl.ds(o * 8, 8), :], out_sem.at[o]
+        for part in range(2):
+            span = (pl.ds(o * 8, 8), pl.ds(part * S * S, S * S))
+            sent.append(
+                pltpu.make_async_copy(block.at[span], vis.at[span], out_sem.at[2 * o + part])
             )
-        )
-        sent[o].start()
+            sent[-1].start()
     for copy in sent:
         copy.wait()
 
@@ -371,7 +371,7 @@
             pltpu.VMEM((S * PITCH, LANES), f32),
             pltpu.VMEM((8 * PITCH, LANES), f32),
             pltpu.VMEM((LO, 2 * S * S), f32),
-            pltpu.SemaphoreType.DMA((LO // 8,)),
+            pltpu.SemaphoreType.DMA((LO // 4,)),
         ],
         compiler_params=pltpu.CompilerParams(vmem_limit_bytes=24 << 20),
         name="correlate",

time: 92.7 us -> 92.8 us (level)
  no operation moved by 1% of the time
where the time goes in v12:
time: 92.8 us; the launch traced here: 92.5 us
  waiting for transfers between devices  35.8 us (39%)
  starting transfers between devices  35 us (38%)
  Pallas kernels  18.9 us (20%)
  local copies, waits for them, and re-layouts  1.22 us (1%)
  between operations  0.93 us (1%)
    ppermute x7, waiting for transfers between devices, routed(): lax.ppermute(value, axis, [(i, dest(i)) for i in range(lax.axis_size(axis...  32.2 us
    all_to_all x1, starting transfers between devices, shards(): recv = lax.all_to_all(msgs, whole, split_axis=0, concat_axis=0, tiled=True)  15.3 us
    ppermute x7, starting transfers between devices, routed(): lax.ppermute(value, axis, [(i, dest(i)) for i in range(lax.axis_size(axis...  15.2 us
    pallas_call x1, Pallas kernels, early_messages(): pl.pallas_call(lambda *refs: early_kernel(nt, *refs), out_shape=(jax.Shap...  8.09 us
    ppermute x1, starting transfers between devices, passed_along(): return lax.ppermute(block, axis, route)  4.51 us
    pallas_call x1, Pallas kernels, tone_sums(): pl.pallas_call(tone_kernel, out_shape=jax.ShapeDtypeStruct((tone_chan.sha...  4.37 us
    pallas_call x1, Pallas kernels, correlated(): pl.pallas_call(lambda *refs: x_kernel(norm_scale, per_source, *refs), out...  3.92 us
    ppermute x1, waiting for transfers between devices, passed_along(): return lax.ppermute(block, axis, route)  3.63 us
  transfers between devices with their start and end apart: 9, of which 7 were waited for; matrix products, arithmetic and copies ran while one was open for 1% of the time, Pallas kernels for 13%

profile of v12, /device:TPU:1, one launch (start us, length us, event | category | flops | bytes accessed | tf_op | source)
XLA Modules:
  0.0 92.5 jit_solution(18052153244212506231)
XLA Ops:
  0.6 0.0 copy-start.3
  0.6 0.0 copy-start.1
  0.7 0.0 copy-start
  0.7 1.2 %slice.3 = bf16[8,32768]{1,0:T(8,128)(2,1)S(1)} slice(bf16[8,131072]{1,0:T(8,128)(2,1)} %refs_0_.2), slice={[0:8], [0:32768]} | slice | bytes 1048576 | tf_op jit(solution)/shard_map/slice | solution.py:408
  1.9 4.5 %collective-permute-start = (bf16[8,32768]{1,0:T(8,128)(2,1)S(1)}, bf16[8,32768]{1,0:T(8,128)(2,1)S(1)}, u32[]{:S(2)}, u32[]{:S(2)}) collective-permute-start(bf16[8,32768]{1,0:T(8,128)(2,1)S(1)} %slice.3), channel_id=1, source_target_pairs={{1,0},{2,1},{3,2},{4,3},{5,4},{6,5},{7,6},{8,7},{9,8},{10,9},{11,1... | collective-permute-start | bytes 1572872 | tf_op jit(solution)/shard_map/ppermute | solution.py:384
  6.4 8.1 %channelize.1 = (bf16[256,32,128]{2,1,0:T(8,128)(2,1)}, f32[4288,128]{1,0:T(8,128)S(1)}) custom-call(bf16[8,131072]{1,0:T(8,128)(2,1)} %refs_0_.2, s32[8]{0:T(128)} %refs_0_.3, s32[8]{0:T(128)} %refs_1_.3, bf16[256,512]{1,0:T(8,128)(2,1)} %constant.10.clone.refs_3_.refs_2_, f32[128,256]{1,0:T(8,128)} %constant.11.clone.refs_4_.refs_3_, ...), custom_call_target="tpu_custom_call" | custom-call | tf_op jit(solution)/shard_map/channelize/pallas_call | solution.py:211
  14.5 3.6 %collective-permute-done.refs_6_ = bf16[8,32768]{1,0:T(8,128)(2,1)S(1)} collective-permute-done((bf16[8,32768]{1,0:T(8,128)(2,1)S(1)}, bf16[8,32768]{1,0:T(8,128)(2,1)S(1)}, u32[]{:S(2)}, u32[]{:S(2)}) %collective-permute-start) | collective-permute-done | bytes 524320 | tf_op jit(solution)/shard_map/ppermute | solution.py:384
  18.2 2.6 %channelize_late.1 = (f32[4288,128]{1,0:T(8,128)S(1)}, bf16[256,32,128]{2,1,0:T(8,128)(2,1)}) custom-call(s32[8]{0:T(128)S(1)} %copy-done.5, s32[8]{0:T(128)S(1)} %copy-done.6, bf16[256,512]{1,0:T(8,128)(2,1)S(1)} %copy-done, f32[128,256]{1,0:T(8,128)S(1)} %copy-done.2, f32[128,256]{1,0:T(8,128)S(1)} %copy-done.1, ...), custom_call_target="tpu_custom_call", output_to_operand_aliasing={{0}: (7, {}), {1}: (8, {})} | custom-call | tf_op jit(solution)/shard_map/channelize_late/pallas_call | solution.py:241
  20.7 15.3 %all-to-all-start = ((bf16[256,32,128]{2,1,0:T(8,128)(2,1)}), bf16[256,32,128]{2,1,0:T(8,128)(2,1)S(1)}, u32[]{:S(2)}, u32[]{:S(2)}) async-start(bf16[256,32,128]{2,1,0:T(8,128)(2,1)} %get-tuple-element.7.msgs), calls=%async_computation | async-start | bytes 4194304 | tf_op jit(solution)/shard_map/all_to_all | solution.py:414
  36.0 4.4 %tones.2 = f32[8,128]{1,0:T(8,128)S(1)} custom-call(s32[8,64]{1,0:T(8,128)S(1)} %copy-done.4, bf16[256,32,128]{2,1,0:T(8,128)(2,1)} %get-tuple-element.7.msgs), custom_call_target="tpu_custom_call" | custom-call | tf_op jit(solution)/shard_map/tones/pallas_call | solution.py:293
  40.4 1.5 %collective-permute-start.1 = (f32[8,128]{1,0:T(8,128)S(1)}, f32[8,128]{1,0:T(8,128)S(1)}, u32[]{:S(2)}, u32[]{:S(2)}) collective-permute-start(f32[8,128]{1,0:T(8,128)S(1)} %tones.2), channel_id=1, source_target_pairs={{0,1},{1,0},{2,3},{3,2},{4,5},{5,4},{6,7},{7,6},{8,9},{9,8},{10,11... | collective-permute-start | bytes 12296 | tf_op jit(solution)/shard_map/ppermute | solution.py:388
  41.9 1.4 %collective-permute-done.1 = f32[8,128]{1,0:T(8,128)S(1)} collective-permute-done((f32[8,128]{1,0:T(8,128)S(1)}, f32[8,128]{1,0:T(8,128)S(1)}, u32[]{:S(2)}, u32[]{:S(2)}) %collective-permute-start.1) | collective-permute-done | bytes 4128 | tf_op jit(solution)/shard_map/ppermute | solution.py:388
  43.3 3.0 %collective-permute-start.2 = (f32[8,128]{1,0:T(8,128)S(1)}, f32[8,128]{1,0:T(8,128)S(1)}, u32[]{:S(2)}, u32[]{:S(2)}) collective-permute-start(f32[8,128]{1,0:T(8,128)S(1)} %add.18), channel_id=1, source_target_pairs={{0,2},{2,0},{4,6},{6,4},{8,10},{10,8},{12,14},{14,12},{16,18},{18,... | collective-permute-start | bytes 12296 | tf_op jit(solution)/shard_map/ppermute | solution.py:388
  46.3 0.8 collective-permute-done.2
  47.1 2.5 %collective-permute-start.6 = (f32[8,128]{1,0:T(8,128)S(1)}, f32[8,128]{1,0:T(8,128)S(1)}, u32[]{:S(2)}, u32[]{:S(2)}) collective-permute-start(f32[8,128]{1,0:T(8,128)S(1)} %add.19), channel_id=1, source_target_pairs={{0,12},{2,30},{4,16},{6,2},{8,20},{10,6},{12,24},{14,10},{16,28},{... | collective-permute-start | bytes 12296 | tf_op jit(solution)/shard_map/ppermute | solution.py:388
  49.6 1.6 %collective-permute-start.5 = (f32[8,128]{1,0:T(8,128)S(1)}, f32[8,128]{1,0:T(8,128)S(1)}, u32[]{:S(2)}, u32[]{:S(2)}) collective-permute-start(f32[8,128]{1,0:T(8,128)S(1)} %add.19), channel_id=1, source_target_pairs={{0,8},{2,26},{4,12},{6,30},{8,16},{10,2},{12,20},{14,6},{16,24},{1... | collective-permute-start | bytes 12296 | tf_op jit(solution)/shard_map/ppermute | solution.py:388
  51.2 0.7 collective-permute-start.4
  51.9 5.9 %collective-permute-start.3 = (f32[8,128]{1,0:T(8,128)S(1)}, f32[8,128]{1,0:T(8,128)S(1)}, u32[]{:S(2)}, u32[]{:S(2)}) collective-permute-start(f32[8,128]{1,0:T(8,128)S(1)} %add.19), channel_id=1, source_target_pairs={{0,0},{2,18},{4,4},{6,22},{8,8},{10,26},{12,12},{14,30},{16,16},{1... | collective-permute-start | bytes 12296 | tf_op jit(solution)/shard_map/ppermute | solution.py:388
  57.8 23.1 %collective-permute-done.6 = f32[8,128]{1,0:T(8,128)S(1)} collective-permute-done((f32[8,128]{1,0:T(8,128)S(1)}, f32[8,128]{1,0:T(8,128)S(1)}, u32[]{:S(2)}, u32[]{:S(2)}) %collective-permute-start.6) | collective-permute-done | bytes 4128 | tf_op jit(solution)/shard_map/ppermute | solution.py:388
  80.9 0.6 collective-permute-done.5
  81.5 5.1 %collective-permute-done.3 = f32[8,128]{1,0:T(8,128)S(1)} collective-permute-done((f32[8,128]{1,0:T(8,128)S(1)}, f32[8,128]{1,0:T(8,128)S(1)}, u32[]{:S(2)}, u32[]{:S(2)}) %collective-permute-start.3) | collective-permute-done | bytes 4128 | tf_op jit(solution)/shard_map/ppermute | solution.py:388
  86.7 1.2 %collective-permute-done.7 = f32[8,128]{1,0:T(8,128)S(1)} collective-permute-done((f32[8,128]{1,0:T(8,128)S(1)}, f32[8,128]{1,0:T(8,128)S(1)}, u32[]{:S(2)}, u32[]{:S(2)}) %collective-permute-start.7) | collective-permute-done | bytes 4128 | tf_op jit(solution)/shard_map/ppermute | solution.py:388
  87.8 0.6 add_multiply_fusion
  88.4 3.9 %correlate.1 = f32[64,8192]{1,0:T(8,128)} custom-call(bf16[256,32,128]{2,1,0:T(8,128)(2,1)S(1)} %all-to-all-done.refs_0_), custom_call_target="tpu_custom_call" | custom-call | tf_op jit(solution)/shard_map/correlate/pallas_call | solution.py:364
  (17 shorter events, 0.1 us)
Async XLA Ops:
  0.6 17.5 %copy-start.3 = (bf16[128,256]{1,0:T(8,128)(2,1)S(1)}, bf16[128,256]{1,0:T(8,128)(2,1)}, u32[]{:S(2)}) copy-start(bf16[128,256]{1,0:T(8,128)(2,1)} %constant.13.clone.refs_6_.refs_5_) | copy-start | bytes 196612
  0.6 17.5 %copy-start.1 = (f32[128,256]{1,0:T(8,128)S(1)}, f32[128,256]{1,0:T(8,128)}, u32[]{:S(2)}) copy-start(f32[128,256]{1,0:T(8,128)} %constant.12.clone.refs_5_.refs_4_) | copy-start | bytes 393220
  0.7 17.5 %copy-start.2 = (f32[128,256]{1,0:T(8,128)S(1)}, f32[128,256]{1,0:T(8,128)}, u32[]{:S(2)}) copy-start(f32[128,256]{1,0:T(8,128)} %constant.11.clone.refs_4_.refs_3_) | copy-start | bytes 393220
  0.7 17.5 %copy-start = (bf16[256,512]{1,0:T(8,128)(2,1)S(1)}, bf16[256,512]{1,0:T(8,128)(2,1)}, u32[]{:S(2)}) copy-start(bf16[256,512]{1,0:T(8,128)(2,1)} %constant.10.clone.refs_3_.refs_2_) | copy-start | bytes 786436
  0.7 17.5 %copy-start.6 = (s32[8]{0:T(128)S(1)}, s32[8]{0:T(128)}, u32[]{:S(2)}) copy-start(s32[8]{0:T(128)} %refs_1_.3) | copy-start | bytes 100
  0.7 17.5 %copy-start.5 = (s32[8]{0:T(128)S(1)}, s32[8]{0:T(128)}, u32[]{:S(2)}) copy-start(s32[8]{0:T(128)} %refs_0_.3) | copy-start | bytes 100
  1.9 16.2 %collective-permute-start = (bf16[8,32768]{1,0:T(8,128)(2,1)S(1)}, bf16[8,32768]{1,0:T(8,128)(2,1)S(1)}, u32[]{:S(2)}, u32[]{:S(2)}) collective-permute-start(bf16[8,32768]{1,0:T(8,128)(2,1)S(1)} %slice.3), channel_id=1, source_target_pairs={{1,0},{2,1},{3,2},{4,3},{5,4},{6,5},{7,6},{8,7},{9,8},{10,9},{11,1... | collective-permute-start | bytes 1572872 | tf_op jit(solution)/shard_map/ppermute | solution.py:384
  20.7 15.3 %copy-start.4 = (s32[8,64]{1,0:T(8,128)S(1)}, s32[8,64]{1,0:T(8,128)}, u32[]{:S(2)}) copy-start(s32[8,64]{1,0:T(8,128)} %tones.3) | copy-start | bytes 6148
  20.7 67.7 %all-to-all-start = ((bf16[256,32,128]{2,1,0:T(8,128)(2,1)}), bf16[256,32,128]{2,1,0:T(8,128)(2,1)S(1)}, u32[]{:S(2)}, u32[]{:S(2)}) async-start(bf16[256,32,128]{2,1,0:T(8,128)(2,1)} %get-tuple-element.7.msgs), calls=%async_computation | async-start | bytes 4194304 | tf_op jit(solution)/shard_map/all_to_all | solution.py:414
  40.4 2.9 %collective-permute-start.1 = (f32[8,128]{1,0:T(8,128)S(1)}, f32[8,128]{1,0:T(8,128)S(1)}, u32[]{:S(2)}, u32[]{:S(2)}) collective-permute-start(f32[8,128]{1,0:T(8,128)S(1)} %tones.2), channel_id=1, source_target_pairs={{0,1},{1,0},{2,3},{3,2},{4,5},{5,4},{6,7},{7,6},{8,9},{9,8},{10,11... | collective-permute-start | bytes 12296 | tf_op jit(solution)/shard_map/ppermute | solution.py:388
  43.3 3.8 %collective-permute-start.2 = (f32[8,128]{1,0:T(8,128)S(1)}, f32[8,128]{1,0:T(8,128)S(1)}, u32[]{:S(2)}, u32[]{:S(2)}) collective-permute-start(f32[8,128]{1,0:T(8,128)S(1)} %add.18), channel_id=1, source_target_pairs={{0,2},{2,0},{4,6},{6,4},{8,10},{10,8},{12,14},{14,12},{16,18},{18,... | collective-permute-start | bytes 12296 | tf_op jit(solution)/shard_map/ppermute | solution.py:388
  47.1 33.8 %collective-permute-start.6 = (f32[8,128]{1,0:T(8,128)S(1)}, f32[8,128]{1,0:T(8,128)S(1)}, u32[]{:S(2)}, u32[]{:S(2)}) collective-permute-start(f32[8,128]{1,0:T(8,128)S(1)} %add.19), channel_id=1, source_target_pairs={{0,12},{2,30},{4,16},{6,2},{8,20},{10,6},{12,24},{14,10},{16,28},{... | collective-permute-start | bytes 12296 | tf_op jit(solution)/shard_map/ppermute | solution.py:388
  49.6 31.9 %collective-permute-start.5 = (f32[8,128]{1,0:T(8,128)S(1)}, f32[8,128]{1,0:T(8,128)S(1)}, u32[]{:S(2)}, u32[]{:S(2)}) collective-permute-start(f32[8,128]{1,0:T(8,128)S(1)} %add.19), channel_id=1, source_target_pairs={{0,8},{2,26},{4,12},{6,30},{8,16},{10,2},{12,20},{14,6},{16,24},{1... | collective-permute-start | bytes 12296 | tf_op jit(solution)/shard_map/ppermute | solution.py:388
  51.2 30.3 %collective-permute-start.4 = (f32[8,128]{1,0:T(8,128)S(1)}, f32[8,128]{1,0:T(8,128)S(1)}, u32[]{:S(2)}, u32[]{:S(2)}) collective-permute-start(f32[8,128]{1,0:T(8,128)S(1)} %add.19), channel_id=1, source_target_pairs={{0,4},{2,22},{4,8},{6,26},{8,12},{10,30},{12,16},{14,2},{16,20},{1... | collective-permute-start | bytes 12296 | tf_op jit(solution)/shard_map/ppermute | solution.py:388
  51.9 34.7 %collective-permute-start.3 = (f32[8,128]{1,0:T(8,128)S(1)}, f32[8,128]{1,0:T(8,128)S(1)}, u32[]{:S(2)}, u32[]{:S(2)}) collective-permute-start(f32[8,128]{1,0:T(8,128)S(1)} %add.19), channel_id=1, source_target_pairs={{0,0},{2,18},{4,4},{6,22},{8,8},{10,26},{12,12},{14,30},{16,16},{1... | collective-permute-start | bytes 12296 | tf_op jit(solution)/shard_map/ppermute | solution.py:388
  86.7 1.2 %collective-permute-start.7 = (f32[8,128]{1,0:T(8,128)S(1)}, f32[8,128]{1,0:T(8,128)S(1)}, u32[]{:S(2)}, u32[]{:S(2)}) collective-permute-start(f32[8,128]{1,0:T(8,128)S(1)} %add_add_fusion), channel_id=1, source_target_pairs={{0,2},{2,0},{4,6},{6,4},{8,10},{10,8},{12,14},{14,12},{16,18},{18,... | collective-permute-start | bytes 12296 | tf_op jit(solution)/shard_map/ppermute | solution.py:388
